TPU v7x, 32 devices: a whole 2x2x4 slice. The times are simulated.
32 devices in a mesh: parts: 2 (over x), gy: 16 (over z, y, core).
Axes of the slice: x: 2, y: 2, z: 4, core: 2. Of those that a mesh axis runs over, the one named last changes fastest.
Arguments:
- zero_filled: float32 [32, 2, 64, 128], P(('parts', 'gy')), parts along dimension 0, may hold values from -6 to 6
- coil_maps: bfloat16 [32, 2, 32, 64, 128], P(('parts', 'gy')), parts along dimension 0, may hold values from -0.75 to 0.75
- offsets: int32 [128], P('parts'), parts along dimension 0, may hold values from 0 to 3
- step_sizes: float32 [1], replicated, may hold values from 0.6 to 1.4
- w_in: bfloat16 [64, 2, 3, 3], replicated, may hold values from -1.5 to 1.5
- b_in: float32 [64], replicated, may hold values from -0.5 to 0.5
- w_mid: bfloat16 [64, 64, 3, 3], replicated, may hold values from -0.25 to 0.25
- b_mid: float32 [64], replicated, may hold values from -0.5 to 0.5
- w_out: bfloat16 [2, 64, 3, 3], replicated, may hold values from -0.125 to 0.125
- b_out: float32 [2], replicated, may hold values from -0.5 to 0.5
Outputs:
- recon: float32 [32, 2, 64, 128], P(('parts', 'gy')), parts along dimension 0
There are 2 independent parts, one for each index of `parts`. A program takes and returns all parts, laid end to end along the dimension named above; an argument that names none is the same for every part. Nothing has to cross between parts.
Inputs may be any that keep to these rules, and one draw needn't show every extreme that they name: Readout row x samples the phase-encode lines offsets[x] + 4 m.
All inputs are finite; a program needn't handle non-finite values.
Results may differ from a plain program's by a relative error of at most 0.0012.
Values may be sent and summed in bfloat16 or wider, within the bound.
No kernel may reach another device: no remote copies, remote signals or barrier semaphores. Data moves between devices by JAX's collectives and lax.ppermute only.
A program may use at most 64 MiB of HBM per device.

v0:
```python
import jax
import jax.numpy as jnp
from jax import lax
from jax.sharding import PartitionSpec as P


def phase_tables(offsets):
    turns = jnp.arange(4, dtype=jnp.int32)[:, None] * offsets[None, :] % 4
    cosines = (turns == 0).astype(jnp.float32) - (turns == 2).astype(jnp.float32)
    sines = (turns == 3).astype(jnp.float32) - (turns == 1).astype(jnp.float32)
    return (cosines, sines)


def fold_normal(maps_list, field_list, cosines, sines):
    folded_real = None
    folded_imag = None
    for partner in range(4):
        maps_real = maps_list[partner][:, 0].astype(jnp.float32)
        maps_imag = maps_list[partner][:, 1].astype(jnp.float32)
        field_real = field_list[partner][:, 0][:, None]
        field_imag = field_list[partner][:, 1][:, None]
        coil_real = maps_real * field_real - maps_imag * field_imag
        coil_imag = maps_real * field_imag + maps_imag * field_real
        cosine = cosines[partner][None, None, :, None]
        sine = sines[partner][None, None, :, None]
        term_real = cosine * coil_real - sine * coil_imag
        term_imag = cosine * coil_imag + sine * coil_real
        if partner == 0:
            folded_real, folded_imag = (term_real, term_imag)
        else:
            folded_real = folded_real + term_real
            folded_imag = folded_imag + term_imag
    folded_real = 0.25 * folded_real
    folded_imag = 0.25 * folded_imag
    own_real = maps_list[0][:, 0].astype(jnp.float32)
    own_imag = maps_list[0][:, 1].astype(jnp.float32)
    normal_real = jnp.sum(own_real * folded_real + own_imag * folded_imag, axis=1)
    normal_imag = jnp.sum(own_real * folded_imag - own_imag * folded_real, axis=1)
    return jnp.stack([normal_real, normal_imag], axis=1)


def convolve(inputs, kernel):
    return lax.conv_general_dilated(
        inputs,
        kernel,
        (1, 1),
        "SAME",
        dimension_numbers=("NCHW", "OIHW", "NCHW"),
        preferred_element_type=jnp.float32,
    )


def denoise(stepped, w_in, b_in, w_mid, b_mid, w_out, b_out):
    stepped_low = stepped.astype(jnp.bfloat16)
    hidden_one = jax.nn.relu(convolve(stepped_low, w_in) + b_in[None, :, None, None]).astype(
        jnp.bfloat16
    )
    hidden_two = jax.nn.relu(convolve(hidden_one, w_mid) + b_mid[None, :, None, None]).astype(
        jnp.bfloat16
    )
    return stepped + convolve(hidden_two, w_out) + b_out[None, :, None, None]


def per_device(zero_filled, coil_maps, offsets, step_sizes, w_in, b_in, w_mid, b_mid, w_out, b_out):
    cosines, sines = phase_tables(offsets)
    devices = lax.axis_size("gy")
    field = zero_filled
    width_piece = zero_filled.shape[2] // devices
    first_row = lax.axis_index("gy") * width_piece
    cos_piece = lax.dynamic_slice_in_dim(cosines, first_row, width_piece, 1)
    sin_piece = lax.dynamic_slice_in_dim(sines, first_row, width_piece, 1)
    maps_whole = lax.all_to_all(coil_maps, "gy", split_axis=3, concat_axis=0, tiled=True)
    quarter = maps_whole.shape[0] // 4
    maps_list = [jnp.roll(maps_whole, -partner * quarter, axis=0) for partner in range(4)]
    whole = lax.all_to_all(field, "gy", split_axis=2, concat_axis=0, tiled=True)
    field_list = [jnp.roll(whole, -partner * quarter, axis=0) for partner in range(4)]
    normal_whole = fold_normal(maps_list, field_list, cos_piece, sin_piece)
    normal = lax.all_to_all(normal_whole, "gy", split_axis=0, concat_axis=2, tiled=True)
    stepped = field - step_sizes[0] * (normal - zero_filled)
    field = denoise(stepped, w_in, b_in, w_mid, b_mid, w_out, b_out)
    return field


def solution(mesh):
    in_specs = (
        P(("parts", "gy"), None, None, None),
        P(("parts", "gy"), None, None, None, None),
        P("parts"),
        P(),
        P(),
        P(),
        P(),
        P(),
        P(),
        P(),
    )
    out_specs = P(("parts", "gy"), None, None, None)
    return jax.shard_map(
        per_device, mesh=mesh, in_specs=in_specs, out_specs=out_specs, check_vma=False
    )
```

profile of v0, /device:TPU:0, one launch (start us, length us, event | category | flops | bytes accessed | tf_op | source)
XLA Modules:
  0.0 121.8 jit_solution(7083519290412785793)
XLA Ops:
  0.0 0.0 copy-start
  0.0 0.0 copy-start.3
  0.0 1.6 %copy.53 = f32[1,2,64,128]{3,1,0,2:T(2,128)} copy(f32[1,2,64,128]{3,2,1,0:T(8,128)} %param.10) | data formatting | bytes 131072 | tf_op args[0]
  1.6 7.4 %all-to-all-start.1 = ((f32[1,2,64,128]{3,1,0,2:T(2,128)}), f32[1,2,64,128]{3,1,0,2:T(2,128)S(1)}, u32[]{:S(2)}, u32[]{:S(2)}) async-start(f32[1,2,64,128]{3,1,0,2:T(2,128)} %copy.53), calls=%async_computation.1 | async-start | bytes 131072 | tf_op jit(solution)/shard_map/all_to_all | solution.py:75
  9.0 2.9 %copy.49 = bf16[1,2,32,64,128]{4,2,1,0,3:T(8,128)(2,1)} copy(bf16[1,2,32,64,128]{4,3,2,1,0:T(8,128)(2,1)} %param.11) | data formatting | bytes 2097152 | tf_op args[1]
  11.9 4.0 %all-to-all-done.1 = f32[1,2,64,128]{3,1,0,2:T(2,128)S(1)} async-done(((f32[1,2,64,128]{3,1,0,2:T(2,128)}), f32[1,2,64,128]{3,1,0,2:T(2,128)S(1)}, u32[]{:S(2)}, u32[]{:S(2)}) %all-to-all-start.1) | async-done | bytes 65568 | tf_op jit(solution)/shard_map/all_to_all | solution.py:75
  15.9 3.7 %all-to-all-start = ((bf16[1,2,32,64,128]{4,2,1,0,3:T(8,128)(2,1)}), bf16[1,2,32,64,128]{4,2,1,0,3:T(8,128)(2,1)S(1)}, u32[]{:S(2)}, u32[]{:S(2)}) async-start(bf16[1,2,32,64,128]{4,2,1,0,3:T(8,128)(2,1)} %copy.49), calls=%async_computation | async-start | bytes 2097152 | tf_op jit(solution)/shard_map/all_to_all | solution.py:72
  19.5 0.0 copy-done.3
  19.6 0.1 constant_dynamic-slice_fusion
  19.8 22.6 %all-to-all-done = bf16[1,2,32,64,128]{4,2,1,0,3:T(8,128)(2,1)S(1)} async-done(((bf16[1,2,32,64,128]{4,2,1,0,3:T(8,128)(2,1)}), bf16[1,2,32,64,128]{4,2,1,0,3:T(8,128)(2,1)S(1)}, u32[]{:S(2)}, u32[]{:S(2)}) %all-to-all-start) | async-done | bytes 1048608 | tf_op jit(solution)/shard_map/all_to_all | solution.py:72
  42.4 0.1 copy.50
  42.5 0.4 slice_bitcast_fusion
  42.9 0.1 slice_bitcast_fusion.3
  43.0 0.1 copy.69
  43.1 0.0 copy-start.1
  43.1 0.0 copy-start.4
  43.1 0.0 copy-start.6
  43.1 0.0 copy-start.8
  43.1 2.8 %fusion.37 = (f32[16,4,128]{2,1,0:T(4,128)S(1)}, f32[16,4,128]{2,1,0:T(4,128)S(1)}) fusion(bf16[16,2,32,4,128]{4,2,1,3,0:T(8,128)(2,1)S(1)} %bitcast.193, bf16[16,2,32,4,128]{4,2,3,1,0:T(8,128)(2,1)S(1)} %bitcast.194, f32[4]{0:T(128)S(1)} %get-tuple-element.38, f32[16,4,128]{2,1,0:T(4,128)S(1)} %get-tuple-element.32, ...), kind=kLoop, calls=%fused_computation.57 | loop fusion | flops 25149440 | bytes 4522112 | tf_op jit(solution)/shard_map/reduce_sum | solution.py:37
  45.9 0.6 pad_maximum_fusion.3
  46.5 6.8 %all-to-all-start.2 = ((f32[16,2,4,128]{3,2,1,0:T(4,128)}), f32[16,2,4,128]{3,2,1,0:T(4,128)S(1)}, u32[]{:S(2)}, u32[]{:S(2)}) async-start(f32[16,2,4,128]{3,2,1,0:T(4,128)} %pad_maximum_fusion.3), calls=%async_computation.2 | async-start | bytes 131072 | tf_op jit(solution)/shard_map/all_to_all | solution.py:78
  54.0 6.2 %all-to-all-done.2 = f32[16,2,4,128]{3,2,1,0:T(4,128)S(1)} async-done(((f32[16,2,4,128]{3,2,1,0:T(4,128)}), f32[16,2,4,128]{3,2,1,0:T(4,128)S(1)}, u32[]{:S(2)}, u32[]{:S(2)}) %all-to-all-start.2) | async-done | bytes 65568 | tf_op jit(solution)/shard_map/all_to_all | solution.py:78
  60.3 0.0 copy-done.1
  60.3 0.1 copy.65
  60.4 0.1 pad.clone
  60.5 0.6 copy.58
  61.1 0.1 slice.240
  61.2 0.0 copy-done.4
  61.3 0.0 copy-done.6
  61.3 0.0 copy-done.8
  61.3 0.0 copy-start.7
  61.3 3.7 %fusion.21 = bf16[64,1,8,17,64]{4,2,3,0,1:T(8,128)(2,1)S(1)} fusion(f32[64]{0:T(128)S(1)} %copy-done.6, pred[8,17]{0,1:T(8,128)(4,1)S(1)} %copy-done.8, bf16[64,2,3,3]{0,1,3,2:T(2,128)(2,1)S(1)} %copy-done.4, bf16[2,64,1,7,2]{3,0,4,1,2:T(2,128)(2,1)S(1)} %slice.240, bf16[2,64,1,8,17]{3,0,4,1,2:T(2,128)(2,1)S(1)} %copy.58), kind=kOutput, calls=%fused_computation.23 | convolution fusion | flops 22747136 | bytes 1155208 | tf_op jit(solution)/shard_map/conv_general_dilated | solution.py:43
  65.0 0.1 fusion.76
  65.0 0.0 copy-done
  65.0 0.0 copy-done.7
  65.0 0.0 copy-start.5
  65.1 5.6 %fusion.23 = bf16[64,1,8,17,64]{4,2,3,0,1:T(8,128)(2,1)S(1)} fusion(f32[64]{0:T(128)S(1)} %copy-done.7, pred[8,17]{0,1:T(8,128)(4,1)S(1)} %copy-done.8, bf16[64,64,3,3]{1,0,3,2:T(8,128)(2,1)S(1)} %copy-done, bf16[64,1,7,1,64]{4,2,3,0,1:T(8,128)(2,1)S(1)} %get-tuple-element.10, bf16[64,1,7,1,64]{4,2,3,0,1:T(8,128)(2,1)S(1)} %get-tuple-element.9, ...), kind=kOutput, calls=%fused_computation.25 | convolution fusion | flops 643497984 | bytes 2417032 | tf_op jit(solution)/shard_map/conv_general_dilated | solution.py:43
  70.6 0.1 fusion.75
  70.7 0.0 copy-done.5
  70.7 0.0 copy-start.2
  70.7 49.3 %fusion.18 = f32[64,8,17,2]{1,3,2,0:T(2,128)S(1)} fusion(bf16[2,64,3,3]{1,0,3,2:T(2,128)(2,1)S(1)} %copy-done.5, bf16[64,1,7,1,64]{4,2,3,0,1:T(8,128)(2,1)S(1)} %get-tuple-element.8, bf16[64,1,7,1,64]{4,2,3,0,1:T(8,128)(2,1)S(1)} %get-tuple-element.7, bf16[64,1,8,17,64]{4,2,3,0,1:T(8,128)(2,1)S(1)} %fusion.23), kind=kOutput, calls=%fused_computation.20 | convolution fusion | flops 26071040 | bytes 1300736 | tf_op jit(solution)/shard_map/conv_general_dilated | solution.py:43
  120.0 1.0 copy.59
  121.0 0.1 copy.64
  121.1 0.0 copy-done.2
  121.1 0.7 fusion.53
  (13 shorter events, 0.2 us)
Async XLA Ops:
  0.0 65.0 %copy-start = (bf16[64,64,3,3]{1,0,3,2:T(8,128)(2,1)S(1)}, bf16[64,64,3,3]{1,0,3,2:T(8,128)(2,1)}, u32[]{:S(2)}) copy-start(bf16[64,64,3,3]{1,0,3,2:T(8,128)(2,1)} %param.16) | copy-start | bytes 221188
  0.0 19.5 %copy-start.3 = (s32[64]{0:T(128)S(1)}, s32[64]{0:T(128)}, u32[]{:S(2)}) copy-start(s32[64]{0:T(128)} %param.12) | copy-start | bytes 772
  1.6 14.3 %all-to-all-start.1 = ((f32[1,2,64,128]{3,1,0,2:T(2,128)}), f32[1,2,64,128]{3,1,0,2:T(2,128)S(1)}, u32[]{:S(2)}, u32[]{:S(2)}) async-start(f32[1,2,64,128]{3,1,0,2:T(2,128)} %copy.53), calls=%async_computation.1 | async-start | bytes 131072 | tf_op jit(solution)/shard_map/all_to_all | solution.py:75
  15.9 26.6 %all-to-all-start = ((bf16[1,2,32,64,128]{4,2,1,0,3:T(8,128)(2,1)}), bf16[1,2,32,64,128]{4,2,1,0,3:T(8,128)(2,1)S(1)}, u32[]{:S(2)}, u32[]{:S(2)}) async-start(bf16[1,2,32,64,128]{4,2,1,0,3:T(8,128)(2,1)} %copy.49), calls=%async_computation | async-start | bytes 2097152 | tf_op jit(solution)/shard_map/all_to_all | solution.py:72
  43.1 17.2 %copy-start.1 = (f32[1,2,64,128]{3,2,1,0:T(8,128)S(1)}, f32[1,2,64,128]{3,2,1,0:T(8,128)}, u32[]{:S(2)}) copy-start(f32[1,2,64,128]{3,2,1,0:T(8,128)} %param.10) | copy-start | bytes 196612
  43.1 18.2 %copy-start.4 = (bf16[64,2,3,3]{0,1,3,2:T(2,128)(2,1)S(1)}, bf16[64,2,3,3]{0,1,3,2:T(2,128)(2,1)}, u32[]{:S(2)}) copy-start(bf16[64,2,3,3]{0,1,3,2:T(2,128)(2,1)} %param.14) | copy-start | bytes 6916
  43.1 18.2 %copy-start.6 = (f32[64]{0:T(128)S(1)}, f32[64]{0:T(128)}, u32[]{:S(2)}) copy-start(f32[64]{0:T(128)} %param.15) | copy-start | bytes 772
  43.1 18.2 %copy-start.8 = (pred[8,17]{0,1:T(8,128)(4,1)S(1)}, pred[8,17]{0,1:T(8,128)(4,1)}, u32[]{:S(2)}) copy-start(pred[8,17]{0,1:T(8,128)(4,1)} %constant.47) | copy-start | bytes 412
  46.5 13.7 %all-to-all-start.2 = ((f32[16,2,4,128]{3,2,1,0:T(4,128)}), f32[16,2,4,128]{3,2,1,0:T(4,128)S(1)}, u32[]{:S(2)}, u32[]{:S(2)}) async-start(f32[16,2,4,128]{3,2,1,0:T(4,128)} %pad_maximum_fusion.3), calls=%async_computation.2 | async-start | bytes 131072 | tf_op jit(solution)/shard_map/all_to_all | solution.py:78
  61.3 3.8 %copy-start.7 = (f32[64]{0:T(128)S(1)}, f32[64]{0:T(128)}, u32[]{:S(2)}) copy-start(f32[64]{0:T(128)} %param.17) | copy-start | bytes 772
  65.0 5.6 %copy-start.5 = (bf16[2,64,3,3]{1,0,3,2:T(2,128)(2,1)S(1)}, bf16[2,64,3,3]{1,0,3,2:T(2,128)(2,1)}, u32[]{:S(2)}) copy-start(bf16[2,64,3,3]{1,0,3,2:T(2,128)(2,1)} %param.18) | copy-start | bytes 6916
  70.7 50.4 %copy-start.2 = (f32[2]{0:T(128)S(1)}, f32[2]{0:T(128)}, u32[]{:S(2)}) copy-start(f32[2]{0:T(128)} %param.19) | copy-start | bytes 28
where the time goes:
time: 122 us
  matrix products  58.5 us (48%)
  waiting for transfers between devices  32.9 us (27%)
  starting transfers between devices  17.9 us (15%)
  local copies, waits for them, and re-layouts  7.39 us (6%)
  other arithmetic  4.21 us (3%)
    conv_general_dilated x3, matrix products, convolve(): lax.conv_general_dilated(inputs, kernel, (1, 1), 'SAME', dimension_number...  58.5 us
    all_to_all x1, waiting for transfers between devices, per_device(): lax.all_to_all(coil_maps, 'gy', split_axis=3, concat_axis=0, tiled=True)  22.6 us
    all_to_all x1, starting transfers between devices, per_device(): whole = lax.all_to_all(field, 'gy', split_axis=2, concat_axis=0, tiled=True)  7.39 us
    all_to_all x1, starting transfers between devices, per_device(): lax.all_to_all(normal_whole, 'gy', split_axis=0, concat_axis=2, tiled=True)  6.81 us
    all_to_all x1, waiting for transfers between devices, per_device(): lax.all_to_all(normal_whole, 'gy', split_axis=0, concat_axis=2, tiled=True)  6.25 us
    unnamed x22, local copies, waits for them, and re-layouts  4.72 us
    all_to_all x1, waiting for transfers between devices, per_device(): whole = lax.all_to_all(field, 'gy', split_axis=2, concat_axis=0, tiled=True)  4 us
    all_to_all x1, starting transfers between devices, per_device(): lax.all_to_all(coil_maps, 'gy', split_axis=3, concat_axis=0, tiled=True)  3.65 us
  transfers between devices with their start and end apart: 3, of which 3 were waited for; matrix products, arithmetic and copies ran while one was open for 3% of the time, Pallas kernels for 0%

commit v1 on v0

v1 whole, which is shorter than its diff:
```python
import functools

import jax
import jax.numpy as jnp
from jax import lax
from jax.experimental import pallas as pl
from jax.experimental.pallas import tpu as pltpu
from jax.sharding import PartitionSpec as P

FOLDS = 4
GROUP = 16
QUAD = 4
PAD = 8

VMEM = pl.BlockSpec(memory_space=pltpu.VMEM)
SMEM = pl.BlockSpec(memory_space=pltpu.SMEM)


def fold_kernel(share_ref, maps_ref, field_ref, one_ref, two_ref, three_ref, offs_ref, out0, out1, out2, out3):
    coils = maps_ref.shape[2]
    offs = offs_ref[...]
    pieces = (None, one_ref, two_ref, three_ref)
    outs = (out0, out1, out2, out3)
    turned = []
    units = []
    for k in range(FOLDS):
        if k == 0:
            real, imag = field_ref[0, 0], field_ref[0, 1]
            turned.append((real, imag))
            units.append(None)
            continue
        piece = pieces[k]
        real = piece[0, coils].astype(jnp.float32) + piece[0, coils + 1].astype(jnp.float32)
        imag = piece[1, coils].astype(jnp.float32) + piece[1, coils + 1].astype(jnp.float32)
        turns = (k * offs) & 3
        zero, one = jnp.zeros_like(real), jnp.ones_like(real)
        cosine = jnp.where(turns == 0, one, jnp.where(turns == 2, -one, zero))
        sine = jnp.where(turns == 1, one, jnp.where(turns == 3, -one, zero))
        units.append((cosine, sine))
        turned.append((cosine * real - sine * imag, cosine * imag + sine * real))

    def step(c, sums):
        maps = []
        fold_real = fold_imag = None
        for k in range(FOLDS):
            if k == 0:
                real, imag = maps_ref[0, 0, c], maps_ref[0, 1, c]
            else:
                real, imag = pieces[k][0, c], pieces[k][1, c]
            real, imag = real.astype(jnp.float32), imag.astype(jnp.float32)
            maps.append((real, imag))
            term_real = real * turned[k][0] - imag * turned[k][1]
            term_imag = real * turned[k][1] + imag * turned[k][0]
            fold_real = term_real if k == 0 else fold_real + term_real
            fold_imag = term_imag if k == 0 else fold_imag + term_imag
        new = []
        for k in range(FOLDS):
            real, imag = maps[k]
            new.append(sums[2 * k] + (real * fold_real + imag * fold_imag))
            new.append(sums[2 * k + 1] + (real * fold_imag - imag * fold_real))
        return tuple(new)

    zeros = tuple(jnp.zeros(offs.shape, jnp.float32) for _ in range(2 * FOLDS))
    sums = lax.fori_loop(0, coils, step, zeros, unroll=4)
    for k in range(FOLDS):
        real, imag = 0.25 * sums[2 * k], 0.25 * sums[2 * k + 1]
        if k == 0:
            outs[k][0], outs[k][1] = real, imag
        else:
            cosine, sine = units[k]
            outs[k][0] = cosine * real + sine * imag
            outs[k][1] = cosine * imag - sine * real


def fold(share, coil_maps, field, pieces, offs):
    _, _, coils, _, z = coil_maps.shape
    rows = offs.shape[0]
    whole = lambda *shape: pl.BlockSpec(shape, lambda i, s: (0,) * len(shape))
    spec = pltpu.PrefetchScalarGridSpec(
        num_scalar_prefetch=1,
        grid=(1,),
        in_specs=[
            pl.BlockSpec((1, 2, coils, rows, z), lambda i, s: (0, 0, 0, s[0], 0)),
            pl.BlockSpec((1, 2, rows, z), lambda i, s: (0, 0, s[0], 0)),
            whole(*pieces[0].shape),
            whole(*pieces[1].shape),
            whole(*pieces[2].shape),
            whole(rows, z),
        ],
        out_specs=[whole(2, rows, z)] * FOLDS,
    )
    return pl.pallas_call(
        fold_kernel,
        grid_spec=spec,
        out_shape=[jax.ShapeDtypeStruct((2, rows, z), jnp.float32)] * FOLDS,
        cost_estimate=pl.CostEstimate(flops=70 * coils * rows * z, bytes_accessed=16 * coils * rows * z, transcendentals=0),
        name="fold",
    )(share, coil_maps, field, *pieces, offs)


def shifted(value, lane, tap, width):
    if tap == 1:
        return value
    if tap == 0:
        return jnp.where(lane == 0, 0.0, pltpu.roll(value, 1, 1))
    return jnp.where(lane == width - 1, 0.0, pltpu.roll(value, width - 1, 1))


def denoise_kernel(
    share_ref, step_ref, tail_ref, field_ref, own_ref, one_ref, two_ref, three_ref,
    w1_ref, b1_ref, w2_ref, b2_ref, w3_ref, out_ref, padded, window, low, hidden_one, hidden_two,
):
    _, _, x_size, z = field_ref.shape
    rows = own_ref.shape[1]
    ch = b1_ref.shape[0]
    share = share_ref[0]
    step = step_ref[0]
    groups = x_size // GROUP
    for k, ref in enumerate((own_ref, one_ref, two_ref, three_ref)):
        start = pl.multiple_of(((share + k) % FOLDS) * rows, rows)
        for part in range(2):
            padded[part, pl.ds(PAD + start, rows), :] = ref[part]
    edge = jnp.zeros((PAD, z), jnp.float32)
    for part in range(2):
        padded[part, 0:PAD, :] = edge
        padded[part, PAD + x_size : PAD + x_size + PAD, :] = edge
        base = field_ref[0, part]
        stepped = base - step * (padded[part, PAD : PAD + x_size, :] - base)
        padded[part, PAD : PAD + x_size, :] = stepped
    lane = lax.broadcasted_iota(jnp.int32, (x_size + 2 * PAD, z), 1)
    for tap in range(3):
        for part in range(2):
            window[tap, part] = shifted(padded[part], lane, tap, z).astype(jnp.bfloat16)
    span = GROUP + 2 * PAD
    for g in range(groups):
        for tap in range(3):
            for part in range(2):
                low[(tap * 2 + part) * span : (tap * 2 + part + 1) * span, g * z : (g + 1) * z] = window[
                    tap, part, g * GROUP : g * GROUP + span, :
                ]
    empty = jnp.zeros((ch, z), jnp.bfloat16)
    for tap in range(3):
        hidden_one[tap, 0:ch, :] = empty
        hidden_one[tap, (x_size + 1) * ch : (x_size + 2) * ch, :] = empty
    hidden_two[0:ch, :] = empty
    hidden_two[(x_size + 1) * ch : (x_size + 2) * ch, :] = empty

    lane = lax.broadcasted_iota(jnp.int32, (ch, z), 1)
    bias = b1_ref[...]
    for r in range(0, GROUP, QUAD):
        for g in range(0, groups, 2):
            out = jnp.dot(
                w1_ref[r * ch : (r + QUAD) * ch, :], low[:, g * z : (g + 2) * z], preferred_element_type=jnp.float32
            )
            for i in range(QUAD):
                for j in range(2):
                    value = jnp.maximum(out[i * ch : (i + 1) * ch, j * z : (j + 1) * z] + bias, 0.0)
                    row = (g + j) * GROUP + r + i + 1
                    for tap in range(3):
                        hidden_one[tap, row * ch : (row + 1) * ch, :] = shifted(value, lane, tap, z).astype(jnp.bfloat16)

    bias = b2_ref[...]
    half = x_size // 2
    for q in range(0, half, QUAD):
        column = lambda first: jnp.concatenate(
            [hidden_one[tap, first * ch : (first + QUAD + 2) * ch, :] for tap in range(3)], axis=0
        )
        out = jnp.dot(
            w2_ref[...], jnp.concatenate([column(q), column(q + half)], axis=1), preferred_element_type=jnp.float32
        )
        for i in range(QUAD):
            for j in range(2):
                value = jnp.maximum(out[i * ch : (i + 1) * ch, j * z : (j + 1) * z] + bias, 0.0)
                row = q + j * half + i + 1
                hidden_two[row * ch : (row + 1) * ch, :] = value.astype(jnp.bfloat16)

    lane = lax.broadcasted_iota(jnp.int32, (2 * GROUP, z), 1)
    for g in range(0, groups, 2):
        column = lambda first: hidden_two[first * GROUP * ch : (first * GROUP + GROUP + 2) * ch, :]
        out = jnp.dot(
            w3_ref[...], jnp.concatenate([column(g), column(g + 1)], axis=1), preferred_element_type=jnp.float32
        )
        for j in range(2):
            total = None
            for tap in range(3):
                part = out[tap * 2 * GROUP : (tap + 1) * 2 * GROUP, j * z : (j + 1) * z]
                part = shifted(part, lane, tap, z)
                total = part if total is None else total + part
            first = (g + j) * GROUP
            for part in range(2):
                out_ref[0, part, first : first + GROUP, :] = (
                    padded[part, PAD + first : PAD + first + GROUP, :]
                    + total[part * GROUP : (part + 1) * GROUP]
                    + tail_ref[part]
                )


def denoise(share, step, field, normals, weights):
    _, _, x_size, z = field.shape
    w1, b1, w2, b2, w3, b_out = weights
    ch = b1.shape[0]
    span = GROUP + 2 * PAD
    return pl.pallas_call(
        denoise_kernel,
        in_specs=[SMEM, SMEM, SMEM] + [VMEM] * 10,
        out_specs=VMEM,
        out_shape=jax.ShapeDtypeStruct(field.shape, jnp.float32),
        scratch_shapes=[
            pltpu.VMEM((2, x_size + 2 * PAD, z), jnp.float32),
            pltpu.VMEM((3, 2, x_size + 2 * PAD, z), jnp.bfloat16),
            pltpu.VMEM((6 * span, x_size // GROUP * z), jnp.bfloat16),
            pltpu.VMEM((3, (x_size + 2) * ch, z), jnp.bfloat16),
            pltpu.VMEM(((x_size + 2) * ch, z), jnp.bfloat16),
        ],
        cost_estimate=pl.CostEstimate(flops=4_000_000_000, bytes_accessed=2_000_000, transcendentals=0),
        name="denoise",
    )(share, step, b_out, field, *normals, w1, b1, w2, b2, w3)


def banded(kernel, axis, copies, length, first, at):
    taps = kernel.shape[axis]
    rows = []
    for r in range(copies):
        pads = [(0, 0)] * kernel.ndim
        pads[axis] = (r + first, length - taps - r - first)
        rows.append(jnp.pad(kernel, pads))
    return jnp.stack(rows, axis=at)


def prepare(w_in, b_in, w_mid, b_mid, w_out, b_out, z):
    ch = w_mid.shape[0]
    span = GROUP + 2 * PAD
    w1 = banded(w_in.transpose(0, 3, 1, 2), 3, GROUP, span, PAD - 1, 0).reshape(GROUP * ch, 6 * span)
    w2 = banded(w_mid.transpose(0, 3, 2, 1), 2, QUAD, QUAD + 2, 0, 0).reshape(QUAD * ch, 3 * (QUAD + 2) * ch)
    w3 = banded(w_out.transpose(3, 0, 2, 1), 2, GROUP, GROUP + 2, 0, 2).reshape(6 * GROUP, (GROUP + 2) * ch)
    b1 = jnp.broadcast_to(b_in[:, None], (ch, z))
    b2 = jnp.broadcast_to(b_mid[:, None], (ch, z))
    return w1, b1, w2, b2, w3, b_out


def per_device(zero_filled, coil_maps, offsets, step_sizes, w_in, b_in, w_mid, b_mid, w_out, b_out):
    devices = lax.axis_size("gy")
    stride = devices // FOLDS
    x_size, z = zero_filled.shape[2:]
    rows = x_size // FOLDS
    share = lax.axis_index("gy") // stride

    def pairs(k):
        return [(j, (j + k * stride) % devices) for j in range(devices)]

    high = lax.reduce_precision(zero_filled[0], exponent_bits=8, mantissa_bits=7)
    split = jnp.stack([high.astype(jnp.bfloat16), (zero_filled[0] - high).astype(jnp.bfloat16)], axis=1)
    pieces = []
    for k in range(1, FOLDS):
        first = ((share + k) % FOLDS) * rows
        piece = jnp.concatenate(
            [
                lax.dynamic_slice_in_dim(coil_maps[0], first, rows, 2),
                lax.dynamic_slice_in_dim(split, first, rows, 2),
            ],
            axis=1,
        )
        pieces.append(lax.ppermute(piece, "gy", pairs(k)))
    weights = prepare(w_in, b_in, w_mid, b_mid, w_out, b_out, z)
    offs = lax.dynamic_slice_in_dim(offsets, share * rows, rows, 0)
    offs = jnp.broadcast_to(offs[:, None], (rows, z))
    index = jnp.reshape(share, (1,)).astype(jnp.int32)
    normals = fold(index, coil_maps, zero_filled, pieces, offs)
    normals = [normals[0]] + [lax.ppermute(normals[k], "gy", pairs(-k)) for k in range(1, FOLDS)]
    return denoise(index, step_sizes, zero_filled, normals, weights)


def solution(mesh):
    in_specs = (
        P(("parts", "gy"), None, None, None),
        P(("parts", "gy"), None, None, None, None),
        P("parts"),
        P(),
        P(),
        P(),
        P(),
        P(),
        P(),
        P(),
    )
    out_specs = P(("parts", "gy"), None, None, None)
    return jax.shard_map(
        per_device, mesh=mesh, in_specs=in_specs, out_specs=out_specs, check_vma=False
    )
```

time: 122 us -> 50 us (0.41)
  matrix products: 58.5 us -> 0 us
  waiting for transfers between devices: 32.9 us -> 15 us
  Pallas kernels: 0 us -> 7.1 us
  other arithmetic: 4.21 us -> 1.26 us
  local copies, waits for them, and re-layouts: 7.39 us -> 10.3 us
  starting transfers between devices: 17.9 us -> 15.2 us
    conv_general_dilated x3 -> x0, matrix products: 58.5 us -> none  [convolve(): lax.conv_general_dilated(inputs, kernel, (1, 1), 'SAME', dimension_number...]
    all_to_all x3 -> x0, waiting for transfers between devices: 32.9 us -> none  [the longest x1 22.6 us: per_device(): lax.all_to_all(coil_maps, 'gy', split_axis=3, concat_axis=0, tiled=True)]
    all_to_all x3 -> x0, starting transfers between devices: 17.9 us -> none  [the longest x1 7.39 us: per_device(): whole = lax.all_to_all(field, 'gy', split_axis=2, concat_axis=0, tiled=True)]
    ppermute x0 -> x6, starting transfers between devices: none -> 15.2 us  [the longest x3 8.08 us: per_device(): lax.ppermute(normals[k], 'gy', pairs(-k))]
    ppermute x0 -> x6, waiting for transfers between devices: none -> 15 us  [the longest x3 15 us: per_device(): pieces.append(lax.ppermute(piece, 'gy', pairs(k)))]
    pallas_call x0 -> x2, Pallas kernels: none -> 7.1 us  [the longest x1 4.57 us: denoise(): pl.pallas_call(denoise_kernel, in_specs=[SMEM, SMEM, SMEM] + [VMEM] * 10,...]
    reshape x0 -> x5, local copies, waits for them, and re-layouts: none -> 5.05 us  [the longest x2 2.51 us: prepare(): banded(w_mid.transpose(0, 3, 2, 1), 2, QUAD, QUAD + 2, 0, 0)]
    unnamed x22 -> x48, local copies, waits for them, and re-layouts: 4.72 us -> 0.98 us
  transfers between devices with their start and end apart: 3 -> 6, of which waited for: 3 -> 2; matrix products, arithmetic and copies ran while one was open for 3% -> 15% of each run, Pallas kernels for 0% -> 0%
where the time goes in v1:
time: 50 us; the launch traced here: 49.8 us
  starting transfers between devices  15.2 us (30%)
  waiting for transfers between devices  15 us (30%)
  local copies, waits for them, and re-layouts  10.3 us (21%)
  Pallas kernels  7.1 us (14%)
  other arithmetic  1.26 us (3%)
  between operations  0.88 us (2%)
    ppermute x3, waiting for transfers between devices, per_device(): pieces.append(lax.ppermute(piece, 'gy', pairs(k)))  15 us
    ppermute x3, starting transfers between devices, per_device(): lax.ppermute(normals[k], 'gy', pairs(-k))  8.08 us
    ppermute x3, starting transfers between devices, per_device(): pieces.append(lax.ppermute(piece, 'gy', pairs(k)))  7.13 us
    pallas_call x1, Pallas kernels, denoise(): pl.pallas_call(denoise_kernel, in_specs=[SMEM, SMEM, SMEM] + [VMEM] * 10,...  4.57 us
    pallas_call x1, Pallas kernels, fold(): pl.pallas_call(fold_kernel, grid_spec=spec, out_shape=[jax.ShapeDtypeStru...  2.52 us
    reshape x2, local copies, waits for them, and re-layouts, prepare(): banded(w_mid.transpose(0, 3, 2, 1), 2, QUAD, QUAD + 2, 0, 0)  2.51 us
    reshape x2, local copies, waits for them, and re-layouts, prepare(): banded(w_in.transpose(0, 3, 1, 2), 3, GROUP, span, PAD - 1, 0)  1.53 us
    dynamic_slice x1, local copies, waits for them, and re-layouts, per_device(): lax.dynamic_slice_in_dim(coil_maps[0], first, rows, 2)  1.27 us
  transfers between devices with their start and end apart: 6, of which 2 were waited for; matrix products, arithmetic and copies ran while one was open for 15% of the time, Pallas kernels for 0%

profile of v1, /device:TPU:0, one launch (start us, length us, event | category | flops | bytes accessed | tf_op | source)
XLA Modules:
  0.0 49.8 jit_solution(1489325471628313650)
XLA Ops:
  0.0 0.9 %fusion = (bf16[2,1,64,128]{3,2,1,0:T(8,128)(2,1)S(1)}, bf16[2,1,64,128]{3,2,1,0:T(8,128)(2,1)S(1)}) fusion(f32[1,2,64,128]{3,2,1,0:T(8,128)} %field_ref.3), kind=kLoop, calls=%fused_computation.51 | loop fusion | flops 65536 | bytes 131072 | tf_op jit(solution)/shard_map/convert_element_type | solution.py:252
  0.9 1.3 %dynamic-slice_bitcast_fusion = (bf16[2,32,16,128]{3,2,1,0:T(8,128)(2,1)S(1)}, bf16[2,32,16,128]{3,2,1,0:T(8,128)(2,1)S(1)}, bf16[2,32,16,128]{3,2,1,0:T(8,128)(2,1)S(1)}) fusion(bf16[1,2,32,64,128]{4,3,2,1,0:T(8,128)(2,1)} %maps_ref.1, s32[]{:T(128)S(6)} %select_n.40, s32[]{:T(128)S(6)} %select_n.38, s32[]{:T(128)S(6)} %select_n.36), kind=kLoop, calls=%fused_computation.8 | loop fusion | bytes 1572876 | tf_op jit(solution)/shard_map/dynamic_slice | solution.py:258
  2.2 0.0 copy-start
  2.2 0.0 copy-start.1
  2.2 3.1 %collective-permute-start = (bf16[2,34,16,128]{3,2,1,0:T(8,128)(2,1)S(1)}, bf16[2,34,16,128]{3,2,1,0:T(8,128)(2,1)}, u32[]{:S(2)}, u32[]{:S(2)}) collective-permute-start(bf16[2,34,16,128]{3,2,1,0:T(8,128)(2,1)S(1)} %pad_maximum_fusion.1), channel_id=1, source_target_pairs={{0,4},{1,5},{2,6},{3,7},{4,8},{5,9},{6,10},{7,11},{8,12},{9,13},{1... | collective-permute-start | bytes 835592 | tf_op jit(solution)/shard_map/ppermute | solution.py:263
  5.3 0.0 copy-start.8
  5.3 0.0 copy-start.2
  5.3 2.7 %collective-permute-start.1 = (bf16[2,34,16,128]{3,2,1,0:T(8,128)(2,1)S(1)}, bf16[2,34,16,128]{3,2,1,0:T(8,128)(2,1)}, u32[]{:S(2)}, u32[]{:S(2)}) collective-permute-start(bf16[2,34,16,128]{3,2,1,0:T(8,128)(2,1)S(1)} %pad_maximum_fusion.2), channel_id=1, source_target_pairs={{0,8},{1,9},{2,10},{3,11},{4,12},{5,13},{6,14},{7,15},{8,0},{9,1},... | collective-permute-start | bytes 835592 | tf_op jit(solution)/shard_map/ppermute | solution.py:263
  8.0 1.4 %collective-permute-start.2 = (bf16[2,34,16,128]{3,2,1,0:T(8,128)(2,1)S(1)}, bf16[2,34,16,128]{3,2,1,0:T(8,128)(2,1)}, u32[]{:S(2)}, u32[]{:S(2)}) collective-permute-start(bf16[2,34,16,128]{3,2,1,0:T(8,128)(2,1)S(1)} %pad_maximum_fusion.3), channel_id=1, source_target_pairs={{0,12},{1,13},{2,14},{3,15},{4,0},{5,1},{6,2},{7,3},{8,4},{9,5},{1... | collective-permute-start | bytes 835592 | tf_op jit(solution)/shard_map/ppermute | solution.py:263
  9.4 0.0 copy-done
  10.1 0.0 copy-done.1
  10.5 0.0 copy-done.8
  10.5 0.1 dynamic_slice.36
  10.6 0.0 copy-done.2
  10.6 0.3 pad_bitcast_fusion.3
  10.9 0.3 pad_maximum_fusion
  11.2 3.9 %collective-permute-done.one_ref = bf16[2,34,16,128]{3,2,1,0:T(8,128)(2,1)} collective-permute-done((bf16[2,34,16,128]{3,2,1,0:T(8,128)(2,1)S(1)}, bf16[2,34,16,128]{3,2,1,0:T(8,128)(2,1)}, u32[]{:S(2)}, u32[]{:S(2)}) %collective-permute-start) | collective-permute-done | bytes 278560 | tf_op jit(solution)/shard_map/ppermute | solution.py:263
  15.1 11.1 %collective-permute-done.1.two_ref = bf16[2,34,16,128]{3,2,1,0:T(8,128)(2,1)} collective-permute-done((bf16[2,34,16,128]{3,2,1,0:T(8,128)(2,1)S(1)}, bf16[2,34,16,128]{3,2,1,0:T(8,128)(2,1)}, u32[]{:S(2)}, u32[]{:S(2)}) %collective-permute-start.1) | collective-permute-done | bytes 278560 | tf_op jit(solution)/shard_map/ppermute | solution.py:263
  26.2 0.0 collective-permute-done.2.three_ref
  26.2 0.7 %broadcast_in_dim.6.offs_ref = s32[16,128]{1,0:T(8,128)} broadcast(s32[16]{0:T(128)S(1)} %dynamic_slice.36), dimensions={0} | broadcast | bytes 8256 | tf_op jit(solution)/shard_map/broadcast_in_dim | solution.py:266
  26.8 2.5 %fold.1 = (f32[2,16,128]{2,1,0:T(8,128)}, f32[2,16,128]{2,1,0:T(8,128)}, f32[2,16,128]{2,1,0:T(8,128)}, f32[2,16,128]{2,1,0:T(8,128)}) custom-call(s32[1]{0:T(128)} %bitcast.share_ref, bf16[1,2,32,64,128]{4,3,2,1,0:T(8,128)(2,1)} %maps_ref.1, f32[1,2,64,128]{3,2,1,0:T(8,128)} %field_ref.3, bf16[2,34,16,128]{3,2,1,0:T(8,128)(2,1)} %collective-permute-done.one_ref, ...), custom_call_target="tpu_custom_call" | custom-call | flops 4587520 | bytes 1048576 | tf_op jit(solution)/shard_map/fold/pallas_call | solution.py:92
  29.4 7.5 %collective-permute-start.3 = (f32[2,16,128]{2,1,0:T(8,128)}, f32[2,16,128]{2,1,0:T(8,128)S(1)}, u32[]{:S(2)}, u32[]{:S(2)}) collective-permute-start(f32[2,16,128]{2,1,0:T(8,128)} %get-tuple-element.10), channel_id=1, source_target_pairs={{0,12},{1,13},{2,14},{3,15},{4,0},{5,1},{6,2},{7,3},{8,4},{9,5},{1... | collective-permute-start | bytes 49160 | tf_op jit(solution)/shard_map/ppermute | solution.py:269
  36.8 0.4 collective-permute-start.4
  37.3 0.2 collective-permute-start.5
  38.1 0.5 %copy.14 = bf16[16,64,3,2,32]{1,0,4,3,2:T(8,128)(2,1)S(1)} copy(bf16[16,64,3,2,32]{1,3,2,4,0:T(2,128)(2,1)S(1)} %constant_dynamic-update-slice_fusion) | data formatting | bytes 786432 | tf_op jit(solution)/shard_map/stack | solution.py:227
  38.6 0.5 %reshape.48 = bf16[1024,192]{0,1:T(8,128)(2,1)S(1)} reshape(bf16[16,64,3,2,32]{1,0,4,3,2:T(8,128)(2,1)S(1)} %copy.14) | data formatting | bytes 786432 | tf_op jit(solution)/shard_map/reshape | solution.py:233
  39.2 1.0 %copy.17.w1_ref = bf16[1024,192]{1,0:T(8,128)(2,1)} copy(bf16[1024,192]{0,1:T(8,128)(2,1)S(1)} %reshape.48) | data formatting | bytes 786432 | tf_op jit(solution)/shard_map/reshape | solution.py:233
  40.2 0.8 %copy.19 = bf16[4,64,3,6,64]{4,3,2,1,0:T(8,128)(2,1)S(1)} copy(bf16[4,64,3,6,64]{4,1,2,3,0:T(8,128)(2,1)S(1)} %pad_maximum_fusion) | data formatting | bytes 1179648 | tf_op jit(solution)/shard_map/reshape | solution.py:234
  41.0 1.7 %reshape.51.w2_ref = bf16[256,1152]{1,0:T(8,128)(2,1)} reshape(bf16[4,64,3,6,64]{4,3,2,1,0:T(8,128)(2,1)S(1)} %copy.19) | data formatting | bytes 1179648 | tf_op jit(solution)/shard_map/reshape | solution.py:234
  42.7 0.0 copy-start.3
  42.7 0.0 copy-start.4
  42.7 0.1 copy.16
  42.8 1.0 %reshape.50.w3_ref = bf16[96,1152]{1,0:T(8,128)(2,1)} reshape(bf16[3,2,16,18,64]{4,3,2,1,0:T(8,128)(2,1)S(1)} %copy.16) | data formatting | bytes 442368 | tf_op jit(solution)/shard_map/reshape | solution.py:235
  43.8 0.0 collective-permute-done.3.one_ref
  43.8 0.0 copy-start.5
  43.8 0.0 collective-permute-done.4.two_ref
  43.8 0.0 copy-start.6
  43.8 0.0 collective-permute-done.5.three_ref
  43.8 0.0 copy-start.7
  43.8 0.0 copy-done.3
  43.9 0.7 %broadcast_in_dim.7.b1_ref = f32[64,128]{1,0:T(8,128)} broadcast(f32[64]{0:T(128)S(1)} %copy-done.3), dimensions={0} | broadcast | bytes 33024 | tf_op jit(solution)/shard_map/broadcast_in_dim | solution.py:236
  44.5 0.0 copy-done.4
  44.5 0.7 %broadcast_in_dim.8.b2_ref = f32[64,128]{1,0:T(8,128)} broadcast(f32[64]{0:T(128)S(1)} %copy-done.4), dimensions={0} | broadcast | bytes 33024 | tf_op jit(solution)/shard_map/broadcast_in_dim | solution.py:237
  45.2 0.0 copy-done.5
  45.2 0.0 copy-done.6
  45.2 0.0 copy-done.7
  45.2 4.6 %denoise.1 = f32[1,2,64,128]{3,2,1,0:T(8,128)} custom-call(s32[1]{0:T(128)} %bitcast.share_ref, f32[1]{0:T(128)S(6)} %copy.51.step_ref, f32[2]{0:T(128)} %tail_ref.1, f32[1,2,64,128]{3,2,1,0:T(8,128)} %field_ref.3, f32[2,16,128]{2,1,0:T(8,128)} %get-tuple-element.9.own_ref, f32[2,16,128]{2,1,0:T(8,128)} %copy-done.5, f32[2,16,128]{2,1,0:T(8,128)} %copy-done.6, ...), custom_call_target="tpu_custom_call" | custom-call | flops 4000000000 | bytes 2000000 | tf_op jit(solution)/shard_map/denoise/pallas_call | solution.py:203
  (36 shorter events, 1.1 us)
Async XLA Ops:
  2.2 7.3 %copy-start = (bf16[64,2,3,3]{0,1,3,2:T(2,128)(2,1)S(1)}, bf16[64,2,3,3]{0,1,3,2:T(2,128)(2,1)}, u32[]{:S(2)}) copy-start(bf16[64,2,3,3]{0,1,3,2:T(2,128)(2,1)} %param.14) | copy-start | bytes 6916
  2.2 7.9 %copy-start.1 = (bf16[2,64,3,3]{1,0,3,2:T(2,128)(2,1)S(1)}, bf16[2,64,3,3]{1,0,3,2:T(2,128)(2,1)}, u32[]{:S(2)}) copy-start(bf16[2,64,3,3]{1,0,3,2:T(2,128)(2,1)} %param.18) | copy-start | bytes 6916
  2.2 12.8 %collective-permute-start = (bf16[2,34,16,128]{3,2,1,0:T(8,128)(2,1)S(1)}, bf16[2,34,16,128]{3,2,1,0:T(8,128)(2,1)}, u32[]{:S(2)}, u32[]{:S(2)}) collective-permute-start(bf16[2,34,16,128]{3,2,1,0:T(8,128)(2,1)S(1)} %pad_maximum_fusion.1), channel_id=1, source_target_pairs={{0,4},{1,5},{2,6},{3,7},{4,8},{5,9},{6,10},{7,11},{8,12},{9,13},{1... | collective-permute-start | bytes 835592 | tf_op jit(solution)/shard_map/ppermute | solution.py:263
  5.3 5.2 %copy-start.8 = (s32[64]{0:T(128)S(1)}, s32[64]{0:T(128)}, u32[]{:S(2)}) copy-start(s32[64]{0:T(128)} %param.12) | copy-start | bytes 772
  5.3 5.3 %copy-start.2 = (bf16[64,64,3,3]{1,0,3,2:T(8,128)(2,1)S(1)}, bf16[64,64,3,3]{1,0,3,2:T(8,128)(2,1)}, u32[]{:S(2)}) copy-start(bf16[64,64,3,3]{1,0,3,2:T(8,128)(2,1)} %param.16) | copy-start | bytes 221188
  5.3 20.8 %collective-permute-start.1 = (bf16[2,34,16,128]{3,2,1,0:T(8,128)(2,1)S(1)}, bf16[2,34,16,128]{3,2,1,0:T(8,128)(2,1)}, u32[]{:S(2)}, u32[]{:S(2)}) collective-permute-start(bf16[2,34,16,128]{3,2,1,0:T(8,128)(2,1)S(1)} %pad_maximum_fusion.2), channel_id=1, source_target_pairs={{0,8},{1,9},{2,10},{3,11},{4,12},{5,13},{6,14},{7,15},{8,0},{9,1},... | collective-permute-start | bytes 835592 | tf_op jit(solution)/shard_map/ppermute | solution.py:263
  8.0 18.1 %collective-permute-start.2 = (bf16[2,34,16,128]{3,2,1,0:T(8,128)(2,1)S(1)}, bf16[2,34,16,128]{3,2,1,0:T(8,128)(2,1)}, u32[]{:S(2)}, u32[]{:S(2)}) collective-permute-start(bf16[2,34,16,128]{3,2,1,0:T(8,128)(2,1)S(1)} %pad_maximum_fusion.3), channel_id=1, source_target_pairs={{0,12},{1,13},{2,14},{3,15},{4,0},{5,1},{6,2},{7,3},{8,4},{9,5},{1... | collective-permute-start | bytes 835592 | tf_op jit(solution)/shard_map/ppermute | solution.py:263
  29.4 14.4 %collective-permute-start.3 = (f32[2,16,128]{2,1,0:T(8,128)}, f32[2,16,128]{2,1,0:T(8,128)S(1)}, u32[]{:S(2)}, u32[]{:S(2)}) collective-permute-start(f32[2,16,128]{2,1,0:T(8,128)} %get-tuple-element.10), channel_id=1, source_target_pairs={{0,12},{1,13},{2,14},{3,15},{4,0},{5,1},{6,2},{7,3},{8,4},{9,5},{1... | collective-permute-start | bytes 49160 | tf_op jit(solution)/shard_map/ppermute | solution.py:269
  36.8 7.0 %collective-permute-start.4 = (f32[2,16,128]{2,1,0:T(8,128)}, f32[2,16,128]{2,1,0:T(8,128)S(1)}, u32[]{:S(2)}, u32[]{:S(2)}) collective-permute-start(f32[2,16,128]{2,1,0:T(8,128)} %get-tuple-element.11), channel_id=1, source_target_pairs={{0,8},{1,9},{2,10},{3,11},{4,12},{5,13},{6,14},{7,15},{8,0},{9,1},... | collective-permute-start | bytes 49160 | tf_op jit(solution)/shard_map/ppermute | solution.py:269
  37.3 6.6 %collective-permute-start.5 = (f32[2,16,128]{2,1,0:T(8,128)}, f32[2,16,128]{2,1,0:T(8,128)S(1)}, u32[]{:S(2)}, u32[]{:S(2)}) collective-permute-start(f32[2,16,128]{2,1,0:T(8,128)} %get-tuple-element.12), channel_id=1, source_target_pairs={{0,4},{1,5},{2,6},{3,7},{4,8},{5,9},{6,10},{7,11},{8,12},{9,13},{1... | collective-permute-start | bytes 49160 | tf_op jit(solution)/shard_map/ppermute | solution.py:269
  42.7 1.1 %copy-start.3 = (f32[64]{0:T(128)S(1)}, f32[64]{0:T(128)}, u32[]{:S(2)}) copy-start(f32[64]{0:T(128)} %param.15) | copy-start | bytes 772
  42.7 1.8 %copy-start.4 = (f32[64]{0:T(128)S(1)}, f32[64]{0:T(128)}, u32[]{:S(2)}) copy-start(f32[64]{0:T(128)} %param.17) | copy-start | bytes 772
  43.8 1.4 %copy-start.5 = (f32[2,16,128]{2,1,0:T(8,128)}, f32[2,16,128]{2,1,0:T(8,128)S(1)}, u32[]{:S(2)}) copy-start(f32[2,16,128]{2,1,0:T(8,128)S(1)} %collective-permute-done.3.one_ref) | copy-start | bytes 49156
  43.8 1.4 %copy-start.6 = (f32[2,16,128]{2,1,0:T(8,128)}, f32[2,16,128]{2,1,0:T(8,128)S(1)}, u32[]{:S(2)}) copy-start(f32[2,16,128]{2,1,0:T(8,128)S(1)} %collective-permute-done.4.two_ref) | copy-start | bytes 49156
  43.8 1.4 %copy-start.7 = (f32[2,16,128]{2,1,0:T(8,128)}, f32[2,16,128]{2,1,0:T(8,128)S(1)}, u32[]{:S(2)}) copy-start(f32[2,16,128]{2,1,0:T(8,128)S(1)} %collective-permute-done.5.three_ref) | copy-start | bytes 49156

commit v2 on v1

--- a/solution.py
+++ b/solution.py
@@ -1,5 +1,3 @@
-import functools
-
 import jax
 import jax.numpy as jnp
 from jax import lax
@@ -10,6 +8,7 @@
 FOLDS = 4
 GROUP = 16
 QUAD = 4
+PAIR = 2
 PAD = 8
 
 VMEM = pl.BlockSpec(memory_space=pltpu.VMEM)
@@ -18,6 +17,7 @@
 
 def fold_kernel(share_ref, maps_ref, field_ref, one_ref, two_ref, three_ref, offs_ref, out0, out1, out2, out3):
     coils = maps_ref.shape[2]
+    share = share_ref[0]
     offs = offs_ref[...]
     pieces = (None, one_ref, two_ref, three_ref)
     outs = (out0, out1, out2, out3)
@@ -32,10 +32,10 @@
         piece = pieces[k]
         real = piece[0, coils].astype(jnp.float32) + piece[0, coils + 1].astype(jnp.float32)
         imag = piece[1, coils].astype(jnp.float32) + piece[1, coils + 1].astype(jnp.float32)
-        turns = (k * offs) & 3
+        turns = (((share ^ k) - share) * offs) & 3
         zero, one = jnp.zeros_like(real), jnp.ones_like(real)
         cosine = jnp.where(turns == 0, one, jnp.where(turns == 2, -one, zero))
-        sine = jnp.where(turns == 1, one, jnp.where(turns == 3, -one, zero))
+        sine = jnp.where(turns == 3, one, jnp.where(turns == 1, -one, zero))
         units.append((cosine, sine))
         turned.append((cosine * real - sine * imag, cosine * imag + sine * real))
 
@@ -94,6 +94,7 @@
         grid_spec=spec,
         out_shape=[jax.ShapeDtypeStruct((2, rows, z), jnp.float32)] * FOLDS,
         cost_estimate=pl.CostEstimate(flops=70 * coils * rows * z, bytes_accessed=16 * coils * rows * z, transcendentals=0),
+        compiler_params=pltpu.CompilerParams(vmem_limit_bytes=8 << 20),
         name="fold",
     )(share, coil_maps, field, *pieces, offs)
 
@@ -117,7 +118,7 @@
     step = step_ref[0]
     groups = x_size // GROUP
     for k, ref in enumerate((own_ref, one_ref, two_ref, three_ref)):
-        start = pl.multiple_of(((share + k) % FOLDS) * rows, rows)
+        start = pl.multiple_of((share ^ k) * rows, rows)
         for part in range(2):
             padded[part, pl.ds(PAD + start, rows), :] = ref[part]
     edge = jnp.zeros((PAD, z), jnp.float32)
@@ -139,13 +140,10 @@
                     tap, part, g * GROUP : g * GROUP + span, :
                 ]
     empty = jnp.zeros((ch, z), jnp.bfloat16)
-    for tap in range(3):
-        hidden_one[tap, 0:ch, :] = empty
-        hidden_one[tap, (x_size + 1) * ch : (x_size + 2) * ch, :] = empty
-    hidden_two[0:ch, :] = empty
-    hidden_two[(x_size + 1) * ch : (x_size + 2) * ch, :] = empty
-
-    lane = lax.broadcasted_iota(jnp.int32, (ch, z), 1)
+    for hidden in (hidden_one, hidden_two):
+        hidden[0:ch, :] = empty
+        hidden[(x_size + 1) * ch : (x_size + 2) * ch, :] = empty
+
     bias = b1_ref[...]
     for r in range(0, GROUP, QUAD):
         for g in range(0, groups, 2):
@@ -156,23 +154,24 @@
                 for j in range(2):
                     value = jnp.maximum(out[i * ch : (i + 1) * ch, j * z : (j + 1) * z] + bias, 0.0)
                     row = (g + j) * GROUP + r + i + 1
-                    for tap in range(3):
-                        hidden_one[tap, row * ch : (row + 1) * ch, :] = shifted(value, lane, tap, z).astype(jnp.bfloat16)
+                    hidden_one[row * ch : (row + 1) * ch, :] = value.astype(jnp.bfloat16)
 
     bias = b2_ref[...]
+    lane = lax.broadcasted_iota(jnp.int32, (ch, z), 1)
     half = x_size // 2
-    for q in range(0, half, QUAD):
-        column = lambda first: jnp.concatenate(
-            [hidden_one[tap, first * ch : (first + QUAD + 2) * ch, :] for tap in range(3)], axis=0
-        )
+    for q in range(0, half, PAIR):
+        column = lambda first: hidden_one[first * ch : (first + PAIR + 2) * ch, :]
         out = jnp.dot(
             w2_ref[...], jnp.concatenate([column(q), column(q + half)], axis=1), preferred_element_type=jnp.float32
         )
-        for i in range(QUAD):
+        for i in range(PAIR):
             for j in range(2):
-                value = jnp.maximum(out[i * ch : (i + 1) * ch, j * z : (j + 1) * z] + bias, 0.0)
+                total = bias
+                for tap in range(3):
+                    first = (tap * PAIR + i) * ch
+                    total = total + shifted(out[first : first + ch, j * z : (j + 1) * z], lane, tap, z)
                 row = q + j * half + i + 1
-                hidden_two[row * ch : (row + 1) * ch, :] = value.astype(jnp.bfloat16)
+                hidden_two[row * ch : (row + 1) * ch, :] = jnp.maximum(total, 0.0).astype(jnp.bfloat16)
 
     lane = lax.broadcasted_iota(jnp.int32, (2 * GROUP, z), 1)
     for g in range(0, groups, 2):
@@ -195,9 +194,9 @@
                 )
 
 
-def denoise(share, step, field, normals, weights):
+def denoise(share, step, field, normals, weights, b_out):
     _, _, x_size, z = field.shape
-    w1, b1, w2, b2, w3, b_out = weights
+    w1, b1, w2, b2, w3 = weights
     ch = b1.shape[0]
     span = GROUP + 2 * PAD
     return pl.pallas_call(
@@ -209,33 +208,111 @@
             pltpu.VMEM((2, x_size + 2 * PAD, z), jnp.float32),
             pltpu.VMEM((3, 2, x_size + 2 * PAD, z), jnp.bfloat16),
             pltpu.VMEM((6 * span, x_size // GROUP * z), jnp.bfloat16),
-            pltpu.VMEM((3, (x_size + 2) * ch, z), jnp.bfloat16),
+            pltpu.VMEM(((x_size + 2) * ch, z), jnp.bfloat16),
             pltpu.VMEM(((x_size + 2) * ch, z), jnp.bfloat16),
         ],
         cost_estimate=pl.CostEstimate(flops=4_000_000_000, bytes_accessed=2_000_000, transcendentals=0),
+        compiler_params=pltpu.CompilerParams(vmem_limit_bytes=16 << 20),
         name="denoise",
     )(share, step, b_out, field, *normals, w1, b1, w2, b2, w3)
 
 
-def banded(kernel, axis, copies, length, first, at):
-    taps = kernel.shape[axis]
-    rows = []
-    for r in range(copies):
-        pads = [(0, 0)] * kernel.ndim
-        pads[axis] = (r + first, length - taps - r - first)
-        rows.append(jnp.pad(kernel, pads))
-    return jnp.stack(rows, axis=at)
-
-
-def prepare(w_in, b_in, w_mid, b_mid, w_out, b_out, z):
+def prepare_kernel(w_in_ref, b_in_ref, w_mid_ref, b_mid_ref, w_out_ref, w1_ref, b1_ref, w2_ref, b2_ref, w3_ref):
+    ch, z = b1_ref.shape
+    span = GROUP + 2 * PAD
+    b1_ref[...] = jnp.transpose(jnp.broadcast_to(b_in_ref[...], (z, ch)))
+    b2_ref[...] = jnp.transpose(jnp.broadcast_to(b_mid_ref[...], (z, ch)))
+    taps = w_in_ref[...]
+    row = lax.broadcasted_iota(jnp.int32, (18, 6 * span), 0)
+    column = lax.broadcasted_iota(jnp.int32, (18, 6 * span), 1)
+    place = (row % 6) * span + row // 6 + (PAD - 1)
+    for r in range(GROUP):
+        select = jnp.where(column == place + r, 1.0, 0.0).astype(jnp.bfloat16)
+        w1_ref[r * ch : (r + 1) * ch, :] = lax.dot_general(
+            taps, select, (((0,), (0,)), ((), ())), preferred_element_type=jnp.float32
+        ).astype(jnp.bfloat16)
+    w2_ref[...] = jnp.zeros_like(w2_ref)
+    for dz in range(3):
+        for dx in range(3):
+            block = w_mid_ref[dx, dz]
+            for r in range(PAIR):
+                first = (dz * PAIR + r) * ch
+                w2_ref[first : first + ch, (r + dx) * ch : (r + dx + 1) * ch] = block
+    wide = (GROUP, (GROUP + 2) * ch)
+    offset = lax.broadcasted_iota(jnp.int32, wide, 1) // ch - lax.broadcasted_iota(jnp.int32, wide, 0)
+    for dz in range(3):
+        for part in range(2):
+            total = jnp.zeros(wide, jnp.float32)
+            for dx in range(3):
+                line = w_out_ref[dx, dz, part : part + 1, :].astype(jnp.float32)
+                line = jnp.concatenate([line] * (GROUP + 2), axis=1)
+                total = jnp.where(offset == dx, jnp.broadcast_to(line, wide), total)
+            first = (dz * 2 + part) * GROUP
+            w3_ref[first : first + GROUP, :] = total.astype(jnp.bfloat16)
+
+
+def prepare(w_in, b_in, w_mid, b_mid, w_out, z):
     ch = w_mid.shape[0]
-    span = GROUP + 2 * PAD
-    w1 = banded(w_in.transpose(0, 3, 1, 2), 3, GROUP, span, PAD - 1, 0).reshape(GROUP * ch, 6 * span)
-    w2 = banded(w_mid.transpose(0, 3, 2, 1), 2, QUAD, QUAD + 2, 0, 0).reshape(QUAD * ch, 3 * (QUAD + 2) * ch)
-    w3 = banded(w_out.transpose(3, 0, 2, 1), 2, GROUP, GROUP + 2, 0, 2).reshape(6 * GROUP, (GROUP + 2) * ch)
-    b1 = jnp.broadcast_to(b_in[:, None], (ch, z))
-    b2 = jnp.broadcast_to(b_mid[:, None], (ch, z))
-    return w1, b1, w2, b2, w3, b_out
+    shapes = [
+        jax.ShapeDtypeStruct((GROUP * ch, 6 * (GROUP + 2 * PAD)), jnp.bfloat16),
+        jax.ShapeDtypeStruct((ch, z), jnp.float32),
+        jax.ShapeDtypeStruct((3 * PAIR * ch, (PAIR + 2) * ch), jnp.bfloat16),
+        jax.ShapeDtypeStruct((ch, z), jnp.float32),
+        jax.ShapeDtypeStruct((6 * GROUP, (GROUP + 2) * ch), jnp.bfloat16),
+    ]
+    return pl.pallas_call(
+        prepare_kernel,
+        in_specs=[VMEM] * 5,
+        out_specs=[VMEM] * 5,
+        out_shape=shapes,
+        cost_estimate=pl.CostEstimate(flops=1_000_000_000, bytes_accessed=8_000_000, transcendentals=0),
+        compiler_params=pltpu.CompilerParams(vmem_limit_bytes=8 << 20),
+        name="prepare",
+    )(
+        w_in.transpose(2, 3, 1, 0).reshape(18, ch),
+        b_in[None],
+        w_mid.transpose(2, 3, 0, 1),
+        b_mid[None],
+        w_out.transpose(2, 3, 0, 1),
+    )
+
+
+def pack_kernel(share_ref, maps_ref, field_ref, one_ref, two_ref, three_ref, sems):
+    coils = maps_ref.shape[2]
+    rows = one_ref.shape[2]
+    copies = []
+    for k, ref in ((2, two_ref), (1, one_ref), (3, three_ref)):
+        first = pl.multiple_of((share_ref[0] ^ k) * rows, rows)
+        for part in range(2):
+            copy = pltpu.make_async_copy(
+                maps_ref.at[0, part, :, pl.ds(first, rows), :], ref.at[part, 0:coils], sems.at[k - 1, part]
+            )
+            copy.start()
+            copies.append(copy)
+    for k, ref in ((2, two_ref), (1, one_ref), (3, three_ref)):
+        first = pl.multiple_of((share_ref[0] ^ k) * rows, rows)
+        for part in range(2):
+            value = field_ref[0, part, pl.ds(first, rows), :]
+            high = value.astype(jnp.bfloat16)
+            ref[part, coils] = high
+            ref[part, coils + 1] = (value - high.astype(jnp.float32)).astype(jnp.bfloat16)
+    for copy in copies:
+        copy.wait()
+
+
+def pack(share, coil_maps, field):
+    _, _, coils, x_size, z = coil_maps.shape
+    piece = jax.ShapeDtypeStruct((2, coils + 2, x_size // FOLDS, z), jnp.bfloat16)
+    return pl.pallas_call(
+        pack_kernel,
+        in_specs=[SMEM, pl.BlockSpec(memory_space=pltpu.HBM), VMEM],
+        out_specs=[VMEM] * 3,
+        out_shape=[piece] * 3,
+        scratch_shapes=[pltpu.SemaphoreType.DMA((3, 2))],
+        cost_estimate=pl.CostEstimate(flops=0, bytes_accessed=2_000_000, transcendentals=0),
+        compiler_params=pltpu.CompilerParams(vmem_limit_bytes=4 << 20),
+        name="pack",
+    )(share, coil_maps, field)
 
 
 def per_device(zero_filled, coil_maps, offsets, step_sizes, w_in, b_in, w_mid, b_mid, w_out, b_out):
@@ -246,28 +323,19 @@
     share = lax.axis_index("gy") // stride
 
     def pairs(k):
-        return [(j, (j + k * stride) % devices) for j in range(devices)]
-
-    high = lax.reduce_precision(zero_filled[0], exponent_bits=8, mantissa_bits=7)
-    split = jnp.stack([high.astype(jnp.bfloat16), (zero_filled[0] - high).astype(jnp.bfloat16)], axis=1)
-    pieces = []
-    for k in range(1, FOLDS):
-        first = ((share + k) % FOLDS) * rows
-        piece = jnp.concatenate(
-            [
-                lax.dynamic_slice_in_dim(coil_maps[0], first, rows, 2),
-                lax.dynamic_slice_in_dim(split, first, rows, 2),
-            ],
-            axis=1,
-        )
-        pieces.append(lax.ppermute(piece, "gy", pairs(k)))
-    weights = prepare(w_in, b_in, w_mid, b_mid, w_out, b_out, z)
+        return [(j, (j // stride ^ k) * stride + j % stride) for j in range(devices)]
+
+    index = jnp.reshape(share, (1,)).astype(jnp.int32)
+    pieces = pack(index, coil_maps, zero_filled)
+    pieces = {k: lax.ppermute(pieces[k - 1], "gy", pairs(k)) for k in (2, 3, 1)}
+    pieces = [pieces[k] for k in range(1, FOLDS)]
+    weights = prepare(w_in, b_in, w_mid, b_mid, w_out, z)
     offs = lax.dynamic_slice_in_dim(offsets, share * rows, rows, 0)
     offs = jnp.broadcast_to(offs[:, None], (rows, z))
-    index = jnp.reshape(share, (1,)).astype(jnp.int32)
+    pieces, weights, offs = lax.optimization_barrier((pieces, weights, offs))
     normals = fold(index, coil_maps, zero_filled, pieces, offs)
-    normals = [normals[0]] + [lax.ppermute(normals[k], "gy", pairs(-k)) for k in range(1, FOLDS)]
-    return denoise(index, step_sizes, zero_filled, normals, weights)
+    normals = [normals[0]] + [lax.ppermute(normals[k], "gy", pairs(k)) for k in range(1, FOLDS)]
+    return denoise(index, step_sizes, zero_filled, normals, weights, b_out)
 
 
 def solution(mesh):

time: 50 us -> 43.9 us (0.88)
  local copies, waits for them, and re-layouts: 10.3 us -> 3.56 us
  waiting for transfers between devices: 15 us -> 21.5 us
  Pallas kernels: 7.1 us -> 4.54 us
  starting transfers between devices: 15.2 us -> 13.3 us
  other arithmetic: 1.26 us -> 0 us
    ppermute x6, waiting for transfers between devices: 15 us -> 21.5 us  [the longest x3 18.1 us: per_device(): pieces = {k: lax.ppermute(pieces[k - 1], 'gy', pairs(k)) for k in (2, 3, 1)}]
    reshape x5 -> x1, local copies, waits for them, and re-layouts: 5.05 us -> 0.02 us  [prepare(): w_in.transpose(2, 3, 1, 0).reshape(18, ch)]
    unnamed x48 -> x22, local copies, waits for them, and re-layouts: 0.98 us -> 3.4 us
    ppermute x6, starting transfers between devices: 15.2 us -> 13.3 us  [the longest x3 7.65 us: per_device(): lax.ppermute(normals[k], 'gy', pairs(k))]
    pallas_call x1, Pallas kernels: 2.52 us -> 0.71 us  [fold(): pl.pallas_call(fold_kernel, grid_spec=spec, out_shape=[jax.ShapeDtypeStru...]
    broadcast_in_dim x2 -> x0, local copies, waits for them, and re-layouts: 1.35 us -> none  [the longest x1 0.68 us: prepare(): b1 = jnp.broadcast_to(b_in[:, None], (ch, z))]
    dynamic_slice x1 -> x0, local copies, waits for them, and re-layouts: 1.27 us -> none  [per_device(): lax.dynamic_slice_in_dim(coil_maps[0], first, rows, 2)]
    pallas_call x1, Pallas kernels: 4.57 us -> 3.31 us  [denoise(): pl.pallas_call(denoise_kernel, in_specs=[SMEM, SMEM, SMEM] + [VMEM] * 10,...]
  transfers between devices with their start and end apart: 6 -> 6, of which waited for: 2 -> 4; matrix products, arithmetic and copies ran while one was open for 15% -> 0% of each run, Pallas kernels for 0% -> 1%
where the time goes in v2:
time: 43.9 us; the launch traced here: 43.7 us
  waiting for transfers between devices  21.5 us (49%)
  starting transfers between devices  13.3 us (30%)
  Pallas kernels  4.54 us (10%)
  local copies, waits for them, and re-layouts  3.56 us (8%)
  between operations  0.72 us (2%)
    ppermute x3, waiting for transfers between devices, per_device(): pieces = {k: lax.ppermute(pieces[k - 1], 'gy', pairs(k)) for k in (2, 3, 1)}  18.1 us
    ppermute x3, starting transfers between devices, per_device(): lax.ppermute(normals[k], 'gy', pairs(k))  7.65 us
    ppermute x3, starting transfers between devices, per_device(): pieces = {k: lax.ppermute(pieces[k - 1], 'gy', pairs(k)) for k in (2, 3, 1)}  5.68 us
    ppermute x3, waiting for transfers between devices, per_device(): lax.ppermute(normals[k], 'gy', pairs(k))  3.48 us
    unnamed x22, local copies, waits for them, and re-layouts  3.4 us
    pallas_call x1, Pallas kernels, denoise(): pl.pallas_call(denoise_kernel, in_specs=[SMEM, SMEM, SMEM] + [VMEM] * 10,...  3.31 us
  transfers between devices with their start and end apart: 6, of which 4 were waited for; matrix products, arithmetic and copies ran while one was open for 0% of the time, Pallas kernels for 1%

profile of v2, /device:TPU:0, one launch (start us, length us, event | category | flops | bytes accessed | tf_op | source)
XLA Modules:
  0.0 43.7 jit_solution(18166859252284185294)
XLA Ops:
  0.0 0.0 copy-start
  0.0 1.2 %copy-done = bf16[1,2,32,64,128]{4,3,2,1,0:T(8,128)(2,1)S(1)} copy-done((bf16[1,2,32,64,128]{4,3,2,1,0:T(8,128)(2,1)S(1)}, bf16[1,2,32,64,128]{4,3,2,1,0:T(8,128)(2,1)}, u32[]{:S(2)}) %copy-start) | copy-done | bytes 1048600
  1.2 0.0 copy-start.2
  1.2 0.8 %copy-done.2 = f32[1,2,64,128]{3,2,1,0:T(8,128)S(1)} copy-done((f32[1,2,64,128]{3,2,1,0:T(8,128)S(1)}, f32[1,2,64,128]{3,2,1,0:T(8,128)}, u32[]{:S(2)}) %copy-start.2) | copy-done | bytes 65560
  2.1 0.0 copy-start.4
  2.1 0.2 pack.1
  2.3 3.1 %collective-permute-start = (bf16[2,34,16,128]{3,2,1,0:T(8,128)(2,1)S(1)}, bf16[2,34,16,128]{3,2,1,0:T(8,128)(2,1)S(1)}, u32[]{:S(2)}, u32[]{:S(2)}) collective-permute-start(bf16[2,34,16,128]{3,2,1,0:T(8,128)(2,1)S(1)} %get-tuple-element.26), channel_id=1, source_target_pairs={{0,4},{1,5},{2,6},{3,7},{4,0},{5,1},{6,2},{7,3},{8,12},{9,13},{10,... | collective-permute-start | bytes 835592 | tf_op jit(solution)/shard_map/ppermute | solution.py:330
  5.4 0.0 copy-start.9
  5.4 2.6 %collective-permute-start.1 = (bf16[2,34,16,128]{3,2,1,0:T(8,128)(2,1)S(1)}, bf16[2,34,16,128]{3,2,1,0:T(8,128)(2,1)S(1)}, u32[]{:S(2)}, u32[]{:S(2)}) collective-permute-start(bf16[2,34,16,128]{3,2,1,0:T(8,128)(2,1)S(1)} %get-tuple-element.27), channel_id=1, source_target_pairs={{0,8},{1,9},{2,10},{3,11},{4,12},{5,13},{6,14},{7,15},{8,0},{9,1},... | collective-permute-start | bytes 835592 | tf_op jit(solution)/shard_map/ppermute | solution.py:330
  7.9 0.0 collective-permute-start.2
  8.0 0.0 copy-done.9
  8.0 0.0 copy-start.10
  8.0 0.6 %copy-done.10 = s32[64]{0:T(128)S(1)} copy-done((s32[64]{0:T(128)S(1)}, s32[64]{0:T(128)}, u32[]{:S(2)}) %copy-start.10) | copy-done | bytes 280
  8.6 0.0 copy-start.5
  8.6 0.1 dynamic_slice.3
  8.7 0.0 copy-start.6
  8.7 0.0 copy-start.7
  8.7 0.0 copy-done.4
  8.7 0.6 %copy-done.5 = bf16[2,64,3,3]{1,0,3,2:T(2,128)(2,1)S(1)} copy-done((bf16[2,64,3,3]{1,0,3,2:T(2,128)(2,1)S(1)}, bf16[2,64,3,3]{1,0,3,2:T(2,128)(2,1)}, u32[]{:S(2)}) %copy-start.5) | copy-done | bytes 2328
  9.3 0.0 copy-done.6
  9.4 0.0 copy-done.7
  9.4 0.0 copy-start.1
  9.4 0.0 copy-start.3
  9.4 0.3 prepare.1
  9.7 7.5 %collective-permute-done.one_ref = bf16[2,34,16,128]{3,2,1,0:T(8,128)(2,1)S(1)} collective-permute-done((bf16[2,34,16,128]{3,2,1,0:T(8,128)(2,1)S(1)}, bf16[2,34,16,128]{3,2,1,0:T(8,128)(2,1)S(1)}, u32[]{:S(2)}, u32[]{:S(2)}) %collective-permute-start) | collective-permute-done | bytes 278560 | tf_op jit(solution)/shard_map/ppermute | solution.py:330
  17.2 10.6 %collective-permute-done.1.two_ref = bf16[2,34,16,128]{3,2,1,0:T(8,128)(2,1)S(1)} collective-permute-done((bf16[2,34,16,128]{3,2,1,0:T(8,128)(2,1)S(1)}, bf16[2,34,16,128]{3,2,1,0:T(8,128)(2,1)S(1)}, u32[]{:S(2)}, u32[]{:S(2)}) %collective-permute-start.1) | collective-permute-done | bytes 278560 | tf_op jit(solution)/shard_map/ppermute | solution.py:330
  27.8 0.0 collective-permute-done.2.three_ref
  27.8 0.1 broadcast_in_dim.14.offs_ref
  27.9 0.0 copy-done.1
  27.9 0.0 copy-done.3
  27.9 0.7 %fold.1 = (f32[2,16,128]{2,1,0:T(8,128)S(1)}, f32[2,16,128]{2,1,0:T(8,128)S(1)}, f32[2,16,128]{2,1,0:T(8,128)S(1)}, f32[2,16,128]{2,1,0:T(8,128)S(1)}) custom-call(s32[1]{0:T(128)} %bitcast.share_ref, bf16[1,2,32,64,128]{4,3,2,1,0:T(8,128)(2,1)S(1)} %copy-done.1, f32[1,2,64,128]{3,2,1,0:T(8,128)S(1)} %copy-done.3, ...), custom_call_target="tpu_custom_call" | custom-call | flops 4587520 | bytes 1048576 | tf_op jit(solution)/shard_map/fold/pallas_call | solution.py:92
  28.6 5.2 %collective-permute-start.3 = (f32[2,16,128]{2,1,0:T(8,128)S(1)}, f32[2,16,128]{2,1,0:T(8,128)S(1)}, u32[]{:S(2)}, u32[]{:S(2)}) collective-permute-start(f32[2,16,128]{2,1,0:T(8,128)S(1)} %get-tuple-element.39), channel_id=1, source_target_pairs={{0,4},{1,5},{2,6},{3,7},{4,0},{5,1},{6,2},{7,3},{8,12},{9,13},{10,... | collective-permute-start | bytes 49160 | tf_op jit(solution)/shard_map/ppermute | solution.py:337
  33.7 1.1 %collective-permute-start.4 = (f32[2,16,128]{2,1,0:T(8,128)S(1)}, f32[2,16,128]{2,1,0:T(8,128)S(1)}, u32[]{:S(2)}, u32[]{:S(2)}) collective-permute-start(f32[2,16,128]{2,1,0:T(8,128)S(1)} %get-tuple-element.40), channel_id=1, source_target_pairs={{0,8},{1,9},{2,10},{3,11},{4,12},{5,13},{6,14},{7,15},{8,0},{9,1},... | collective-permute-start | bytes 49160 | tf_op jit(solution)/shard_map/ppermute | solution.py:337
  34.8 1.4 %collective-permute-start.5 = (f32[2,16,128]{2,1,0:T(8,128)S(1)}, f32[2,16,128]{2,1,0:T(8,128)S(1)}, u32[]{:S(2)}, u32[]{:S(2)}) collective-permute-start(f32[2,16,128]{2,1,0:T(8,128)S(1)} %get-tuple-element.41), channel_id=1, source_target_pairs={{0,12},{1,13},{2,14},{3,15},{4,8},{5,9},{6,10},{7,11},{8,4},{9,5},... | collective-permute-start | bytes 49160 | tf_op jit(solution)/shard_map/ppermute | solution.py:337
  36.9 0.0 copy-start.8
  36.9 0.0 collective-permute-done.3.one_ref
  36.9 1.5 %collective-permute-done.4.two_ref = f32[2,16,128]{2,1,0:T(8,128)S(1)} collective-permute-done((f32[2,16,128]{2,1,0:T(8,128)S(1)}, f32[2,16,128]{2,1,0:T(8,128)S(1)}, u32[]{:S(2)}, u32[]{:S(2)}) %collective-permute-start.4) | collective-permute-done | bytes 16416 | tf_op jit(solution)/shard_map/ppermute | solution.py:337
  38.4 2.0 %collective-permute-done.5.three_ref = f32[2,16,128]{2,1,0:T(8,128)S(1)} collective-permute-done((f32[2,16,128]{2,1,0:T(8,128)S(1)}, f32[2,16,128]{2,1,0:T(8,128)S(1)}, u32[]{:S(2)}, u32[]{:S(2)}) %collective-permute-start.5) | collective-permute-done | bytes 16416 | tf_op jit(solution)/shard_map/ppermute | solution.py:337
  40.4 0.0 copy-done.8
  40.4 3.3 %denoise.1 = f32[1,2,64,128]{3,2,1,0:T(8,128)} custom-call(s32[1]{0:T(128)} %bitcast.share_ref, f32[1]{0:T(128)S(6)} %copy.11.step_ref, f32[2]{0:T(128)S(1)} %copy-done.8, f32[1,2,64,128]{3,2,1,0:T(8,128)S(1)} %copy-done.3, f32[2,16,128]{2,1,0:T(8,128)S(1)} %get-tuple-element.38.own_ref, f32[2,16,128]{2,1,0:T(8,128)S(1)} %collective-permute-done.3.one_ref, ...), custom_call_target="tpu_custom_call" | custom-call | flops 4000000000 | bytes 2000000 | tf_op jit(solution)/shard_map/denoise/pallas_call | solution.py:202
  (1 shorter events, 0.0 us)
Async XLA Ops:
  0.0 1.2 %copy-start = (bf16[1,2,32,64,128]{4,3,2,1,0:T(8,128)(2,1)S(1)}, bf16[1,2,32,64,128]{4,3,2,1,0:T(8,128)(2,1)}, u32[]{:S(2)}) copy-start(bf16[1,2,32,64,128]{4,3,2,1,0:T(8,128)(2,1)} %maps_ref.3) | copy-start | bytes 3145732
  1.2 0.8 %copy-start.2 = (f32[1,2,64,128]{3,2,1,0:T(8,128)S(1)}, f32[1,2,64,128]{3,2,1,0:T(8,128)}, u32[]{:S(2)}) copy-start(f32[1,2,64,128]{3,2,1,0:T(8,128)} %field_ref.5) | copy-start | bytes 196612
  2.1 6.6 %copy-start.4 = (bf16[64,64,3,3]{1,0,3,2:T(8,128)(2,1)S(1)}, bf16[64,64,3,3]{1,0,3,2:T(8,128)(2,1)}, u32[]{:S(2)}) copy-start(bf16[64,64,3,3]{1,0,3,2:T(8,128)(2,1)} %param.16) | copy-start | bytes 221188
  2.3 14.9 %collective-permute-start = (bf16[2,34,16,128]{3,2,1,0:T(8,128)(2,1)S(1)}, bf16[2,34,16,128]{3,2,1,0:T(8,128)(2,1)S(1)}, u32[]{:S(2)}, u32[]{:S(2)}) collective-permute-start(bf16[2,34,16,128]{3,2,1,0:T(8,128)(2,1)S(1)} %get-tuple-element.26), channel_id=1, source_target_pairs={{0,4},{1,5},{2,6},{3,7},{4,0},{5,1},{6,2},{7,3},{8,12},{9,13},{10,... | collective-permute-start | bytes 835592 | tf_op jit(solution)/shard_map/ppermute | solution.py:330
  5.4 2.6 %copy-start.9 = (bf16[64,2,3,3]{0,1,3,2:T(2,128)(2,1)S(1)}, bf16[64,2,3,3]{0,1,3,2:T(2,128)(2,1)}, u32[]{:S(2)}) copy-start(bf16[64,2,3,3]{0,1,3,2:T(2,128)(2,1)} %param.14) | copy-start | bytes 6916
  5.4 22.4 %collective-permute-start.1 = (bf16[2,34,16,128]{3,2,1,0:T(8,128)(2,1)S(1)}, bf16[2,34,16,128]{3,2,1,0:T(8,128)(2,1)S(1)}, u32[]{:S(2)}, u32[]{:S(2)}) collective-permute-start(bf16[2,34,16,128]{3,2,1,0:T(8,128)(2,1)S(1)} %get-tuple-element.27), channel_id=1, source_target_pairs={{0,8},{1,9},{2,10},{3,11},{4,12},{5,13},{6,14},{7,15},{8,0},{9,1},... | collective-permute-start | bytes 835592 | tf_op jit(solution)/shard_map/ppermute | solution.py:330
  7.9 19.8 %collective-permute-start.2 = (bf16[2,34,16,128]{3,2,1,0:T(8,128)(2,1)S(1)}, bf16[2,34,16,128]{3,2,1,0:T(8,128)(2,1)S(1)}, u32[]{:S(2)}, u32[]{:S(2)}) collective-permute-start(bf16[2,34,16,128]{3,2,1,0:T(8,128)(2,1)S(1)} %get-tuple-element.28), channel_id=1, source_target_pairs={{0,12},{1,13},{2,14},{3,15},{4,8},{5,9},{6,10},{7,11},{8,4},{9,5},... | collective-permute-start | bytes 835592 | tf_op jit(solution)/shard_map/ppermute | solution.py:330
  8.0 0.7 %copy-start.10 = (s32[64]{0:T(128)S(1)}, s32[64]{0:T(128)}, u32[]{:S(2)}) copy-start(s32[64]{0:T(128)} %param.12) | copy-start | bytes 772
  8.6 0.7 %copy-start.5 = (bf16[2,64,3,3]{1,0,3,2:T(2,128)(2,1)S(1)}, bf16[2,64,3,3]{1,0,3,2:T(2,128)(2,1)}, u32[]{:S(2)}) copy-start(bf16[2,64,3,3]{1,0,3,2:T(2,128)(2,1)} %param.18) | copy-start | bytes 6916
  8.7 0.7 %copy-start.6 = (f32[64]{0:T(128)S(1)}, f32[64]{0:T(128)}, u32[]{:S(2)}) copy-start(f32[64]{0:T(128)} %param.15) | copy-start | bytes 772
  8.7 0.7 %copy-start.7 = (f32[64]{0:T(128)S(1)}, f32[64]{0:T(128)}, u32[]{:S(2)}) copy-start(f32[64]{0:T(128)} %param.17) | copy-start | bytes 772
  9.4 18.5 %copy-start.1 = (bf16[1,2,32,64,128]{4,3,2,1,0:T(8,128)(2,1)S(1)}, bf16[1,2,32,64,128]{4,3,2,1,0:T(8,128)(2,1)}, u32[]{:S(2)}) copy-start(bf16[1,2,32,64,128]{4,3,2,1,0:T(8,128)(2,1)} %maps_ref.3) | copy-start | bytes 3145732
  9.4 18.5 %copy-start.3 = (f32[1,2,64,128]{3,2,1,0:T(8,128)S(1)}, f32[1,2,64,128]{3,2,1,0:T(8,128)}, u32[]{:S(2)}) copy-start(f32[1,2,64,128]{3,2,1,0:T(8,128)} %field_ref.5) | copy-start | bytes 196612
  28.6 8.3 %collective-permute-start.3 = (f32[2,16,128]{2,1,0:T(8,128)S(1)}, f32[2,16,128]{2,1,0:T(8,128)S(1)}, u32[]{:S(2)}, u32[]{:S(2)}) collective-permute-start(f32[2,16,128]{2,1,0:T(8,128)S(1)} %get-tuple-element.39), channel_id=1, source_target_pairs={{0,4},{1,5},{2,6},{3,7},{4,0},{5,1},{6,2},{7,3},{8,12},{9,13},{10,... | collective-permute-start | bytes 49160 | tf_op jit(solution)/shard_map/ppermute | solution.py:337
  33.7 4.6 %collective-permute-start.4 = (f32[2,16,128]{2,1,0:T(8,128)S(1)}, f32[2,16,128]{2,1,0:T(8,128)S(1)}, u32[]{:S(2)}, u32[]{:S(2)}) collective-permute-start(f32[2,16,128]{2,1,0:T(8,128)S(1)} %get-tuple-element.40), channel_id=1, source_target_pairs={{0,8},{1,9},{2,10},{3,11},{4,12},{5,13},{6,14},{7,15},{8,0},{9,1},... | collective-permute-start | bytes 49160 | tf_op jit(solution)/shard_map/ppermute | solution.py:337
  34.8 5.5 %collective-permute-start.5 = (f32[2,16,128]{2,1,0:T(8,128)S(1)}, f32[2,16,128]{2,1,0:T(8,128)S(1)}, u32[]{:S(2)}, u32[]{:S(2)}) collective-permute-start(f32[2,16,128]{2,1,0:T(8,128)S(1)} %get-tuple-element.41), channel_id=1, source_target_pairs={{0,12},{1,13},{2,14},{3,15},{4,8},{5,9},{6,10},{7,11},{8,4},{9,5},... | collective-permute-start | bytes 49160 | tf_op jit(solution)/shard_map/ppermute | solution.py:337
  36.9 3.5 %copy-start.8 = (f32[2]{0:T(128)S(1)}, f32[2]{0:T(128)}, u32[]{:S(2)}) copy-start(f32[2]{0:T(128)} %tail_ref.1) | copy-start | bytes 28

commit v3 on v2

--- a/solution.py
+++ b/solution.py
@@ -1,3 +1,5 @@
+import functools
+
 import jax
 import jax.numpy as jnp
 from jax import lax
@@ -10,14 +12,25 @@
 QUAD = 4
 PAIR = 2
 PAD = 8
+ORDERS = ((2, 3, 1), (1, 2, 3))
+PACK_LIMIT = 8 << 20
 
 VMEM = pl.BlockSpec(memory_space=pltpu.VMEM)
+HBM = pl.BlockSpec(memory_space=pltpu.HBM)
 SMEM = pl.BlockSpec(memory_space=pltpu.SMEM)
 
 
-def fold_kernel(share_ref, maps_ref, field_ref, one_ref, two_ref, three_ref, offs_ref, out0, out1, out2, out3):
+def place(stride):
+    position = lax.axis_index("gy")
+    odd = position % 2
+    return position // stride, [jnp.where(odd == 0, even, other) for even, other in zip(*ORDERS)]
+
+
+def fold_kernel(stride, maps_ref, field_ref, one_ref, two_ref, three_ref, offs_ref, out0, out1, out2, out3):
     coils = maps_ref.shape[2]
-    share = share_ref[0]
+    rows = out0.shape[1]
+    share, distances = place(stride)
+    own = pl.ds(pl.multiple_of(share * rows, rows), rows)
     offs = offs_ref[...]
     pieces = (None, one_ref, two_ref, three_ref)
     outs = (out0, out1, out2, out3)
@@ -25,14 +38,14 @@
     units = []
     for k in range(FOLDS):
         if k == 0:
-            real, imag = field_ref[0, 0], field_ref[0, 1]
+            real, imag = field_ref[0, 0, own, :], field_ref[0, 1, own, :]
             turned.append((real, imag))
             units.append(None)
             continue
         piece = pieces[k]
         real = piece[0, coils].astype(jnp.float32) + piece[0, coils + 1].astype(jnp.float32)
         imag = piece[1, coils].astype(jnp.float32) + piece[1, coils + 1].astype(jnp.float32)
-        turns = (((share ^ k) - share) * offs) & 3
+        turns = (((share ^ distances[k - 1]) - share) * offs) & 3
         zero, one = jnp.zeros_like(real), jnp.ones_like(real)
         cosine = jnp.where(turns == 0, one, jnp.where(turns == 2, -one, zero))
         sine = jnp.where(turns == 3, one, jnp.where(turns == 1, -one, zero))
@@ -44,7 +57,7 @@
         fold_real = fold_imag = None
         for k in range(FOLDS):
             if k == 0:
-                real, imag = maps_ref[0, 0, c], maps_ref[0, 1, c]
+                real, imag = maps_ref[0, 0, c, own, :], maps_ref[0, 1, c, own, :]
             else:
                 real, imag = pieces[k][0, c], pieces[k][1, c]
             real, imag = real.astype(jnp.float32), imag.astype(jnp.float32)
@@ -61,7 +74,7 @@
         return tuple(new)
 
     zeros = tuple(jnp.zeros(offs.shape, jnp.float32) for _ in range(2 * FOLDS))
-    sums = lax.fori_loop(0, coils, step, zeros, unroll=4)
+    sums = lax.fori_loop(0, coils, step, zeros, unroll=8)
     for k in range(FOLDS):
         real, imag = 0.25 * sums[2 * k], 0.25 * sums[2 * k + 1]
         if k == 0:
@@ -72,31 +85,18 @@
             outs[k][1] = cosine * imag - sine * real
 
 
-def fold(share, coil_maps, field, pieces, offs):
-    _, _, coils, _, z = coil_maps.shape
-    rows = offs.shape[0]
-    whole = lambda *shape: pl.BlockSpec(shape, lambda i, s: (0,) * len(shape))
-    spec = pltpu.PrefetchScalarGridSpec(
-        num_scalar_prefetch=1,
-        grid=(1,),
-        in_specs=[
-            pl.BlockSpec((1, 2, coils, rows, z), lambda i, s: (0, 0, 0, s[0], 0)),
-            pl.BlockSpec((1, 2, rows, z), lambda i, s: (0, 0, s[0], 0)),
-            whole(*pieces[0].shape),
-            whole(*pieces[1].shape),
-            whole(*pieces[2].shape),
-            whole(rows, z),
-        ],
-        out_specs=[whole(2, rows, z)] * FOLDS,
-    )
+def fold(stride, coil_maps, field, pieces, offs):
+    coils = coil_maps.shape[2]
+    rows, z = offs.shape
     return pl.pallas_call(
-        fold_kernel,
-        grid_spec=spec,
+        functools.partial(fold_kernel, stride),
+        in_specs=[VMEM] * 6,
+        out_specs=[VMEM] * FOLDS,
         out_shape=[jax.ShapeDtypeStruct((2, rows, z), jnp.float32)] * FOLDS,
         cost_estimate=pl.CostEstimate(flops=70 * coils * rows * z, bytes_accessed=16 * coils * rows * z, transcendentals=0),
         compiler_params=pltpu.CompilerParams(vmem_limit_bytes=8 << 20),
         name="fold",
-    )(share, coil_maps, field, *pieces, offs)
+    )(coil_maps, field, *pieces, offs)
 
 
 def shifted(value, lane, tap, width):
@@ -108,17 +108,16 @@
 
 
 def denoise_kernel(
-    share_ref, step_ref, tail_ref, field_ref, own_ref, one_ref, two_ref, three_ref,
+    stride, step_ref, tail_ref, field_ref, own_ref, one_ref, two_ref, three_ref,
     w1_ref, b1_ref, w2_ref, b2_ref, w3_ref, out_ref, padded, window, low, hidden_one, hidden_two,
 ):
     _, _, x_size, z = field_ref.shape
     rows = own_ref.shape[1]
     ch = b1_ref.shape[0]
-    share = share_ref[0]
-    step = step_ref[0]
+    share, distances = place(stride)
     groups = x_size // GROUP
     for k, ref in enumerate((own_ref, one_ref, two_ref, three_ref)):
-        start = pl.multiple_of((share ^ k) * rows, rows)
+        start = pl.multiple_of((share if k == 0 else share ^ distances[k - 1]) * rows, rows)
         for part in range(2):
             padded[part, pl.ds(PAD + start, rows), :] = ref[part]
     edge = jnp.zeros((PAD, z), jnp.float32)
@@ -126,7 +125,7 @@
         padded[part, 0:PAD, :] = edge
         padded[part, PAD + x_size : PAD + x_size + PAD, :] = edge
         base = field_ref[0, part]
-        stepped = base - step * (padded[part, PAD : PAD + x_size, :] - base)
+        stepped = base - step_ref[...] * (padded[part, PAD : PAD + x_size, :] - base)
         padded[part, PAD : PAD + x_size, :] = stepped
     lane = lax.broadcasted_iota(jnp.int32, (x_size + 2 * PAD, z), 1)
     for tap in range(3):
@@ -190,18 +189,18 @@
                 out_ref[0, part, first : first + GROUP, :] = (
                     padded[part, PAD + first : PAD + first + GROUP, :]
                     + total[part * GROUP : (part + 1) * GROUP]
-                    + tail_ref[part]
+                    + tail_ref[part * GROUP : (part + 1) * GROUP, :]
                 )
 
 
-def denoise(share, step, field, normals, weights, b_out):
+def denoise(stride, field, normals, weights):
     _, _, x_size, z = field.shape
-    w1, b1, w2, b2, w3 = weights
+    w1, b1, w2, b2, w3, tail, step = weights
     ch = b1.shape[0]
     span = GROUP + 2 * PAD
     return pl.pallas_call(
-        denoise_kernel,
-        in_specs=[SMEM, SMEM, SMEM] + [VMEM] * 10,
+        functools.partial(denoise_kernel, stride),
+        in_specs=[VMEM] * 12,
         out_specs=VMEM,
         out_shape=jax.ShapeDtypeStruct(field.shape, jnp.float32),
         scratch_shapes=[
@@ -214,12 +213,18 @@
         cost_estimate=pl.CostEstimate(flops=4_000_000_000, bytes_accessed=2_000_000, transcendentals=0),
         compiler_params=pltpu.CompilerParams(vmem_limit_bytes=16 << 20),
         name="denoise",
-    )(share, step, b_out, field, *normals, w1, b1, w2, b2, w3)
-
-
-def prepare_kernel(w_in_ref, b_in_ref, w_mid_ref, b_mid_ref, w_out_ref, w1_ref, b1_ref, w2_ref, b2_ref, w3_ref):
+    )(step, tail, field, *normals, w1, b1, w2, b2, w3)
+
+
+def prepare_kernel(
+    w_in_ref, b_in_ref, w_mid_ref, b_mid_ref, w_out_ref, b_out_ref, step_in_ref,
+    w1_ref, b1_ref, w2_ref, b2_ref, w3_ref, tail_ref, step_ref,
+):
     ch, z = b1_ref.shape
     span = GROUP + 2 * PAD
+    step_ref[...] = jnp.full(step_ref.shape, step_in_ref[0])
+    for part in range(2):
+        tail_ref[part * GROUP : (part + 1) * GROUP, :] = jnp.full((GROUP, z), b_out_ref[part])
     b1_ref[...] = jnp.transpose(jnp.broadcast_to(b_in_ref[...], (z, ch)))
     b2_ref[...] = jnp.transpose(jnp.broadcast_to(b_mid_ref[...], (z, ch)))
     taps = w_in_ref[...]
@@ -251,7 +256,7 @@
             w3_ref[first : first + GROUP, :] = total.astype(jnp.bfloat16)
 
 
-def prepare(w_in, b_in, w_mid, b_mid, w_out, z):
+def prepare(w_in, b_in, w_mid, b_mid, w_out, b_out, step, x_size, z):
     ch = w_mid.shape[0]
     shapes = [
         jax.ShapeDtypeStruct((GROUP * ch, 6 * (GROUP + 2 * PAD)), jnp.bfloat16),
@@ -259,11 +264,13 @@
         jax.ShapeDtypeStruct((3 * PAIR * ch, (PAIR + 2) * ch), jnp.bfloat16),
         jax.ShapeDtypeStruct((ch, z), jnp.float32),
         jax.ShapeDtypeStruct((6 * GROUP, (GROUP + 2) * ch), jnp.bfloat16),
+        jax.ShapeDtypeStruct((2 * GROUP, z), jnp.float32),
+        jax.ShapeDtypeStruct((x_size, z), jnp.float32),
     ]
     return pl.pallas_call(
         prepare_kernel,
-        in_specs=[VMEM] * 5,
-        out_specs=[VMEM] * 5,
+        in_specs=[VMEM] * 5 + [SMEM] * 2,
+        out_specs=[VMEM] * 7,
         out_shape=shapes,
         cost_estimate=pl.CostEstimate(flops=1_000_000_000, bytes_accessed=8_000_000, transcendentals=0),
         compiler_params=pltpu.CompilerParams(vmem_limit_bytes=8 << 20),
@@ -274,25 +281,32 @@
         w_mid.transpose(2, 3, 0, 1),
         b_mid[None],
         w_out.transpose(2, 3, 0, 1),
+        b_out,
+        step,
     )
 
 
-def pack_kernel(share_ref, maps_ref, field_ref, one_ref, two_ref, three_ref, sems):
+def pack_kernel(stride, maps_ref, field_ref, one_ref, two_ref, three_ref, held, sems, field_sem):
     coils = maps_ref.shape[2]
     rows = one_ref.shape[2]
+    share, distances = place(stride)
+    field_copy = pltpu.make_async_copy(field_ref.at[0], held, field_sem)
+    field_copy.start()
     copies = []
-    for k, ref in ((2, two_ref), (1, one_ref), (3, three_ref)):
-        first = pl.multiple_of((share_ref[0] ^ k) * rows, rows)
+    outs = (one_ref, two_ref, three_ref)
+    for i, ref in enumerate(outs):
+        first = pl.multiple_of((share ^ distances[i]) * rows, rows)
         for part in range(2):
             copy = pltpu.make_async_copy(
-                maps_ref.at[0, part, :, pl.ds(first, rows), :], ref.at[part, 0:coils], sems.at[k - 1, part]
+                maps_ref.at[0, part, :, pl.ds(first, rows), :], ref.at[part, 0:coils], sems.at[i, part]
             )
             copy.start()
             copies.append(copy)
-    for k, ref in ((2, two_ref), (1, one_ref), (3, three_ref)):
-        first = pl.multiple_of((share_ref[0] ^ k) * rows, rows)
-        for part in range(2):
-            value = field_ref[0, part, pl.ds(first, rows), :]
+    field_copy.wait()
+    for i, ref in enumerate(outs):
+        first = pl.multiple_of((share ^ distances[i]) * rows, rows)
+        for part in range(2):
+            value = held[part, pl.ds(first, rows), :]
             high = value.astype(jnp.bfloat16)
             ref[part, coils] = high
             ref[part, coils + 1] = (value - high.astype(jnp.float32)).astype(jnp.bfloat16)
@@ -300,19 +314,23 @@
         copy.wait()
 
 
-def pack(share, coil_maps, field):
+def pack(stride, coil_maps, field):
     _, _, coils, x_size, z = coil_maps.shape
     piece = jax.ShapeDtypeStruct((2, coils + 2, x_size // FOLDS, z), jnp.bfloat16)
     return pl.pallas_call(
-        pack_kernel,
-        in_specs=[SMEM, pl.BlockSpec(memory_space=pltpu.HBM), VMEM],
+        functools.partial(pack_kernel, stride),
+        in_specs=[HBM, HBM],
         out_specs=[VMEM] * 3,
         out_shape=[piece] * 3,
-        scratch_shapes=[pltpu.SemaphoreType.DMA((3, 2))],
+        scratch_shapes=[
+            pltpu.VMEM((2, x_size, z), jnp.float32),
+            pltpu.SemaphoreType.DMA((3, 2)),
+            pltpu.SemaphoreType.DMA,
+        ],
         cost_estimate=pl.CostEstimate(flops=0, bytes_accessed=2_000_000, transcendentals=0),
-        compiler_params=pltpu.CompilerParams(vmem_limit_bytes=4 << 20),
+        compiler_params=pltpu.CompilerParams(vmem_limit_bytes=PACK_LIMIT),
         name="pack",
-    )(share, coil_maps, field)
+    )(*(pltpu.with_memory_space_constraint(array, pltpu.HBM) for array in (coil_maps, field)))
 
 
 def per_device(zero_filled, coil_maps, offsets, step_sizes, w_in, b_in, w_mid, b_mid, w_out, b_out):
@@ -322,20 +340,21 @@
     rows = x_size // FOLDS
     share = lax.axis_index("gy") // stride
 
-    def pairs(k):
-        return [(j, (j // stride ^ k) * stride + j % stride) for j in range(devices)]
-
-    index = jnp.reshape(share, (1,)).astype(jnp.int32)
-    pieces = pack(index, coil_maps, zero_filled)
-    pieces = {k: lax.ppermute(pieces[k - 1], "gy", pairs(k)) for k in (2, 3, 1)}
-    pieces = [pieces[k] for k in range(1, FOLDS)]
-    weights = prepare(w_in, b_in, w_mid, b_mid, w_out, z)
+    def trade(values):
+        out = []
+        for value, distances in zip(values, zip(*ORDERS)):
+            pairs = [(j, (j // stride ^ distances[j % 2]) * stride + j % stride) for j in range(devices)]
+            out.append(lax.ppermute(value, "gy", pairs))
+        return out
+
+    pieces = trade(pack(stride, coil_maps, zero_filled))
+    weights = prepare(w_in, b_in, w_mid, b_mid, w_out, b_out, step_sizes, x_size, z)
     offs = lax.dynamic_slice_in_dim(offsets, share * rows, rows, 0)
     offs = jnp.broadcast_to(offs[:, None], (rows, z))
     pieces, weights, offs = lax.optimization_barrier((pieces, weights, offs))
-    normals = fold(index, coil_maps, zero_filled, pieces, offs)
-    normals = [normals[0]] + [lax.ppermute(normals[k], "gy", pairs(k)) for k in range(1, FOLDS)]
-    return denoise(index, step_sizes, zero_filled, normals, weights, b_out)
+    normals = fold(stride, coil_maps, zero_filled, pieces, offs)
+    normals = [normals[0]] + trade(normals[1:])
+    return denoise(stride, zero_filled, normals, weights)
 
 
 def solution(mesh):

time: 43.9 us -> 42.2 us (0.961)
  waiting for transfers between devices: 21.5 us -> 19.4 us
  local copies, waits for them, and re-layouts: 3.56 us -> 1.52 us
  starting transfers between devices: 13.3 us -> 14.8 us
  Pallas kernels: 4.54 us -> 5.58 us
    ppermute x6, waiting for transfers between devices: 21.5 us -> 19.4 us  [trade(): out.append(lax.ppermute(value, 'gy', pairs))]
    unnamed x22 -> x18, local copies, waits for them, and re-layouts: 3.4 us -> 1.36 us
    ppermute x6, starting transfers between devices: 13.3 us -> 14.8 us  [trade(): out.append(lax.ppermute(value, 'gy', pairs))]
    pallas_call x4, Pallas kernels: 4.54 us -> 5.58 us  [the longest x1 2.72 us: denoise(): pl.pallas_call(functools.partial(denoise_kernel, stride), in_specs=[VMEM]...]
  transfers between devices with their start and end apart: 6 -> 6, of which waited for: 4 -> 3; matrix products, arithmetic and copies ran while one was open for 0% -> 0% of each run, Pallas kernels for 1% -> 2%
where the time goes in v3:
time: 42.2 us; the launch traced here: 42 us
  waiting for transfers between devices  19.4 us (46%)
  starting transfers between devices  14.8 us (35%)
  Pallas kernels  5.58 us (13%)
  local copies, waits for them, and re-layouts  1.52 us (4%)
  between operations  0.72 us (2%)
    ppermute x6, waiting for transfers between devices, trade(): out.append(lax.ppermute(value, 'gy', pairs))  19.4 us
    ppermute x6, starting transfers between devices, trade(): out.append(lax.ppermute(value, 'gy', pairs))  14.8 us
    pallas_call x1, Pallas kernels, denoise(): pl.pallas_call(functools.partial(denoise_kernel, stride), in_specs=[VMEM]...  2.72 us
    unnamed x18, local copies, waits for them, and re-layouts  1.36 us
    pallas_call x1, Pallas kernels, pack(): pl.pallas_call(functools.partial(pack_kernel, stride), in_specs=[HBM, HBM...  1.32 us
    pallas_call x1, Pallas kernels, prepare(): pl.pallas_call(prepare_kernel, in_specs=[VMEM] * 5 + [SMEM] * 2, out_spec...  0.87 us
  transfers between devices with their start and end apart: 6, of which 3 were waited for; matrix products, arithmetic and copies ran while one was open for 0% of the time, Pallas kernels for 2%

profile of v3, /device:TPU:0, one launch (start us, length us, event | category | flops | bytes accessed | tf_op | source)
XLA Modules:
  0.0 42.0 jit_solution(10328038015716337432)
XLA Ops:
  0.0 0.0 copy-start.2
  0.0 1.3 %pack.1 = (bf16[2,34,16,128]{3,2,1,0:T(8,128)(2,1)S(1)}, bf16[2,34,16,128]{3,2,1,0:T(8,128)(2,1)S(1)}, bf16[2,34,16,128]{3,2,1,0:T(8,128)(2,1)S(1)}) custom-call(bf16[1,2,32,64,128]{4,3,2,1,0:T(8,128)(2,1)} %maps_ref.3, f32[1,2,64,128]{3,2,1,0:T(8,128)} %field_ref.5), custom_call_target="tpu_custom_call" | custom-call | bytes 2000000 | tf_op jit(solution)/shard_map/pack/pallas_call | solution.py:320
  1.3 4.1 %collective-permute-start = (bf16[2,34,16,128]{3,2,1,0:T(8,128)(2,1)S(1)}, bf16[2,34,16,128]{3,2,1,0:T(8,128)(2,1)S(1)}, u32[]{:S(2)}, u32[]{:S(2)}) collective-permute-start(bf16[2,34,16,128]{3,2,1,0:T(8,128)(2,1)S(1)} %get-tuple-element.30), channel_id=1, source_target_pairs={{0,8},{1,5},{2,10},{3,7},{4,12},{5,1},{6,14},{7,3},{8,0},{9,13},{1... | collective-permute-start | bytes 835592 | tf_op jit(solution)/shard_map/ppermute | solution.py:347
  5.4 1.3 %collective-permute-start.1 = (bf16[2,34,16,128]{3,2,1,0:T(8,128)(2,1)S(1)}, bf16[2,34,16,128]{3,2,1,0:T(8,128)(2,1)S(1)}, u32[]{:S(2)}, u32[]{:S(2)}) collective-permute-start(bf16[2,34,16,128]{3,2,1,0:T(8,128)(2,1)S(1)} %get-tuple-element.31), channel_id=1, source_target_pairs={{0,12},{1,9},{2,14},{3,11},{4,8},{5,13},{6,10},{7,15},{8,4},{9,1},... | collective-permute-start | bytes 835592 | tf_op jit(solution)/shard_map/ppermute | solution.py:347
  6.8 0.2 collective-permute-start.2
  7.0 0.0 copy-start.7
  7.7 0.0 copy-done.7
  7.7 0.0 copy-start.8
  7.7 0.6 %copy-done.8 = s32[64]{0:T(128)S(1)} copy-done((s32[64]{0:T(128)S(1)}, s32[64]{0:T(128)}, u32[]{:S(2)}) %copy-start.8) | copy-done | bytes 280
  8.4 0.0 copy-start.3
  8.4 0.1 dynamic_slice.3
  8.5 0.0 copy-start.4
  8.5 0.0 copy-start.5
  8.5 0.0 copy-start.6
  8.5 0.0 copy-done.2
  8.5 0.6 %copy-done.3 = bf16[2,64,3,3]{1,0,3,2:T(2,128)(2,1)S(1)} copy-done((bf16[2,64,3,3]{1,0,3,2:T(2,128)(2,1)S(1)}, bf16[2,64,3,3]{1,0,3,2:T(2,128)(2,1)}, u32[]{:S(2)}) %copy-start.3) | copy-done | bytes 2328
  9.1 0.0 copy-done.4
  9.1 0.0 copy-done.5
  9.1 0.0 copy-done.6
  9.1 0.0 copy-start
  9.1 0.0 copy-start.1
  9.1 0.9 %prepare.1 = (bf16[1024,192]{1,0:T(8,128)(2,1)S(1)}, f32[64,128]{1,0:T(8,128)S(1)}, bf16[384,256]{1,0:T(8,128)(2,1)S(1)}, f32[64,128]{1,0:T(8,128)S(1)}, bf16[96...) custom-call(bf16[18,64]{1,0:T(8,128)(2,1)S(1)} %reshape.4.w_in_ref, f32[1,64]{1,0:T(1,128)S(1)} %bitcast.7, ...), custom_call_target="tpu_custom_call" | custom-call | flops 1000000000 | bytes 8000000 | tf_op jit(solution)/shard_map/prepare/pallas_call | solution.py:270
  10.0 14.5 %collective-permute-done.one_ref = bf16[2,34,16,128]{3,2,1,0:T(8,128)(2,1)S(1)} collective-permute-done((bf16[2,34,16,128]{3,2,1,0:T(8,128)(2,1)S(1)}, bf16[2,34,16,128]{3,2,1,0:T(8,128)(2,1)S(1)}, u32[]{:S(2)}, u32[]{:S(2)}) %collective-permute-start) | collective-permute-done | bytes 278560 | tf_op jit(solution)/shard_map/ppermute | solution.py:347
  24.5 0.0 collective-permute-done.1.two_ref
  24.5 0.0 collective-permute-done.2.three_ref
  24.5 0.1 broadcast_in_dim.14.offs_ref
  24.6 0.0 copy-done
  24.6 0.0 copy-done.1
  24.6 0.7 %fold.1 = (f32[2,16,128]{2,1,0:T(8,128)S(1)}, f32[2,16,128]{2,1,0:T(8,128)S(1)}, f32[2,16,128]{2,1,0:T(8,128)S(1)}, f32[2,16,128]{2,1,0:T(8,128)S(1)}) custom-call(bf16[1,2,32,64,128]{4,3,2,1,0:T(8,128)(2,1)S(1)} %copy-done, f32[1,2,64,128]{3,2,1,0:T(8,128)S(1)} %copy-done.1, bf16[2,34,16,128]{3,2,1,0:T(8,128)(2,1)S(1)} %collective-permute-done.one_ref, ...), custom_call_target="tpu_custom_call" | custom-call | flops 4587520 | bytes 1048576 | tf_op jit(solution)/shard_map/fold/pallas_call | solution.py:91
  25.3 8.5 %collective-permute-start.3 = (f32[2,16,128]{2,1,0:T(8,128)S(1)}, f32[2,16,128]{2,1,0:T(8,128)S(1)}, u32[]{:S(2)}, u32[]{:S(2)}) collective-permute-start(f32[2,16,128]{2,1,0:T(8,128)S(1)} %get-tuple-element.47), channel_id=1, source_target_pairs={{0,8},{1,5},{2,10},{3,7},{4,12},{5,1},{6,14},{7,3},{8,0},{9,13},{1... | collective-permute-start | bytes 49160 | tf_op jit(solution)/shard_map/ppermute | solution.py:347
  33.7 0.5 %collective-permute-start.4 = (f32[2,16,128]{2,1,0:T(8,128)S(1)}, f32[2,16,128]{2,1,0:T(8,128)S(1)}, u32[]{:S(2)}, u32[]{:S(2)}) collective-permute-start(f32[2,16,128]{2,1,0:T(8,128)S(1)} %get-tuple-element.48), channel_id=1, source_target_pairs={{0,12},{1,9},{2,14},{3,11},{4,8},{5,13},{6,10},{7,15},{8,4},{9,1},... | collective-permute-start | bytes 49160 | tf_op jit(solution)/shard_map/ppermute | solution.py:347
  34.2 0.2 collective-permute-start.5
  34.4 1.2 %collective-permute-done.3.one_ref = f32[2,16,128]{2,1,0:T(8,128)S(1)} collective-permute-done((f32[2,16,128]{2,1,0:T(8,128)S(1)}, f32[2,16,128]{2,1,0:T(8,128)S(1)}, u32[]{:S(2)}, u32[]{:S(2)}) %collective-permute-start.3) | collective-permute-done | bytes 16416 | tf_op jit(solution)/shard_map/ppermute | solution.py:347
  35.6 3.7 %collective-permute-done.4.two_ref = f32[2,16,128]{2,1,0:T(8,128)S(1)} collective-permute-done((f32[2,16,128]{2,1,0:T(8,128)S(1)}, f32[2,16,128]{2,1,0:T(8,128)S(1)}, u32[]{:S(2)}, u32[]{:S(2)}) %collective-permute-start.4) | collective-permute-done | bytes 16416 | tf_op jit(solution)/shard_map/ppermute | solution.py:347
  39.3 0.0 collective-permute-done.5.three_ref
  39.3 2.7 %denoise.1 = f32[1,2,64,128]{3,2,1,0:T(8,128)} custom-call(f32[64,128]{1,0:T(8,128)S(1)} %get-tuple-element.40.step_ref, f32[32,128]{1,0:T(8,128)S(1)} %get-tuple-element.41.tail_ref, f32[1,2,64,128]{3,2,1,0:T(8,128)S(1)} %copy-done.1, f32[2,16,128]{2,1,0:T(8,128)S(1)} %get-tuple-element.46.own_ref, f32[2,16,128]{2,1,0:T(8,128)S(1)} %collective-permute-done.3.one_ref, ...), custom_call_target="tpu_custom_call" | custom-call | flops 4000000000 | bytes 2000000 | tf_op jit(solution)/shard_map/denoise/pallas_call | solution.py:201
  (1 shorter events, 0.0 us)
Async XLA Ops:
  0.0 8.5 %copy-start.2 = (bf16[64,64,3,3]{1,0,3,2:T(8,128)(2,1)S(1)}, bf16[64,64,3,3]{1,0,3,2:T(8,128)(2,1)}, u32[]{:S(2)}) copy-start(bf16[64,64,3,3]{1,0,3,2:T(8,128)(2,1)} %param.16) | copy-start | bytes 221188
  1.3 23.2 %collective-permute-start = (bf16[2,34,16,128]{3,2,1,0:T(8,128)(2,1)S(1)}, bf16[2,34,16,128]{3,2,1,0:T(8,128)(2,1)S(1)}, u32[]{:S(2)}, u32[]{:S(2)}) collective-permute-start(bf16[2,34,16,128]{3,2,1,0:T(8,128)(2,1)S(1)} %get-tuple-element.30), channel_id=1, source_target_pairs={{0,8},{1,5},{2,10},{3,7},{4,12},{5,1},{6,14},{7,3},{8,0},{9,13},{1... | collective-permute-start | bytes 835592 | tf_op jit(solution)/shard_map/ppermute | solution.py:347
  5.4 19.1 %collective-permute-start.1 = (bf16[2,34,16,128]{3,2,1,0:T(8,128)(2,1)S(1)}, bf16[2,34,16,128]{3,2,1,0:T(8,128)(2,1)S(1)}, u32[]{:S(2)}, u32[]{:S(2)}) collective-permute-start(bf16[2,34,16,128]{3,2,1,0:T(8,128)(2,1)S(1)} %get-tuple-element.31), channel_id=1, source_target_pairs={{0,12},{1,9},{2,14},{3,11},{4,8},{5,13},{6,10},{7,15},{8,4},{9,1},... | collective-permute-start | bytes 835592 | tf_op jit(solution)/shard_map/ppermute | solution.py:347
  6.8 17.7 %collective-permute-start.2 = (bf16[2,34,16,128]{3,2,1,0:T(8,128)(2,1)S(1)}, bf16[2,34,16,128]{3,2,1,0:T(8,128)(2,1)S(1)}, u32[]{:S(2)}, u32[]{:S(2)}) collective-permute-start(bf16[2,34,16,128]{3,2,1,0:T(8,128)(2,1)S(1)} %get-tuple-element.32), channel_id=1, source_target_pairs={{0,4},{1,13},{2,6},{3,15},{4,0},{5,9},{6,2},{7,11},{8,12},{9,5},{1... | collective-permute-start | bytes 835592 | tf_op jit(solution)/shard_map/ppermute | solution.py:347
  7.0 0.7 %copy-start.7 = (bf16[64,2,3,3]{0,1,3,2:T(2,128)(2,1)S(1)}, bf16[64,2,3,3]{0,1,3,2:T(2,128)(2,1)}, u32[]{:S(2)}) copy-start(bf16[64,2,3,3]{0,1,3,2:T(2,128)(2,1)} %param.14) | copy-start | bytes 6916
  7.7 0.7 %copy-start.8 = (s32[64]{0:T(128)S(1)}, s32[64]{0:T(128)}, u32[]{:S(2)}) copy-start(s32[64]{0:T(128)} %param.12) | copy-start | bytes 772
  8.4 0.7 %copy-start.3 = (bf16[2,64,3,3]{1,0,3,2:T(2,128)(2,1)S(1)}, bf16[2,64,3,3]{1,0,3,2:T(2,128)(2,1)}, u32[]{:S(2)}) copy-start(bf16[2,64,3,3]{1,0,3,2:T(2,128)(2,1)} %param.18) | copy-start | bytes 6916
  8.5 0.7 %copy-start.4 = (f32[64]{0:T(128)S(1)}, f32[64]{0:T(128)}, u32[]{:S(2)}) copy-start(f32[64]{0:T(128)} %param.15) | copy-start | bytes 772
  8.5 0.7 %copy-start.5 = (f32[64]{0:T(128)S(1)}, f32[64]{0:T(128)}, u32[]{:S(2)}) copy-start(f32[64]{0:T(128)} %param.17) | copy-start | bytes 772
  8.5 0.7 %copy-start.6 = (f32[2]{0:T(128)S(1)}, f32[2]{0:T(128)}, u32[]{:S(2)}) copy-start(f32[2]{0:T(128)} %b_out_ref.1) | copy-start | bytes 28
  9.1 15.4 %copy-start = (bf16[1,2,32,64,128]{4,3,2,1,0:T(8,128)(2,1)S(1)}, bf16[1,2,32,64,128]{4,3,2,1,0:T(8,128)(2,1)}, u32[]{:S(2)}) copy-start(bf16[1,2,32,64,128]{4,3,2,1,0:T(8,128)(2,1)} %maps_ref.3) | copy-start | bytes 3145732
  9.1 15.4 %copy-start.1 = (f32[1,2,64,128]{3,2,1,0:T(8,128)S(1)}, f32[1,2,64,128]{3,2,1,0:T(8,128)}, u32[]{:S(2)}) copy-start(f32[1,2,64,128]{3,2,1,0:T(8,128)} %field_ref.5) | copy-start | bytes 196612
  25.3 10.4 %collective-permute-start.3 = (f32[2,16,128]{2,1,0:T(8,128)S(1)}, f32[2,16,128]{2,1,0:T(8,128)S(1)}, u32[]{:S(2)}, u32[]{:S(2)}) collective-permute-start(f32[2,16,128]{2,1,0:T(8,128)S(1)} %get-tuple-element.47), channel_id=1, source_target_pairs={{0,8},{1,5},{2,10},{3,7},{4,12},{5,1},{6,14},{7,3},{8,0},{9,13},{1... | collective-permute-start | bytes 49160 | tf_op jit(solution)/shard_map/ppermute | solution.py:347
  33.7 5.5 %collective-permute-start.4 = (f32[2,16,128]{2,1,0:T(8,128)S(1)}, f32[2,16,128]{2,1,0:T(8,128)S(1)}, u32[]{:S(2)}, u32[]{:S(2)}) collective-permute-start(f32[2,16,128]{2,1,0:T(8,128)S(1)} %get-tuple-element.48), channel_id=1, source_target_pairs={{0,12},{1,9},{2,14},{3,11},{4,8},{5,13},{6,10},{7,15},{8,4},{9,1},... | collective-permute-start | bytes 49160 | tf_op jit(solution)/shard_map/ppermute | solution.py:347
  34.2 5.1 %collective-permute-start.5 = (f32[2,16,128]{2,1,0:T(8,128)S(1)}, f32[2,16,128]{2,1,0:T(8,128)S(1)}, u32[]{:S(2)}, u32[]{:S(2)}) collective-permute-start(f32[2,16,128]{2,1,0:T(8,128)S(1)} %get-tuple-element.49), channel_id=1, source_target_pairs={{0,4},{1,13},{2,6},{3,15},{4,0},{5,9},{6,2},{7,11},{8,12},{9,5},{1... | collective-permute-start | bytes 49160 | tf_op jit(solution)/shard_map/ppermute | solution.py:347

commit v4 on v3

--- a/solution.py
+++ b/solution.py
@@ -12,7 +12,8 @@
 QUAD = 4
 PAIR = 2
 PAD = 8
-ORDERS = ((2, 3, 1), (1, 2, 3))
+ORDERS = ((1, 2, 3), (3, 2, 1))
+BACK = (3, 2, 1)
 PACK_LIMIT = 8 << 20
 
 VMEM = pl.BlockSpec(memory_space=pltpu.VMEM)
@@ -30,6 +31,7 @@
     coils = maps_ref.shape[2]
     rows = out0.shape[1]
     share, distances = place(stride)
+    odd = distances[0] != ORDERS[0][0]
     own = pl.ds(pl.multiple_of(share * rows, rows), rows)
     offs = offs_ref[...]
     pieces = (None, one_ref, two_ref, three_ref)
@@ -75,14 +77,16 @@
 
     zeros = tuple(jnp.zeros(offs.shape, jnp.float32) for _ in range(2 * FOLDS))
     sums = lax.fori_loop(0, coils, step, zeros, unroll=8)
-    for k in range(FOLDS):
+    out0[0], out0[1] = 0.25 * sums[0], 0.25 * sums[1]
+    results = []
+    for k in range(1, FOLDS):
         real, imag = 0.25 * sums[2 * k], 0.25 * sums[2 * k + 1]
-        if k == 0:
-            outs[k][0], outs[k][1] = real, imag
-        else:
-            cosine, sine = units[k]
-            outs[k][0] = cosine * real + sine * imag
-            outs[k][1] = cosine * imag - sine * real
+        cosine, sine = units[k]
+        results.append((cosine * real + sine * imag, cosine * imag - sine * real))
+    for slot, distance in enumerate(BACK):
+        even, other = (results[order.index(distance)] for order in ORDERS)
+        for part in range(2):
+            outs[slot + 1][part] = jnp.where(odd, other[part], even[part])
 
 
 def fold(stride, coil_maps, field, pieces, offs):
@@ -114,10 +118,10 @@
     _, _, x_size, z = field_ref.shape
     rows = own_ref.shape[1]
     ch = b1_ref.shape[0]
-    share, distances = place(stride)
+    share, _ = place(stride)
     groups = x_size // GROUP
     for k, ref in enumerate((own_ref, one_ref, two_ref, three_ref)):
-        start = pl.multiple_of((share if k == 0 else share ^ distances[k - 1]) * rows, rows)
+        start = pl.multiple_of((share if k == 0 else share ^ BACK[k - 1]) * rows, rows)
         for part in range(2):
             padded[part, pl.ds(PAD + start, rows), :] = ref[part]
     edge = jnp.zeros((PAD, z), jnp.float32)
@@ -340,20 +344,20 @@
     rows = x_size // FOLDS
     share = lax.axis_index("gy") // stride
 
-    def trade(values):
+    def trade(values, *orders):
         out = []
-        for value, distances in zip(values, zip(*ORDERS)):
+        for value, distances in zip(values, zip(*orders)):
             pairs = [(j, (j // stride ^ distances[j % 2]) * stride + j % stride) for j in range(devices)]
             out.append(lax.ppermute(value, "gy", pairs))
         return out
 
-    pieces = trade(pack(stride, coil_maps, zero_filled))
+    pieces = trade(pack(stride, coil_maps, zero_filled), *ORDERS)
     weights = prepare(w_in, b_in, w_mid, b_mid, w_out, b_out, step_sizes, x_size, z)
     offs = lax.dynamic_slice_in_dim(offsets, share * rows, rows, 0)
     offs = jnp.broadcast_to(offs[:, None], (rows, z))
     pieces, weights, offs = lax.optimization_barrier((pieces, weights, offs))
     normals = fold(stride, coil_maps, zero_filled, pieces, offs)
-    normals = [normals[0]] + trade(normals[1:])
+    normals = [normals[0]] + trade(normals[1:], BACK, BACK)
     return denoise(stride, zero_filled, normals, weights)
 
 

time: 42.2 us -> 39.7 us (0.941)
  starting transfers between devices: 14.8 us -> 12.7 us
    ppermute x6, starting transfers between devices: 14.8 us -> 12.7 us  [trade(): out.append(lax.ppermute(value, 'gy', pairs))]
    ppermute x6, waiting for transfers between devices: 19.4 us -> 19 us  [trade(): out.append(lax.ppermute(value, 'gy', pairs))]
  transfers between devices with their start and end apart: 6 -> 6, of which waited for: 3 -> 4; matrix products, arithmetic and copies ran while one was open for 0% -> 0% of each run, Pallas kernels for 2% -> 2%
where the time goes in v4:
time: 39.7 us; the launch traced here: 39.5 us
  waiting for transfers between devices  19 us (48%)
  starting transfers between devices  12.7 us (32%)
  Pallas kernels  5.58 us (14%)
  local copies, waits for them, and re-layouts  1.52 us (4%)
  between operations  0.72 us (2%)
    ppermute x6, waiting for transfers between devices, trade(): out.append(lax.ppermute(value, 'gy', pairs))  19 us
    ppermute x6, starting transfers between devices, trade(): out.append(lax.ppermute(value, 'gy', pairs))  12.7 us
    pallas_call x1, Pallas kernels, denoise(): pl.pallas_call(functools.partial(denoise_kernel, stride), in_specs=[VMEM]...  2.72 us
    unnamed x18, local copies, waits for them, and re-layouts  1.36 us
    pallas_call x1, Pallas kernels, pack(): pl.pallas_call(functools.partial(pack_kernel, stride), in_specs=[HBM, HBM...  1.34 us
    pallas_call x1, Pallas kernels, prepare(): pl.pallas_call(prepare_kernel, in_specs=[VMEM] * 5 + [SMEM] * 2, out_spec...  0.86 us
  transfers between devices with their start and end apart: 6, of which 4 were waited for; matrix products, arithmetic and copies ran while one was open for 0% of the time, Pallas kernels for 2%

profile of v4, /device:TPU:0, one launch (start us, length us, event | category | flops | bytes accessed | tf_op | source)
XLA Modules:
  0.0 39.5 jit_solution(10837044234124107924)
XLA Ops:
  0.0 0.0 copy-start.2
  0.0 1.3 %pack.1 = (bf16[2,34,16,128]{3,2,1,0:T(8,128)(2,1)S(1)}, bf16[2,34,16,128]{3,2,1,0:T(8,128)(2,1)S(1)}, bf16[2,34,16,128]{3,2,1,0:T(8,128)(2,1)S(1)}) custom-call(bf16[1,2,32,64,128]{4,3,2,1,0:T(8,128)(2,1)} %maps_ref.3, f32[1,2,64,128]{3,2,1,0:T(8,128)} %field_ref.5), custom_call_target="tpu_custom_call" | custom-call | bytes 2000000 | tf_op jit(solution)/shard_map/pack/pallas_call | solution.py:324
  1.3 3.1 %collective-permute-start = (bf16[2,34,16,128]{3,2,1,0:T(8,128)(2,1)S(1)}, bf16[2,34,16,128]{3,2,1,0:T(8,128)(2,1)S(1)}, u32[]{:S(2)}, u32[]{:S(2)}) collective-permute-start(bf16[2,34,16,128]{3,2,1,0:T(8,128)(2,1)S(1)} %get-tuple-element.30), channel_id=1, source_target_pairs={{0,4},{1,13},{2,6},{3,15},{4,0},{5,9},{6,2},{7,11},{8,12},{9,5},{1... | collective-permute-start | bytes 835592 | tf_op jit(solution)/shard_map/ppermute | solution.py:351
  4.4 2.6 %collective-permute-start.1 = (bf16[2,34,16,128]{3,2,1,0:T(8,128)(2,1)S(1)}, bf16[2,34,16,128]{3,2,1,0:T(8,128)(2,1)S(1)}, u32[]{:S(2)}, u32[]{:S(2)}) collective-permute-start(bf16[2,34,16,128]{3,2,1,0:T(8,128)(2,1)S(1)} %get-tuple-element.31), channel_id=1, source_target_pairs={{0,8},{1,9},{2,10},{3,11},{4,12},{5,13},{6,14},{7,15},{8,0},{9,1},... | collective-permute-start | bytes 835592 | tf_op jit(solution)/shard_map/ppermute | solution.py:351
  7.0 0.0 collective-permute-start.2
  7.0 0.0 copy-start.7
  7.7 0.0 copy-done.7
  7.7 0.0 copy-start.8
  7.8 0.6 %copy-done.8 = s32[64]{0:T(128)S(1)} copy-done((s32[64]{0:T(128)S(1)}, s32[64]{0:T(128)}, u32[]{:S(2)}) %copy-start.8) | copy-done | bytes 280
  8.4 0.0 copy-start.3
  8.4 0.1 dynamic_slice.3
  8.5 0.0 copy-start.4
  8.5 0.0 copy-start.5
  8.5 0.0 copy-start.6
  8.5 0.0 copy-done.2
  8.5 0.6 %copy-done.3 = bf16[2,64,3,3]{1,0,3,2:T(2,128)(2,1)S(1)} copy-done((bf16[2,64,3,3]{1,0,3,2:T(2,128)(2,1)S(1)}, bf16[2,64,3,3]{1,0,3,2:T(2,128)(2,1)}, u32[]{:S(2)}) %copy-start.3) | copy-done | bytes 2328
  9.1 0.0 copy-done.4
  9.1 0.0 copy-done.5
  9.1 0.0 copy-done.6
  9.2 0.0 copy-start
  9.2 0.0 copy-start.1
  9.2 0.9 %prepare.1 = (bf16[1024,192]{1,0:T(8,128)(2,1)S(1)}, f32[64,128]{1,0:T(8,128)S(1)}, bf16[384,256]{1,0:T(8,128)(2,1)S(1)}, f32[64,128]{1,0:T(8,128)S(1)}, bf16[96...) custom-call(bf16[18,64]{1,0:T(8,128)(2,1)S(1)} %reshape.4.w_in_ref, f32[1,64]{1,0:T(1,128)S(1)} %bitcast.7, ...), custom_call_target="tpu_custom_call" | custom-call | flops 1000000000 | bytes 8000000 | tf_op jit(solution)/shard_map/prepare/pallas_call | solution.py:274
  10.0 4.9 %collective-permute-done.one_ref = bf16[2,34,16,128]{3,2,1,0:T(8,128)(2,1)S(1)} collective-permute-done((bf16[2,34,16,128]{3,2,1,0:T(8,128)(2,1)S(1)}, bf16[2,34,16,128]{3,2,1,0:T(8,128)(2,1)S(1)}, u32[]{:S(2)}, u32[]{:S(2)}) %collective-permute-start) | collective-permute-done | bytes 278560 | tf_op jit(solution)/shard_map/ppermute | solution.py:351
  14.9 10.5 %collective-permute-done.1.two_ref = bf16[2,34,16,128]{3,2,1,0:T(8,128)(2,1)S(1)} collective-permute-done((bf16[2,34,16,128]{3,2,1,0:T(8,128)(2,1)S(1)}, bf16[2,34,16,128]{3,2,1,0:T(8,128)(2,1)S(1)}, u32[]{:S(2)}, u32[]{:S(2)}) %collective-permute-start.1) | collective-permute-done | bytes 278560 | tf_op jit(solution)/shard_map/ppermute | solution.py:351
  25.4 0.0 collective-permute-done.2.three_ref
  25.4 0.1 broadcast_in_dim.14.offs_ref
  25.4 0.0 copy-done
  25.4 0.0 copy-done.1
  25.5 0.7 %fold.1 = (f32[2,16,128]{2,1,0:T(8,128)S(1)}, f32[2,16,128]{2,1,0:T(8,128)S(1)}, f32[2,16,128]{2,1,0:T(8,128)S(1)}, f32[2,16,128]{2,1,0:T(8,128)S(1)}) custom-call(bf16[1,2,32,64,128]{4,3,2,1,0:T(8,128)(2,1)S(1)} %copy-done, f32[1,2,64,128]{3,2,1,0:T(8,128)S(1)} %copy-done.1, bf16[2,34,16,128]{3,2,1,0:T(8,128)(2,1)S(1)} %collective-permute-done.one_ref, ...), custom_call_target="tpu_custom_call" | custom-call | flops 4587520 | bytes 1048576 | tf_op jit(solution)/shard_map/fold/pallas_call | solution.py:95
  26.1 3.7 %collective-permute-start.3 = (f32[2,16,128]{2,1,0:T(8,128)S(1)}, f32[2,16,128]{2,1,0:T(8,128)S(1)}, u32[]{:S(2)}, u32[]{:S(2)}) collective-permute-start(f32[2,16,128]{2,1,0:T(8,128)S(1)} %get-tuple-element.47), channel_id=1, source_target_pairs={{0,12},{1,13},{2,14},{3,15},{4,8},{5,9},{6,10},{7,11},{8,4},{9,5},... | collective-permute-start | bytes 49160 | tf_op jit(solution)/shard_map/ppermute | solution.py:351
  29.8 3.2 %collective-permute-start.4 = (f32[2,16,128]{2,1,0:T(8,128)S(1)}, f32[2,16,128]{2,1,0:T(8,128)S(1)}, u32[]{:S(2)}, u32[]{:S(2)}) collective-permute-start(f32[2,16,128]{2,1,0:T(8,128)S(1)} %get-tuple-element.48), channel_id=1, source_target_pairs={{0,8},{1,9},{2,10},{3,11},{4,12},{5,13},{6,14},{7,15},{8,0},{9,1},... | collective-permute-start | bytes 49160 | tf_op jit(solution)/shard_map/ppermute | solution.py:351
  33.0 0.1 collective-permute-start.5
  33.1 0.0 collective-permute-done.3.one_ref
  33.1 1.8 %collective-permute-done.4.two_ref = f32[2,16,128]{2,1,0:T(8,128)S(1)} collective-permute-done((f32[2,16,128]{2,1,0:T(8,128)S(1)}, f32[2,16,128]{2,1,0:T(8,128)S(1)}, u32[]{:S(2)}, u32[]{:S(2)}) %collective-permute-start.4) | collective-permute-done | bytes 16416 | tf_op jit(solution)/shard_map/ppermute | solution.py:351
  34.9 1.8 %collective-permute-done.5.three_ref = f32[2,16,128]{2,1,0:T(8,128)S(1)} collective-permute-done((f32[2,16,128]{2,1,0:T(8,128)S(1)}, f32[2,16,128]{2,1,0:T(8,128)S(1)}, u32[]{:S(2)}, u32[]{:S(2)}) %collective-permute-start.5) | collective-permute-done | bytes 16416 | tf_op jit(solution)/shard_map/ppermute | solution.py:351
  36.8 2.7 %denoise.1 = f32[1,2,64,128]{3,2,1,0:T(8,128)} custom-call(f32[64,128]{1,0:T(8,128)S(1)} %get-tuple-element.40.step_ref, f32[32,128]{1,0:T(8,128)S(1)} %get-tuple-element.41.tail_ref, f32[1,2,64,128]{3,2,1,0:T(8,128)S(1)} %copy-done.1, f32[2,16,128]{2,1,0:T(8,128)S(1)} %get-tuple-element.46.own_ref, f32[2,16,128]{2,1,0:T(8,128)S(1)} %collective-permute-done.3.one_ref, ...), custom_call_target="tpu_custom_call" | custom-call | flops 4000000000 | bytes 2000000 | tf_op jit(solution)/shard_map/denoise/pallas_call | solution.py:205
  (1 shorter events, 0.0 us)
Async XLA Ops:
  0.0 8.5 %copy-start.2 = (bf16[64,64,3,3]{1,0,3,2:T(8,128)(2,1)S(1)}, bf16[64,64,3,3]{1,0,3,2:T(8,128)(2,1)}, u32[]{:S(2)}) copy-start(bf16[64,64,3,3]{1,0,3,2:T(8,128)(2,1)} %param.16) | copy-start | bytes 221188
  1.3 13.5 %collective-permute-start = (bf16[2,34,16,128]{3,2,1,0:T(8,128)(2,1)S(1)}, bf16[2,34,16,128]{3,2,1,0:T(8,128)(2,1)S(1)}, u32[]{:S(2)}, u32[]{:S(2)}) collective-permute-start(bf16[2,34,16,128]{3,2,1,0:T(8,128)(2,1)S(1)} %get-tuple-element.30), channel_id=1, source_target_pairs={{0,4},{1,13},{2,6},{3,15},{4,0},{5,9},{6,2},{7,11},{8,12},{9,5},{1... | collective-permute-start | bytes 835592 | tf_op jit(solution)/shard_map/ppermute | solution.py:351
  4.4 20.9 %collective-permute-start.1 = (bf16[2,34,16,128]{3,2,1,0:T(8,128)(2,1)S(1)}, bf16[2,34,16,128]{3,2,1,0:T(8,128)(2,1)S(1)}, u32[]{:S(2)}, u32[]{:S(2)}) collective-permute-start(bf16[2,34,16,128]{3,2,1,0:T(8,128)(2,1)S(1)} %get-tuple-element.31), channel_id=1, source_target_pairs={{0,8},{1,9},{2,10},{3,11},{4,12},{5,13},{6,14},{7,15},{8,0},{9,1},... | collective-permute-start | bytes 835592 | tf_op jit(solution)/shard_map/ppermute | solution.py:351
  7.0 18.3 %collective-permute-start.2 = (bf16[2,34,16,128]{3,2,1,0:T(8,128)(2,1)S(1)}, bf16[2,34,16,128]{3,2,1,0:T(8,128)(2,1)S(1)}, u32[]{:S(2)}, u32[]{:S(2)}) collective-permute-start(bf16[2,34,16,128]{3,2,1,0:T(8,128)(2,1)S(1)} %get-tuple-element.32), channel_id=1, source_target_pairs={{0,12},{1,5},{2,14},{3,7},{4,8},{5,1},{6,10},{7,3},{8,4},{9,13},{1... | collective-permute-start | bytes 835592 | tf_op jit(solution)/shard_map/ppermute | solution.py:351
  7.0 0.7 %copy-start.7 = (bf16[64,2,3,3]{0,1,3,2:T(2,128)(2,1)S(1)}, bf16[64,2,3,3]{0,1,3,2:T(2,128)(2,1)}, u32[]{:S(2)}) copy-start(bf16[64,2,3,3]{0,1,3,2:T(2,128)(2,1)} %param.14) | copy-start | bytes 6916
  7.7 0.7 %copy-start.8 = (s32[64]{0:T(128)S(1)}, s32[64]{0:T(128)}, u32[]{:S(2)}) copy-start(s32[64]{0:T(128)} %param.12) | copy-start | bytes 772
  8.4 0.7 %copy-start.3 = (bf16[2,64,3,3]{1,0,3,2:T(2,128)(2,1)S(1)}, bf16[2,64,3,3]{1,0,3,2:T(2,128)(2,1)}, u32[]{:S(2)}) copy-start(bf16[2,64,3,3]{1,0,3,2:T(2,128)(2,1)} %param.18) | copy-start | bytes 6916
  8.5 0.7 %copy-start.4 = (f32[64]{0:T(128)S(1)}, f32[64]{0:T(128)}, u32[]{:S(2)}) copy-start(f32[64]{0:T(128)} %param.15) | copy-start | bytes 772
  8.5 0.7 %copy-start.5 = (f32[64]{0:T(128)S(1)}, f32[64]{0:T(128)}, u32[]{:S(2)}) copy-start(f32[64]{0:T(128)} %param.17) | copy-start | bytes 772
  8.5 0.7 %copy-start.6 = (f32[2]{0:T(128)S(1)}, f32[2]{0:T(128)}, u32[]{:S(2)}) copy-start(f32[2]{0:T(128)} %b_out_ref.1) | copy-start | bytes 28
  9.2 16.3 %copy-start = (bf16[1,2,32,64,128]{4,3,2,1,0:T(8,128)(2,1)S(1)}, bf16[1,2,32,64,128]{4,3,2,1,0:T(8,128)(2,1)}, u32[]{:S(2)}) copy-start(bf16[1,2,32,64,128]{4,3,2,1,0:T(8,128)(2,1)} %maps_ref.3) | copy-start | bytes 3145732
  9.2 16.3 %copy-start.1 = (f32[1,2,64,128]{3,2,1,0:T(8,128)S(1)}, f32[1,2,64,128]{3,2,1,0:T(8,128)}, u32[]{:S(2)}) copy-start(f32[1,2,64,128]{3,2,1,0:T(8,128)} %field_ref.5) | copy-start | bytes 196612
  26.1 7.0 %collective-permute-start.3 = (f32[2,16,128]{2,1,0:T(8,128)S(1)}, f32[2,16,128]{2,1,0:T(8,128)S(1)}, u32[]{:S(2)}, u32[]{:S(2)}) collective-permute-start(f32[2,16,128]{2,1,0:T(8,128)S(1)} %get-tuple-element.47), channel_id=1, source_target_pairs={{0,12},{1,13},{2,14},{3,15},{4,8},{5,9},{6,10},{7,11},{8,4},{9,5},... | collective-permute-start | bytes 49160 | tf_op jit(solution)/shard_map/ppermute | solution.py:351
  29.8 5.1 %collective-permute-start.4 = (f32[2,16,128]{2,1,0:T(8,128)S(1)}, f32[2,16,128]{2,1,0:T(8,128)S(1)}, u32[]{:S(2)}, u32[]{:S(2)}) collective-permute-start(f32[2,16,128]{2,1,0:T(8,128)S(1)} %get-tuple-element.48), channel_id=1, source_target_pairs={{0,8},{1,9},{2,10},{3,11},{4,12},{5,13},{6,14},{7,15},{8,0},{9,1},... | collective-permute-start | bytes 49160 | tf_op jit(solution)/shard_map/ppermute | solution.py:351
  33.0 3.7 %collective-permute-start.5 = (f32[2,16,128]{2,1,0:T(8,128)S(1)}, f32[2,16,128]{2,1,0:T(8,128)S(1)}, u32[]{:S(2)}, u32[]{:S(2)}) collective-permute-start(f32[2,16,128]{2,1,0:T(8,128)S(1)} %get-tuple-element.49), channel_id=1, source_target_pairs={{0,4},{1,5},{2,6},{3,7},{4,0},{5,1},{6,2},{7,3},{8,12},{9,13},{10,... | collective-permute-start | bytes 49160 | tf_op jit(solution)/shard_map/ppermute | solution.py:351

commit v5 on v4

--- a/solution.py
+++ b/solution.py
@@ -15,6 +15,8 @@
 ORDERS = ((1, 2, 3), (3, 2, 1))
 BACK = (3, 2, 1)
 PACK_LIMIT = 8 << 20
+CHUNKS = 2
+SENT = ((0, (0, 1)), (1, (0,)), (2, (0,)), (1, (1,)), (2, (1,)))
 
 VMEM = pl.BlockSpec(memory_space=pltpu.VMEM)
 HBM = pl.BlockSpec(memory_space=pltpu.HBM)
@@ -27,14 +29,14 @@
     return position // stride, [jnp.where(odd == 0, even, other) for even, other in zip(*ORDERS)]
 
 
-def fold_kernel(stride, maps_ref, field_ref, one_ref, two_ref, three_ref, offs_ref, out0, out1, out2, out3):
+def fold_kernel(stride, chunk, maps_ref, field_ref, one_ref, two_ref, three_ref, offs_ref, out0, out1, out2, out3):
     coils = maps_ref.shape[2]
     rows = out0.shape[1]
     share, distances = place(stride)
     odd = distances[0] != ORDERS[0][0]
-    own = pl.ds(pl.multiple_of(share * rows, rows), rows)
-    offs = offs_ref[...]
-    pieces = (None, one_ref, two_ref, three_ref)
+    own = pl.ds(pl.multiple_of((chunk * FOLDS + share) * rows, rows), rows)
+    offs = offs_ref[chunk]
+    pieces = (None, one_ref.at[:, :, pl.ds(chunk * rows, rows), :], two_ref, three_ref)
     outs = (out0, out1, out2, out3)
     turned = []
     units = []
@@ -89,11 +91,11 @@
             outs[slot + 1][part] = jnp.where(odd, other[part], even[part])
 
 
-def fold(stride, coil_maps, field, pieces, offs):
+def fold(stride, chunk, coil_maps, field, pieces, offs):
     coils = coil_maps.shape[2]
-    rows, z = offs.shape
+    _, rows, z = offs.shape
     return pl.pallas_call(
-        functools.partial(fold_kernel, stride),
+        functools.partial(fold_kernel, stride, chunk),
         in_specs=[VMEM] * 6,
         out_specs=[VMEM] * FOLDS,
         out_shape=[jax.ShapeDtypeStruct((2, rows, z), jnp.float32)] * FOLDS,
@@ -111,102 +113,157 @@
     return jnp.where(lane == width - 1, 0.0, pltpu.roll(value, width - 1, 1))
 
 
-def denoise_kernel(
-    stride, step_ref, tail_ref, field_ref, own_ref, one_ref, two_ref, three_ref,
-    w1_ref, b1_ref, w2_ref, b2_ref, w3_ref, out_ref, padded, window, low, hidden_one, hidden_two,
-):
+def denoise_kernel(stride, chunk, *refs):
+    step_ref, tail_ref, field_ref, w1_ref, b1_ref, w2_ref, b2_ref, w3_ref, *normals = refs[:12]
+    padded, window, low, hidden_one, hidden_two = refs[-5:]
     _, _, x_size, z = field_ref.shape
-    rows = own_ref.shape[1]
     ch = b1_ref.shape[0]
+    half = x_size // 2
+    cut = half - QUAD
+    if chunk == 0:
+        out_ref, line_ref, one_ref, two_ref = refs[12:16]
+        begin, end, blank = 0, half, 0
+    else:
+        done_ref, line_ref, one_ref, two_ref, out_ref = refs[12:17]
+        begin, end, blank = half, x_size, half - GROUP
     share, _ = place(stride)
-    groups = x_size // GROUP
-    for k, ref in enumerate((own_ref, one_ref, two_ref, three_ref)):
-        start = pl.multiple_of((share if k == 0 else share ^ BACK[k - 1]) * rows, rows)
-        for part in range(2):
-            padded[part, pl.ds(PAD + start, rows), :] = ref[part]
+    rows = normals[0].shape[1]
+    for k, ref in enumerate(normals):
+        source = share if k == 0 else share ^ BACK[k - 1]
+        start = pl.multiple_of(PAD + begin + source * rows, rows)
+        for part in range(2):
+            padded[part, pl.ds(start, rows), :] = ref[part]
     edge = jnp.zeros((PAD, z), jnp.float32)
     for part in range(2):
-        padded[part, 0:PAD, :] = edge
-        padded[part, PAD + x_size : PAD + x_size + PAD, :] = edge
-        base = field_ref[0, part]
-        stepped = base - step_ref[...] * (padded[part, PAD : PAD + x_size, :] - base)
-        padded[part, PAD : PAD + x_size, :] = stepped
-    lane = lax.broadcasted_iota(jnp.int32, (x_size + 2 * PAD, z), 1)
+        padded[part, PAD + end : PAD + end + PAD, :] = edge
+        if chunk == 0:
+            padded[part, 0:PAD, :] = edge
+        else:
+            padded[part, half - GROUP : half - GROUP + PAD, :] = edge
+            padded[part, half - GROUP + PAD : half - GROUP + 2 * PAD, :] = edge
+            padded[part, half : half + PAD, :] = line_ref[part]
+        base = field_ref[0, part, begin:end, :]
+        stepped = base - step_ref[begin:end, :] * (padded[part, PAD + begin : PAD + end, :] - base)
+        padded[part, PAD + begin : PAD + end, :] = stepped
+    first, last = blank, end + 2 * PAD
+    lane = lax.broadcasted_iota(jnp.int32, (last - first, z), 1)
     for tap in range(3):
         for part in range(2):
-            window[tap, part] = shifted(padded[part], lane, tap, z).astype(jnp.bfloat16)
+            window[tap, part, first:last, :] = shifted(padded[part, first:last, :], lane, tap, z).astype(jnp.bfloat16)
     span = GROUP + 2 * PAD
-    for g in range(groups):
+    groups = range(blank // GROUP, end // GROUP)
+    for g in groups:
         for tap in range(3):
             for part in range(2):
                 low[(tap * 2 + part) * span : (tap * 2 + part + 1) * span, g * z : (g + 1) * z] = window[
                     tap, part, g * GROUP : g * GROUP + span, :
                 ]
+
+    def block(x, count=1):
+        return slice((x + 1) * ch, (x + 1 + count) * ch)
+
     empty = jnp.zeros((ch, z), jnp.bfloat16)
-    for hidden in (hidden_one, hidden_two):
-        hidden[0:ch, :] = empty
-        hidden[(x_size + 1) * ch : (x_size + 2) * ch, :] = empty
+    hidden_one[block(end)] = empty
+    hidden_two[block(end)] = empty
+    if chunk == 0:
+        hidden_one[block(-1)] = empty
+        hidden_two[block(-1)] = empty
+    else:
+        hidden_one[block(cut - 1, QUAD)] = one_ref[...]
+        for x in range(half - GROUP - 1, cut - 1):
+            hidden_two[block(x)] = empty
+        hidden_two[block(cut - 1)] = two_ref[...]
 
     bias = b1_ref[...]
+    if chunk == 1:
+        g = half // GROUP - 1
+        out = jnp.dot(
+            w1_ref[(GROUP - 1) * ch :, :], low[:, g * z : (g + 1) * z], preferred_element_type=jnp.float32
+        )
+        hidden_one[block(half - 1)] = jnp.maximum(out + bias, 0.0).astype(jnp.bfloat16)
     for r in range(0, GROUP, QUAD):
-        for g in range(0, groups, 2):
+        for g in range(begin // GROUP, end // GROUP, 2):
             out = jnp.dot(
                 w1_ref[r * ch : (r + QUAD) * ch, :], low[:, g * z : (g + 2) * z], preferred_element_type=jnp.float32
             )
             for i in range(QUAD):
                 for j in range(2):
                     value = jnp.maximum(out[i * ch : (i + 1) * ch, j * z : (j + 1) * z] + bias, 0.0)
-                    row = (g + j) * GROUP + r + i + 1
-                    hidden_one[row * ch : (row + 1) * ch, :] = value.astype(jnp.bfloat16)
+                    hidden_one[block((g + j) * GROUP + r + i)] = value.astype(jnp.bfloat16)
 
     bias = b2_ref[...]
     lane = lax.broadcasted_iota(jnp.int32, (ch, z), 1)
-    half = x_size // 2
-    for q in range(0, half, PAIR):
-        column = lambda first: hidden_one[first * ch : (first + PAIR + 2) * ch, :]
+    start = 0 if chunk == 0 else cut
+    stride = (end - start) // 2
+    for q in range(start, start + stride, PAIR):
         out = jnp.dot(
-            w2_ref[...], jnp.concatenate([column(q), column(q + half)], axis=1), preferred_element_type=jnp.float32
+            w2_ref[...],
+            jnp.concatenate([hidden_one[block(q - 1, PAIR + 2)], hidden_one[block(q + stride - 1, PAIR + 2)]], axis=1),
+            preferred_element_type=jnp.float32,
         )
         for i in range(PAIR):
             for j in range(2):
                 total = bias
                 for tap in range(3):
-                    first = (tap * PAIR + i) * ch
-                    total = total + shifted(out[first : first + ch, j * z : (j + 1) * z], lane, tap, z)
-                row = q + j * half + i + 1
-                hidden_two[row * ch : (row + 1) * ch, :] = jnp.maximum(total, 0.0).astype(jnp.bfloat16)
+                    at = (tap * PAIR + i) * ch
+                    total = total + shifted(out[at : at + ch, j * z : (j + 1) * z], lane, tap, z)
+                hidden_two[block(q + j * stride + i)] = jnp.maximum(total, 0.0).astype(jnp.bfloat16)
 
     lane = lax.broadcasted_iota(jnp.int32, (2 * GROUP, z), 1)
-    for g in range(0, groups, 2):
-        column = lambda first: hidden_two[first * GROUP * ch : (first * GROUP + GROUP + 2) * ch, :]
-        out = jnp.dot(
-            w3_ref[...], jnp.concatenate([column(g), column(g + 1)], axis=1), preferred_element_type=jnp.float32
-        )
-        for j in range(2):
-            total = None
-            for tap in range(3):
-                part = out[tap * 2 * GROUP : (tap + 1) * 2 * GROUP, j * z : (j + 1) * z]
-                part = shifted(part, lane, tap, z)
-                total = part if total is None else total + part
-            first = (g + j) * GROUP
-            for part in range(2):
-                out_ref[0, part, first : first + GROUP, :] = (
-                    padded[part, PAD + first : PAD + first + GROUP, :]
-                    + total[part * GROUP : (part + 1) * GROUP]
-                    + tail_ref[part * GROUP : (part + 1) * GROUP, :]
-                )
-
-
-def denoise(stride, field, normals, weights):
+    starts = [g * GROUP for g in groups]
+    out = jnp.dot(
+        w3_ref[...],
+        jnp.concatenate([hidden_two[block(x - 1, GROUP + 2)] for x in starts], axis=1),
+        preferred_element_type=jnp.float32,
+    )
+    for j, x in enumerate(starts):
+        total = None
+        for tap in range(3):
+            part = out[tap * 2 * GROUP : (tap + 1) * 2 * GROUP, j * z : (j + 1) * z]
+            part = shifted(part, lane, tap, z)
+            total = part if total is None else total + part
+        for part in range(2):
+            value = (
+                padded[part, PAD + x : PAD + x + GROUP, :]
+                + total[part * GROUP : (part + 1) * GROUP]
+                + tail_ref[part * GROUP : (part + 1) * GROUP, :]
+            )
+            if chunk == 0:
+                out_ref[part, x : x + GROUP, :] = value
+            elif x < half:
+                keep = lax.broadcasted_iota(jnp.int32, (GROUP, z), 0) < cut - x
+                out_ref[0, part, 0:x, :] = done_ref[part, 0:x, :]
+                out_ref[0, part, x:half, :] = jnp.where(keep, done_ref[part, x:half, :], value)
+            else:
+                out_ref[0, part, x : x + GROUP, :] = value
+    if chunk == 0:
+        for part in range(2):
+            line_ref[part] = padded[part, half : half + PAD, :]
+        one_ref[...] = hidden_one[block(cut - 1, QUAD)]
+        two_ref[...] = hidden_two[block(cut - 1)]
+
+
+def denoise(stride, chunk, field, normals, weights, state):
     _, _, x_size, z = field.shape
     w1, b1, w2, b2, w3, tail, step = weights
     ch = b1.shape[0]
     span = GROUP + 2 * PAD
+    if chunk == 0:
+        out_shape = [
+            jax.ShapeDtypeStruct((2, x_size // 2, z), jnp.float32),
+            jax.ShapeDtypeStruct((2, PAD, z), jnp.float32),
+            jax.ShapeDtypeStruct((QUAD * ch, z), jnp.bfloat16),
+            jax.ShapeDtypeStruct((ch, z), jnp.bfloat16),
+        ]
+        out_specs = [VMEM] * 4
+    else:
+        out_shape = jax.ShapeDtypeStruct(field.shape, jnp.float32)
+        out_specs = VMEM
     return pl.pallas_call(
-        functools.partial(denoise_kernel, stride),
-        in_specs=[VMEM] * 12,
-        out_specs=VMEM,
-        out_shape=jax.ShapeDtypeStruct(field.shape, jnp.float32),
+        functools.partial(denoise_kernel, stride, chunk),
+        in_specs=[VMEM] * (12 + len(state)),
+        out_specs=out_specs,
+        out_shape=out_shape,
         scratch_shapes=[
             pltpu.VMEM((2, x_size + 2 * PAD, z), jnp.float32),
             pltpu.VMEM((3, 2, x_size + 2 * PAD, z), jnp.bfloat16),
@@ -214,10 +271,10 @@
             pltpu.VMEM(((x_size + 2) * ch, z), jnp.bfloat16),
             pltpu.VMEM(((x_size + 2) * ch, z), jnp.bfloat16),
         ],
-        cost_estimate=pl.CostEstimate(flops=4_000_000_000, bytes_accessed=2_000_000, transcendentals=0),
+        cost_estimate=pl.CostEstimate(flops=2_000_000_000, bytes_accessed=2_000_000, transcendentals=0),
         compiler_params=pltpu.CompilerParams(vmem_limit_bytes=16 << 20),
-        name="denoise",
-    )(step, tail, field, *normals, w1, b1, w2, b2, w3)
+        name=("denoise_first", "denoise_rest")[chunk],
+    )(step, tail, field, w1, b1, w2, b2, w3, *normals, *state)
 
 
 def prepare_kernel(
@@ -290,45 +347,49 @@
     )
 
 
-def pack_kernel(stride, maps_ref, field_ref, one_ref, two_ref, three_ref, held, sems, field_sem):
+def pack_kernel(stride, maps_ref, field_ref, *refs):
+    outs, (held, sems, field_sem) = refs[:-3], refs[-3:]
     coils = maps_ref.shape[2]
-    rows = one_ref.shape[2]
+    rows = outs[-1].shape[2]
     share, distances = place(stride)
     field_copy = pltpu.make_async_copy(field_ref.at[0], held, field_sem)
     field_copy.start()
     copies = []
-    outs = (one_ref, two_ref, three_ref)
-    for i, ref in enumerate(outs):
-        first = pl.multiple_of((share ^ distances[i]) * rows, rows)
-        for part in range(2):
-            copy = pltpu.make_async_copy(
-                maps_ref.at[0, part, :, pl.ds(first, rows), :], ref.at[part, 0:coils], sems.at[i, part]
-            )
-            copy.start()
-            copies.append(copy)
+    spans = []
+    for ref, (i, chunks) in zip(outs, SENT):
+        for at, chunk in enumerate(chunks):
+            first = pl.multiple_of((chunk * FOLDS + (share ^ distances[i])) * rows, rows)
+            here, there = pl.ds(first, rows), pl.ds(at * rows, rows)
+            spans.append((ref, here, there))
+            for part in range(2):
+                copy = pltpu.make_async_copy(
+                    maps_ref.at[0, part, :, here, :], ref.at[part, 0:coils, there, :], sems.at[len(copies)]
+                )
+                copy.start()
+                copies.append(copy)
     field_copy.wait()
-    for i, ref in enumerate(outs):
-        first = pl.multiple_of((share ^ distances[i]) * rows, rows)
-        for part in range(2):
-            value = held[part, pl.ds(first, rows), :]
+    for ref, here, there in spans:
+        for part in range(2):
+            value = held[part, here, :]
             high = value.astype(jnp.bfloat16)
-            ref[part, coils] = high
-            ref[part, coils + 1] = (value - high.astype(jnp.float32)).astype(jnp.bfloat16)
+            ref[part, coils, there, :] = high
+            ref[part, coils + 1, there, :] = (value - high.astype(jnp.float32)).astype(jnp.bfloat16)
     for copy in copies:
         copy.wait()
 
 
 def pack(stride, coil_maps, field):
     _, _, coils, x_size, z = coil_maps.shape
-    piece = jax.ShapeDtypeStruct((2, coils + 2, x_size // FOLDS, z), jnp.bfloat16)
+    rows = x_size // FOLDS // CHUNKS
+    pieces = [jax.ShapeDtypeStruct((2, coils + 2, len(chunks) * rows, z), jnp.bfloat16) for _, chunks in SENT]
     return pl.pallas_call(
         functools.partial(pack_kernel, stride),
         in_specs=[HBM, HBM],
-        out_specs=[VMEM] * 3,
-        out_shape=[piece] * 3,
+        out_specs=[VMEM] * len(pieces),
+        out_shape=pieces,
         scratch_shapes=[
             pltpu.VMEM((2, x_size, z), jnp.float32),
-            pltpu.SemaphoreType.DMA((3, 2)),
+            pltpu.SemaphoreType.DMA((2 * sum(len(chunks) for _, chunks in SENT),)),
             pltpu.SemaphoreType.DMA,
         ],
         cost_estimate=pl.CostEstimate(flops=0, bytes_accessed=2_000_000, transcendentals=0),
@@ -341,24 +402,30 @@
     devices = lax.axis_size("gy")
     stride = devices // FOLDS
     x_size, z = zero_filled.shape[2:]
-    rows = x_size // FOLDS
+    rows = x_size // FOLDS // CHUNKS
     share = lax.axis_index("gy") // stride
 
-    def trade(values, *orders):
-        out = []
-        for value, distances in zip(values, zip(*orders)):
-            pairs = [(j, (j // stride ^ distances[j % 2]) * stride + j % stride) for j in range(devices)]
-            out.append(lax.ppermute(value, "gy", pairs))
-        return out
-
-    pieces = trade(pack(stride, coil_maps, zero_filled), *ORDERS)
+    def trade(value, distances):
+        pairs = [(j, (j // stride ^ distances[j % 2]) * stride + j % stride) for j in range(devices)]
+        return lax.ppermute(value, "gy", pairs)
+
+    sent = pack(stride, coil_maps, zero_filled)
+    pieces = [trade(value, [order[i] for order in ORDERS]) for value, (i, _) in zip(sent, SENT)]
+    chunks = [
+        [next(piece for piece, (j, held) in zip(pieces, SENT) if i == j and chunk in held) for i in range(FOLDS - 1)]
+        for chunk in range(CHUNKS)
+    ]
     weights = prepare(w_in, b_in, w_mid, b_mid, w_out, b_out, step_sizes, x_size, z)
-    offs = lax.dynamic_slice_in_dim(offsets, share * rows, rows, 0)
-    offs = jnp.broadcast_to(offs[:, None], (rows, z))
-    pieces, weights, offs = lax.optimization_barrier((pieces, weights, offs))
-    normals = fold(stride, coil_maps, zero_filled, pieces, offs)
-    normals = [normals[0]] + trade(normals[1:], BACK, BACK)
-    return denoise(stride, zero_filled, normals, weights)
+    offs = lax.dynamic_index_in_dim(offsets.reshape(CHUNKS, FOLDS, rows), share, 1, keepdims=False)
+    offs = jnp.broadcast_to(offs[:, :, None], (CHUNKS, rows, z))
+    chunks[0], weights, offs = lax.optimization_barrier((chunks[0], weights, offs))
+    first = fold(stride, 0, coil_maps, zero_filled, chunks[0], offs)
+    first = [first[0]] + [trade(value, (k, k)) for value, k in zip(first[1:], BACK)]
+    rest = fold(stride, 1, coil_maps, zero_filled, chunks[1], offs)
+    back = [trade(value, (k, k)) for value, k in zip(rest[1:], BACK)]
+    first, own = lax.optimization_barrier((first, rest[0]))
+    state = denoise(stride, 0, zero_filled, first, weights, [])
+    return denoise(stride, 1, zero_filled, [own] + back, weights, state)
 
 
 def solution(mesh):

time: 39.7 us -> 39.1 us (0.985)
  waiting for transfers between devices: 19 us -> 5.54 us
  starting transfers between devices: 12.7 us -> 22.5 us
  local copies, waits for them, and re-layouts: 1.52 us -> 3.5 us
  Pallas kernels: 5.58 us -> 6.63 us
    ppermute x6 -> x11, waiting for transfers between devices: 19 us -> 5.54 us  [trade(): return lax.ppermute(value, 'gy', pairs)]
    ppermute x6 -> x11, starting transfers between devices: 12.7 us -> 22.5 us  [trade(): return lax.ppermute(value, 'gy', pairs)]
    unnamed x18 -> x28, local copies, waits for them, and re-layouts: 1.36 us -> 2.63 us
    pallas_call x2 -> x4, Pallas kernels: 3.38 us -> 4.4 us  [the longest x2 3.72 us: denoise(): pl.pallas_call(functools.partial(denoise_kernel, stride, chunk), in_specs...]
    reshape x0 -> x1, local copies, waits for them, and re-layouts: none -> 0.77 us  [per_device(): offsets.reshape(CHUNKS, FOLDS, rows)]
  transfers between devices with their start and end apart: 6 -> 11, of which waited for: 4 -> 2; matrix products, arithmetic and copies ran while one was open for 0% -> 2% of each run, Pallas kernels for 2% -> 8%
where the time goes in v5:
time: 39.1 us; the launch traced here: 38.9 us
  starting transfers between devices  22.5 us (58%)
  Pallas kernels  6.63 us (17%)
  waiting for transfers between devices  5.54 us (14%)
  local copies, waits for them, and re-layouts  3.5 us (9%)
  between operations  0.81 us (2%)
    ppermute x11, starting transfers between devices, trade(): return lax.ppermute(value, 'gy', pairs)  22.5 us
    ppermute x11, waiting for transfers between devices, trade(): return lax.ppermute(value, 'gy', pairs)  5.54 us
    pallas_call x2, Pallas kernels, denoise(): pl.pallas_call(functools.partial(denoise_kernel, stride, chunk), in_specs...  3.72 us
    unnamed x28, local copies, waits for them, and re-layouts  2.63 us
    pallas_call x1, Pallas kernels, pack(): pl.pallas_call(functools.partial(pack_kernel, stride), in_specs=[HBM, HBM...  1.35 us
    pallas_call x1, Pallas kernels, prepare(): pl.pallas_call(prepare_kernel, in_specs=[VMEM] * 5 + [SMEM] * 2, out_spec...  0.87 us
  transfers between devices with their start and end apart: 11, of which 2 were waited for; matrix products, arithmetic and copies ran while one was open for 2% of the time, Pallas kernels for 8%

profile of v5, /device:TPU:0, one launch (start us, length us, event | category | flops | bytes accessed | tf_op | source)
XLA Modules:
  0.0 38.9 jit_solution(7153850107077223383)
XLA Ops:
  0.0 1.4 %pack.1 = (bf16[2,34,16,128]{3,2,1,0:T(8,128)(2,1)S(1)}, bf16[2,34,8,128]{3,2,1,0:T(8,128)(2,1)S(1)}, bf16[2,34,8,128]{3,2,1,0:T(8,128)(2,1)S(1)}, bf16[2,34,8,1...) custom-call(bf16[1,2,32,64,128]{4,3,2,1,0:T(8,128)(2,1)} %maps_ref.5, f32[1,2,64,128]{3,2,1,0:T(8,128)} %refs_2_.3), custom_call_target="tpu_custom_call" | custom-call | bytes 2000000 | tf_op jit(solution)/shard_map/pack/pallas_call | solution.py:385
  1.4 0.0 copy-start.13
  1.4 3.1 %collective-permute-start = (bf16[2,34,16,128]{3,2,1,0:T(8,128)(2,1)S(1)}, bf16[2,34,16,128]{3,2,1,0:T(8,128)(2,1)S(1)}, u32[]{:S(2)}, u32[]{:S(2)}) collective-permute-start(bf16[2,34,16,128]{3,2,1,0:T(8,128)(2,1)S(1)} %get-tuple-element.45), channel_id=1, source_target_pairs={{0,4},{1,13},{2,6},{3,15},{4,0},{5,9},{6,2},{7,11},{8,12},{9,5},{1... | collective-permute-start | bytes 835592 | tf_op jit(solution)/shard_map/ppermute | solution.py:410
  4.5 2.6 %collective-permute-start.1 = (bf16[2,34,8,128]{3,2,1,0:T(8,128)(2,1)S(1)}, bf16[2,34,8,128]{3,2,1,0:T(8,128)(2,1)S(1)}, u32[]{:S(2)}, u32[]{:S(2)}) collective-permute-start(bf16[2,34,8,128]{3,2,1,0:T(8,128)(2,1)S(1)} %get-tuple-element.46), channel_id=1, source_target_pairs={{0,8},{1,9},{2,10},{3,11},{4,12},{5,13},{6,14},{7,15},{8,0},{9,1},... | collective-permute-start | bytes 417800 | tf_op jit(solution)/shard_map/ppermute | solution.py:410
  7.1 0.0 collective-permute-start.2
  7.1 1.9 %collective-permute-start.6 = (bf16[2,34,8,128]{3,2,1,0:T(8,128)(2,1)S(1)}, bf16[2,34,8,128]{3,2,1,0:T(8,128)(2,1)S(1)}, u32[]{:S(2)}, u32[]{:S(2)}) collective-permute-start(bf16[2,34,8,128]{3,2,1,0:T(8,128)(2,1)S(1)} %get-tuple-element.70), channel_id=1, source_target_pairs={{0,8},{1,9},{2,10},{3,11},{4,12},{5,13},{6,14},{7,15},{8,0},{9,1},... | collective-permute-start | bytes 417800 | tf_op jit(solution)/shard_map/ppermute | solution.py:410
  9.0 1.9 %collective-permute-start.7 = (bf16[2,34,8,128]{3,2,1,0:T(8,128)(2,1)S(1)}, bf16[2,34,8,128]{3,2,1,0:T(8,128)(2,1)S(1)}, u32[]{:S(2)}, u32[]{:S(2)}) collective-permute-start(bf16[2,34,8,128]{3,2,1,0:T(8,128)(2,1)S(1)} %get-tuple-element.71), channel_id=1, source_target_pairs={{0,12},{1,5},{2,14},{3,7},{4,8},{5,1},{6,10},{7,3},{8,4},{9,13},{1... | collective-permute-start | bytes 417800 | tf_op jit(solution)/shard_map/ppermute | solution.py:410
  10.9 0.0 copy-done.13
  11.6 0.0 copy-start.4
  11.6 0.0 copy-start.5
  11.6 0.0 copy-start.6
  11.6 0.0 copy-done.2
  11.6 0.0 copy-done.3
  11.6 0.6 %copy-done.4 = f32[64]{0:T(128)S(1)} copy-done((f32[64]{0:T(128)S(1)}, f32[64]{0:T(128)}, u32[]{:S(2)}) %copy-start.4) | copy-done | bytes 280
  12.2 0.0 copy-done.5
  12.2 0.0 copy-done.6
  12.3 0.9 %prepare.1 = (bf16[1024,192]{1,0:T(8,128)(2,1)S(1)}, f32[64,128]{1,0:T(8,128)S(1)}, bf16[384,256]{1,0:T(8,128)(2,1)S(1)}, f32[64,128]{1,0:T(8,128)S(1)}, bf16[96...) custom-call(bf16[18,64]{1,0:T(8,128)(2,1)S(1)} %reshape.8.w_in_ref, f32[1,64]{1,0:T(1,128)S(1)} %bitcast.8, ...), custom_call_target="tpu_custom_call" | custom-call | flops 1000000000 | bytes 8000000 | tf_op jit(solution)/shard_map/prepare/pallas_call | solution.py:331
  13.1 0.0 copy-start.7
  13.2 0.7 %copy-done.7 = bf16[96,1152]{1,0:T(8,128)(2,1)} copy-done((bf16[96,1152]{1,0:T(8,128)(2,1)}, bf16[96,1152]{1,0:T(8,128)(2,1)S(1)}, u32[]{:S(2)}) %copy-start.7) | copy-done | bytes 221208
  13.8 0.7 %copy-done.9 = bf16[384,256]{1,0:T(8,128)(2,1)} copy-done((bf16[384,256]{1,0:T(8,128)(2,1)}, bf16[384,256]{1,0:T(8,128)(2,1)S(1)}, u32[]{:S(2)}) %copy-start.9) | copy-done | bytes 196632
  14.5 0.6 %copy-done.11 = f32[32,128]{1,0:T(8,128)} copy-done((f32[32,128]{1,0:T(8,128)}, f32[32,128]{1,0:T(8,128)S(1)}, u32[]{:S(2)}) %copy-start.11) | copy-done | bytes 16408
  15.1 0.8 %reshape.9 = s32[2,4,8]{2,1,0:T(4,128)S(1)} reshape(s32[64]{0:T(128)} %param.12) | data formatting | bytes 512 | tf_op jit(solution)/shard_map/reshape | solution.py:419
  15.9 0.0 collective-permute-done.1.two_ref
  15.9 4.6 %collective-permute-done.2.three_ref = bf16[2,34,8,128]{3,2,1,0:T(8,128)(2,1)S(1)} collective-permute-done((bf16[2,34,8,128]{3,2,1,0:T(8,128)(2,1)S(1)}, bf16[2,34,8,128]{3,2,1,0:T(8,128)(2,1)S(1)}, u32[]{:S(2)}, u32[]{:S(2)}) %collective-permute-start.2) | collective-permute-done | bytes 139296 | tf_op jit(solution)/shard_map/ppermute | solution.py:410
  20.4 0.0 collective-permute-done.one_ref
  20.5 0.1 broadcast_in_dim.17.offs_ref
  20.5 0.0 copy-done
  20.5 0.3 fold.2
  20.9 1.9 %collective-permute-start.3 = (f32[2,8,128]{2,1,0:T(8,128)S(1)}, f32[2,8,128]{2,1,0:T(8,128)S(1)}, u32[]{:S(2)}, u32[]{:S(2)}) collective-permute-start(f32[2,8,128]{2,1,0:T(8,128)S(1)} %get-tuple-element.67), channel_id=1, source_target_pairs={{0,12},{1,13},{2,14},{3,15},{4,8},{5,9},{6,10},{7,11},{8,4},{9,5},... | collective-permute-start | bytes 24584 | tf_op jit(solution)/shard_map/ppermute | solution.py:410
  22.8 6.0 %collective-permute-start.4 = (f32[2,8,128]{2,1,0:T(8,128)S(1)}, f32[2,8,128]{2,1,0:T(8,128)S(1)}, u32[]{:S(2)}, u32[]{:S(2)}) collective-permute-start(f32[2,8,128]{2,1,0:T(8,128)S(1)} %get-tuple-element.68), channel_id=1, source_target_pairs={{0,8},{1,9},{2,10},{3,11},{4,12},{5,13},{6,14},{7,15},{8,0},{9,1},... | collective-permute-start | bytes 24584 | tf_op jit(solution)/shard_map/ppermute | solution.py:410
  28.8 0.6 %collective-permute-start.5 = (f32[2,8,128]{2,1,0:T(8,128)S(1)}, f32[2,8,128]{2,1,0:T(8,128)S(1)}, u32[]{:S(2)}, u32[]{:S(2)}) collective-permute-start(f32[2,8,128]{2,1,0:T(8,128)S(1)} %get-tuple-element.69), channel_id=1, source_target_pairs={{0,4},{1,5},{2,6},{3,7},{4,0},{5,1},{6,2},{7,3},{8,12},{9,13},{10,... | collective-permute-start | bytes 24584 | tf_op jit(solution)/shard_map/ppermute | solution.py:410
  29.4 0.0 collective-permute-done.6.two_ref
  29.4 0.0 collective-permute-done.7.three_ref
  29.4 0.3 fold.3
  29.7 2.4 %collective-permute-start.8 = (f32[2,8,128]{2,1,0:T(8,128)S(1)}, f32[2,8,128]{2,1,0:T(8,128)S(1)}, u32[]{:S(2)}, u32[]{:S(2)}) collective-permute-start(f32[2,8,128]{2,1,0:T(8,128)S(1)} %get-tuple-element.74), channel_id=1, source_target_pairs={{0,12},{1,13},{2,14},{3,15},{4,8},{5,9},{6,10},{7,11},{8,4},{9,5},... | collective-permute-start | bytes 24584 | tf_op jit(solution)/shard_map/ppermute | solution.py:410
  32.1 0.7 %collective-permute-start.9 = (f32[2,8,128]{2,1,0:T(8,128)S(1)}, f32[2,8,128]{2,1,0:T(8,128)S(1)}, u32[]{:S(2)}, u32[]{:S(2)}) collective-permute-start(f32[2,8,128]{2,1,0:T(8,128)S(1)} %get-tuple-element.75), channel_id=1, source_target_pairs={{0,8},{1,9},{2,10},{3,11},{4,12},{5,13},{6,14},{7,15},{8,0},{9,1},... | collective-permute-start | bytes 24584 | tf_op jit(solution)/shard_map/ppermute | solution.py:410
  32.8 0.0 collective-permute-done.3.refs_9_
  32.8 1.4 %collective-permute-start.10 = (f32[2,8,128]{2,1,0:T(8,128)S(1)}, f32[2,8,128]{2,1,0:T(8,128)S(1)}, u32[]{:S(2)}, u32[]{:S(2)}) collective-permute-start(f32[2,8,128]{2,1,0:T(8,128)S(1)} %get-tuple-element.76), channel_id=1, source_target_pairs={{0,4},{1,5},{2,6},{3,7},{4,0},{5,1},{6,2},{7,3},{8,12},{9,13},{10,... | collective-permute-start | bytes 24584 | tf_op jit(solution)/shard_map/ppermute | solution.py:410
  34.2 0.0 collective-permute-done.4.refs_10_
  34.2 0.0 collective-permute-done.5.refs_11_
  34.2 0.0 copy-done.8
  34.2 0.0 copy-done.10
  34.2 0.0 copy-done.12
  34.2 1.5 %denoise_first.1 = (f32[2,32,128]{2,1,0:T(8,128)S(1)}, f32[2,8,128]{2,1,0:T(8,128)S(1)}, bf16[256,128]{1,0:T(8,128)(2,1)S(1)}, bf16[64,128]{1,0:T(8,128)(2,1)S(1)}) custom-call(f32[64,128]{1,0:T(8,128)S(1)} %get-tuple-element.55.refs_0_, f32[32,128]{1,0:T(8,128)S(1)} %copy-done.12, f32[1,2,64,128]{3,2,1,0:T(8,128)S(1)} %copy-done.1, ...), custom_call_target="tpu_custom_call" | custom-call | flops 2000000000 | bytes 2000000 | tf_op jit(solution)/shard_map/denoise_first/pallas_call | solution.py:262
  35.7 0.0 collective-permute-done.8.refs_9_
  35.7 1.0 %collective-permute-done.9.refs_10_ = f32[2,8,128]{2,1,0:T(8,128)S(1)} collective-permute-done((f32[2,8,128]{2,1,0:T(8,128)S(1)}, f32[2,8,128]{2,1,0:T(8,128)S(1)}, u32[]{:S(2)}, u32[]{:S(2)}) %collective-permute-start.9) | collective-permute-done | bytes 8224 | tf_op jit(solution)/shard_map/ppermute | solution.py:410
  36.7 0.0 collective-permute-done.10.refs_11_
  36.7 2.3 %denoise_rest.1 = f32[1,2,64,128]{3,2,1,0:T(8,128)} custom-call(f32[64,128]{1,0:T(8,128)S(1)} %get-tuple-element.55.refs_0_, f32[32,128]{1,0:T(8,128)S(1)} %copy-done.12, f32[1,2,64,128]{3,2,1,0:T(8,128)S(1)} %copy-done.1, bf16[1024,192]{1,0:T(8,128)(2,1)S(1)} %get-tuple-element.57.refs_3_, f32[64,128]{1,0:T(8,128)S(1)} %get-tuple-element.58.refs_4_, ...), custom_call_target="tpu_custom_call" | custom-call | flops 2000000000 | bytes 2000000 | tf_op jit(solution)/shard_map/denoise_rest/pallas_call | solution.py:262
  (12 shorter events, 0.0 us)
Async XLA Ops:
  0.0 11.6 %copy-start.2 = (bf16[64,64,3,3]{1,0,3,2:T(8,128)(2,1)S(1)}, bf16[64,64,3,3]{1,0,3,2:T(8,128)(2,1)}, u32[]{:S(2)}) copy-start(bf16[64,64,3,3]{1,0,3,2:T(8,128)(2,1)} %param.16) | copy-start | bytes 221188
  1.4 9.5 %copy-start.13 = (bf16[64,2,3,3]{0,1,3,2:T(2,128)(2,1)S(1)}, bf16[64,2,3,3]{0,1,3,2:T(2,128)(2,1)}, u32[]{:S(2)}) copy-start(bf16[64,2,3,3]{0,1,3,2:T(2,128)(2,1)} %param.14) | copy-start | bytes 6916
  1.4 19.1 %collective-permute-start = (bf16[2,34,16,128]{3,2,1,0:T(8,128)(2,1)S(1)}, bf16[2,34,16,128]{3,2,1,0:T(8,128)(2,1)S(1)}, u32[]{:S(2)}, u32[]{:S(2)}) collective-permute-start(bf16[2,34,16,128]{3,2,1,0:T(8,128)(2,1)S(1)} %get-tuple-element.45), channel_id=1, source_target_pairs={{0,4},{1,13},{2,6},{3,15},{4,0},{5,9},{6,2},{7,11},{8,12},{9,5},{1... | collective-permute-start | bytes 835592 | tf_op jit(solution)/shard_map/ppermute | solution.py:410
  4.5 11.4 %collective-permute-start.1 = (bf16[2,34,8,128]{3,2,1,0:T(8,128)(2,1)S(1)}, bf16[2,34,8,128]{3,2,1,0:T(8,128)(2,1)S(1)}, u32[]{:S(2)}, u32[]{:S(2)}) collective-permute-start(bf16[2,34,8,128]{3,2,1,0:T(8,128)(2,1)S(1)} %get-tuple-element.46), channel_id=1, source_target_pairs={{0,8},{1,9},{2,10},{3,11},{4,12},{5,13},{6,14},{7,15},{8,0},{9,1},... | collective-permute-start | bytes 417800 | tf_op jit(solution)/shard_map/ppermute | solution.py:410
  7.1 13.4 %collective-permute-start.2 = (bf16[2,34,8,128]{3,2,1,0:T(8,128)(2,1)S(1)}, bf16[2,34,8,128]{3,2,1,0:T(8,128)(2,1)S(1)}, u32[]{:S(2)}, u32[]{:S(2)}) collective-permute-start(bf16[2,34,8,128]{3,2,1,0:T(8,128)(2,1)S(1)} %get-tuple-element.47), channel_id=1, source_target_pairs={{0,12},{1,5},{2,14},{3,7},{4,8},{5,1},{6,10},{7,3},{8,4},{9,13},{1... | collective-permute-start | bytes 417800 | tf_op jit(solution)/shard_map/ppermute | solution.py:410
  7.1 22.3 %collective-permute-start.6 = (bf16[2,34,8,128]{3,2,1,0:T(8,128)(2,1)S(1)}, bf16[2,34,8,128]{3,2,1,0:T(8,128)(2,1)S(1)}, u32[]{:S(2)}, u32[]{:S(2)}) collective-permute-start(bf16[2,34,8,128]{3,2,1,0:T(8,128)(2,1)S(1)} %get-tuple-element.70), channel_id=1, source_target_pairs={{0,8},{1,9},{2,10},{3,11},{4,12},{5,13},{6,14},{7,15},{8,0},{9,1},... | collective-permute-start | bytes 417800 | tf_op jit(solution)/shard_map/ppermute | solution.py:410
  9.0 20.4 %collective-permute-start.7 = (bf16[2,34,8,128]{3,2,1,0:T(8,128)(2,1)S(1)}, bf16[2,34,8,128]{3,2,1,0:T(8,128)(2,1)S(1)}, u32[]{:S(2)}, u32[]{:S(2)}) collective-permute-start(bf16[2,34,8,128]{3,2,1,0:T(8,128)(2,1)S(1)} %get-tuple-element.71), channel_id=1, source_target_pairs={{0,12},{1,5},{2,14},{3,7},{4,8},{5,1},{6,10},{7,3},{8,4},{9,13},{1... | collective-permute-start | bytes 417800 | tf_op jit(solution)/shard_map/ppermute | solution.py:410
  10.9 0.7 %copy-start.3 = (bf16[2,64,3,3]{1,0,3,2:T(2,128)(2,1)S(1)}, bf16[2,64,3,3]{1,0,3,2:T(2,128)(2,1)}, u32[]{:S(2)}) copy-start(bf16[2,64,3,3]{1,0,3,2:T(2,128)(2,1)} %param.18) | copy-start | bytes 6916
  11.6 0.7 %copy-start.4 = (f32[64]{0:T(128)S(1)}, f32[64]{0:T(128)}, u32[]{:S(2)}) copy-start(f32[64]{0:T(128)} %param.15) | copy-start | bytes 772
  11.6 0.7 %copy-start.5 = (f32[64]{0:T(128)S(1)}, f32[64]{0:T(128)}, u32[]{:S(2)}) copy-start(f32[64]{0:T(128)} %param.17) | copy-start | bytes 772
  11.6 0.7 %copy-start.6 = (f32[2]{0:T(128)S(1)}, f32[2]{0:T(128)}, u32[]{:S(2)}) copy-start(f32[2]{0:T(128)} %b_out_ref.1) | copy-start | bytes 28
  12.3 8.3 %copy-start = (bf16[1,2,32,64,128]{4,3,2,1,0:T(8,128)(2,1)S(1)}, bf16[1,2,32,64,128]{4,3,2,1,0:T(8,128)(2,1)}, u32[]{:S(2)}) copy-start(bf16[1,2,32,64,128]{4,3,2,1,0:T(8,128)(2,1)} %maps_ref.5) | copy-start | bytes 3145732
  13.1 0.7 %copy-start.7 = (bf16[96,1152]{1,0:T(8,128)(2,1)}, bf16[96,1152]{1,0:T(8,128)(2,1)S(1)}, u32[]{:S(2)}) copy-start(bf16[96,1152]{1,0:T(8,128)(2,1)S(1)} %get-tuple-element.61.refs_7_) | copy-start | bytes 663556
  13.8 0.7 %copy-start.9 = (bf16[384,256]{1,0:T(8,128)(2,1)}, bf16[384,256]{1,0:T(8,128)(2,1)S(1)}, u32[]{:S(2)}) copy-start(bf16[384,256]{1,0:T(8,128)(2,1)S(1)} %get-tuple-element.59.refs_5_) | copy-start | bytes 589828
  14.5 0.6 %copy-start.11 = (f32[32,128]{1,0:T(8,128)}, f32[32,128]{1,0:T(8,128)S(1)}, u32[]{:S(2)}) copy-start(f32[32,128]{1,0:T(8,128)S(1)} %get-tuple-element.56.refs_1_) | copy-start | bytes 49156
  15.1 5.4 %copy-start.1 = (f32[1,2,64,128]{3,2,1,0:T(8,128)S(1)}, f32[1,2,64,128]{3,2,1,0:T(8,128)}, u32[]{:S(2)}) copy-start(f32[1,2,64,128]{3,2,1,0:T(8,128)} %refs_2_.3) | copy-start | bytes 196612
  20.9 11.9 %collective-permute-start.3 = (f32[2,8,128]{2,1,0:T(8,128)S(1)}, f32[2,8,128]{2,1,0:T(8,128)S(1)}, u32[]{:S(2)}, u32[]{:S(2)}) collective-permute-start(f32[2,8,128]{2,1,0:T(8,128)S(1)} %get-tuple-element.67), channel_id=1, source_target_pairs={{0,12},{1,13},{2,14},{3,15},{4,8},{5,9},{6,10},{7,11},{8,4},{9,5},... | collective-permute-start | bytes 24584 | tf_op jit(solution)/shard_map/ppermute | solution.py:410
  22.8 11.4 %collective-permute-start.4 = (f32[2,8,128]{2,1,0:T(8,128)S(1)}, f32[2,8,128]{2,1,0:T(8,128)S(1)}, u32[]{:S(2)}, u32[]{:S(2)}) collective-permute-start(f32[2,8,128]{2,1,0:T(8,128)S(1)} %get-tuple-element.68), channel_id=1, source_target_pairs={{0,8},{1,9},{2,10},{3,11},{4,12},{5,13},{6,14},{7,15},{8,0},{9,1},... | collective-permute-start | bytes 24584 | tf_op jit(solution)/shard_map/ppermute | solution.py:410
  28.8 5.4 %copy-start.8 = (bf16[96,1152]{1,0:T(8,128)(2,1)S(1)}, bf16[96,1152]{1,0:T(8,128)(2,1)}, u32[]{:S(2)}) copy-start(bf16[96,1152]{1,0:T(8,128)(2,1)} %copy-done.7) | copy-start | bytes 663556
  28.8 5.4 %copy-start.10 = (bf16[384,256]{1,0:T(8,128)(2,1)S(1)}, bf16[384,256]{1,0:T(8,128)(2,1)}, u32[]{:S(2)}) copy-start(bf16[384,256]{1,0:T(8,128)(2,1)} %copy-done.9) | copy-start | bytes 589828
  28.8 5.4 %copy-start.12 = (f32[32,128]{1,0:T(8,128)S(1)}, f32[32,128]{1,0:T(8,128)}, u32[]{:S(2)}) copy-start(f32[32,128]{1,0:T(8,128)} %copy-done.11) | copy-start | bytes 49156
  28.8 5.4 %collective-permute-start.5 = (f32[2,8,128]{2,1,0:T(8,128)S(1)}, f32[2,8,128]{2,1,0:T(8,128)S(1)}, u32[]{:S(2)}, u32[]{:S(2)}) collective-permute-start(f32[2,8,128]{2,1,0:T(8,128)S(1)} %get-tuple-element.69), channel_id=1, source_target_pairs={{0,4},{1,5},{2,6},{3,7},{4,0},{5,1},{6,2},{7,3},{8,12},{9,13},{10,... | collective-permute-start | bytes 24584 | tf_op jit(solution)/shard_map/ppermute | solution.py:410
  29.7 6.0 %collective-permute-start.8 = (f32[2,8,128]{2,1,0:T(8,128)S(1)}, f32[2,8,128]{2,1,0:T(8,128)S(1)}, u32[]{:S(2)}, u32[]{:S(2)}) collective-permute-start(f32[2,8,128]{2,1,0:T(8,128)S(1)} %get-tuple-element.74), channel_id=1, source_target_pairs={{0,12},{1,13},{2,14},{3,15},{4,8},{5,9},{6,10},{7,11},{8,4},{9,5},... | collective-permute-start | bytes 24584 | tf_op jit(solution)/shard_map/ppermute | solution.py:410
  32.1 4.5 %collective-permute-start.9 = (f32[2,8,128]{2,1,0:T(8,128)S(1)}, f32[2,8,128]{2,1,0:T(8,128)S(1)}, u32[]{:S(2)}, u32[]{:S(2)}) collective-permute-start(f32[2,8,128]{2,1,0:T(8,128)S(1)} %get-tuple-element.75), channel_id=1, source_target_pairs={{0,8},{1,9},{2,10},{3,11},{4,12},{5,13},{6,14},{7,15},{8,0},{9,1},... | collective-permute-start | bytes 24584 | tf_op jit(solution)/shard_map/ppermute | solution.py:410
  32.8 3.9 %collective-permute-start.10 = (f32[2,8,128]{2,1,0:T(8,128)S(1)}, f32[2,8,128]{2,1,0:T(8,128)S(1)}, u32[]{:S(2)}, u32[]{:S(2)}) collective-permute-start(f32[2,8,128]{2,1,0:T(8,128)S(1)} %get-tuple-element.76), channel_id=1, source_target_pairs={{0,4},{1,5},{2,6},{3,7},{4,0},{5,1},{6,2},{7,3},{8,12},{9,13},{10,... | collective-permute-start | bytes 24584 | tf_op jit(solution)/shard_map/ppermute | solution.py:410

commit v6 on v5

--- a/solution.py
+++ b/solution.py
@@ -181,12 +181,12 @@
             w1_ref[(GROUP - 1) * ch :, :], low[:, g * z : (g + 1) * z], preferred_element_type=jnp.float32
         )
         hidden_one[block(half - 1)] = jnp.maximum(out + bias, 0.0).astype(jnp.bfloat16)
-    for r in range(0, GROUP, QUAD):
+    for r in range(0, GROUP, 8):
         for g in range(begin // GROUP, end // GROUP, 2):
             out = jnp.dot(
-                w1_ref[r * ch : (r + QUAD) * ch, :], low[:, g * z : (g + 2) * z], preferred_element_type=jnp.float32
+                w1_ref[r * ch : (r + 8) * ch, :], low[:, g * z : (g + 2) * z], preferred_element_type=jnp.float32
             )
-            for i in range(QUAD):
+            for i in range(8):
                 for j in range(2):
                     value = jnp.maximum(out[i * ch : (i + 1) * ch, j * z : (j + 1) * z] + bias, 0.0)
                     hidden_one[block((g + j) * GROUP + r + i)] = value.astype(jnp.bfloat16)
@@ -194,15 +194,16 @@
     bias = b2_ref[...]
     lane = lax.broadcasted_iota(jnp.int32, (ch, z), 1)
     start = 0 if chunk == 0 else cut
-    stride = (end - start) // 2
+    spread = 8 if chunk == 0 else 6
+    stride = (end - start) // spread
     for q in range(start, start + stride, PAIR):
         out = jnp.dot(
             w2_ref[...],
-            jnp.concatenate([hidden_one[block(q - 1, PAIR + 2)], hidden_one[block(q + stride - 1, PAIR + 2)]], axis=1),
+            jnp.concatenate([hidden_one[block(q + j * stride - 1, PAIR + 2)] for j in range(spread)], axis=1),
             preferred_element_type=jnp.float32,
         )
         for i in range(PAIR):
-            for j in range(2):
+            for j in range(spread):
                 total = bias
                 for tap in range(3):
                     at = (tap * PAIR + i) * ch

time: 39.1 us -> 39.1 us (level)
  no operation moved by 1% of the time
where the time goes in v6:
time: 39.1 us; the launch traced here: 38.9 us
  starting transfers between devices  22.5 us (58%)
  Pallas kernels  6.56 us (17%)
  waiting for transfers between devices  5.54 us (14%)
  local copies, waits for them, and re-layouts  3.5 us (9%)
  between operations  0.81 us (2%)
    ppermute x11, starting transfers between devices, trade(): return lax.ppermute(value, 'gy', pairs)  22.5 us
    ppermute x11, waiting for transfers between devices, trade(): return lax.ppermute(value, 'gy', pairs)  5.54 us
    pallas_call x2, Pallas kernels, denoise(): pl.pallas_call(functools.partial(denoise_kernel, stride, chunk), in_specs...  3.65 us
    unnamed x28, local copies, waits for them, and re-layouts  2.63 us
    pallas_call x1, Pallas kernels, pack(): pl.pallas_call(functools.partial(pack_kernel, stride), in_specs=[HBM, HBM...  1.35 us
    pallas_call x1, Pallas kernels, prepare(): pl.pallas_call(prepare_kernel, in_specs=[VMEM] * 5 + [SMEM] * 2, out_spec...  0.87 us
  transfers between devices with their start and end apart: 11, of which 2 were waited for; matrix products, arithmetic and copies ran while one was open for 2% of the time, Pallas kernels for 8%

profile of v6, /device:TPU:0, one launch (start us, length us, event | category | flops | bytes accessed | tf_op | source)
XLA Modules:
  0.0 38.9 jit_solution(6433378138944905838)
XLA Ops:
  0.0 1.4 %pack.1 = (bf16[2,34,16,128]{3,2,1,0:T(8,128)(2,1)S(1)}, bf16[2,34,8,128]{3,2,1,0:T(8,128)(2,1)S(1)}, bf16[2,34,8,128]{3,2,1,0:T(8,128)(2,1)S(1)}, bf16[2,34,8,1...) custom-call(bf16[1,2,32,64,128]{4,3,2,1,0:T(8,128)(2,1)} %maps_ref.5, f32[1,2,64,128]{3,2,1,0:T(8,128)} %refs_2_.3), custom_call_target="tpu_custom_call" | custom-call | bytes 2000000 | tf_op jit(solution)/shard_map/pack/pallas_call | solution.py:386
  1.4 0.0 copy-start.13
  1.4 3.1 %collective-permute-start = (bf16[2,34,16,128]{3,2,1,0:T(8,128)(2,1)S(1)}, bf16[2,34,16,128]{3,2,1,0:T(8,128)(2,1)S(1)}, u32[]{:S(2)}, u32[]{:S(2)}) collective-permute-start(bf16[2,34,16,128]{3,2,1,0:T(8,128)(2,1)S(1)} %get-tuple-element.45), channel_id=1, source_target_pairs={{0,4},{1,13},{2,6},{3,15},{4,0},{5,9},{6,2},{7,11},{8,12},{9,5},{1... | collective-permute-start | bytes 835592 | tf_op jit(solution)/shard_map/ppermute | solution.py:411
  4.5 2.6 %collective-permute-start.1 = (bf16[2,34,8,128]{3,2,1,0:T(8,128)(2,1)S(1)}, bf16[2,34,8,128]{3,2,1,0:T(8,128)(2,1)S(1)}, u32[]{:S(2)}, u32[]{:S(2)}) collective-permute-start(bf16[2,34,8,128]{3,2,1,0:T(8,128)(2,1)S(1)} %get-tuple-element.46), channel_id=1, source_target_pairs={{0,8},{1,9},{2,10},{3,11},{4,12},{5,13},{6,14},{7,15},{8,0},{9,1},... | collective-permute-start | bytes 417800 | tf_op jit(solution)/shard_map/ppermute | solution.py:411
  7.1 0.0 collective-permute-start.2
  7.1 1.9 %collective-permute-start.6 = (bf16[2,34,8,128]{3,2,1,0:T(8,128)(2,1)S(1)}, bf16[2,34,8,128]{3,2,1,0:T(8,128)(2,1)S(1)}, u32[]{:S(2)}, u32[]{:S(2)}) collective-permute-start(bf16[2,34,8,128]{3,2,1,0:T(8,128)(2,1)S(1)} %get-tuple-element.70), channel_id=1, source_target_pairs={{0,8},{1,9},{2,10},{3,11},{4,12},{5,13},{6,14},{7,15},{8,0},{9,1},... | collective-permute-start | bytes 417800 | tf_op jit(solution)/shard_map/ppermute | solution.py:411
  9.0 1.9 %collective-permute-start.7 = (bf16[2,34,8,128]{3,2,1,0:T(8,128)(2,1)S(1)}, bf16[2,34,8,128]{3,2,1,0:T(8,128)(2,1)S(1)}, u32[]{:S(2)}, u32[]{:S(2)}) collective-permute-start(bf16[2,34,8,128]{3,2,1,0:T(8,128)(2,1)S(1)} %get-tuple-element.71), channel_id=1, source_target_pairs={{0,12},{1,5},{2,14},{3,7},{4,8},{5,1},{6,10},{7,3},{8,4},{9,13},{1... | collective-permute-start | bytes 417800 | tf_op jit(solution)/shard_map/ppermute | solution.py:411
  10.9 0.0 copy-done.13
  11.6 0.0 copy-start.4
  11.6 0.0 copy-start.5
  11.6 0.0 copy-start.6
  11.6 0.0 copy-done.2
  11.6 0.0 copy-done.3
  11.6 0.6 %copy-done.4 = f32[64]{0:T(128)S(1)} copy-done((f32[64]{0:T(128)S(1)}, f32[64]{0:T(128)}, u32[]{:S(2)}) %copy-start.4) | copy-done | bytes 280
  12.2 0.0 copy-done.5
  12.2 0.0 copy-done.6
  12.3 0.9 %prepare.1 = (bf16[1024,192]{1,0:T(8,128)(2,1)S(1)}, f32[64,128]{1,0:T(8,128)S(1)}, bf16[384,256]{1,0:T(8,128)(2,1)S(1)}, f32[64,128]{1,0:T(8,128)S(1)}, bf16[96...) custom-call(bf16[18,64]{1,0:T(8,128)(2,1)S(1)} %reshape.8.w_in_ref, f32[1,64]{1,0:T(1,128)S(1)} %bitcast.8, ...), custom_call_target="tpu_custom_call" | custom-call | flops 1000000000 | bytes 8000000 | tf_op jit(solution)/shard_map/prepare/pallas_call | solution.py:332
  13.1 0.0 copy-start.7
  13.2 0.7 %copy-done.7 = bf16[96,1152]{1,0:T(8,128)(2,1)} copy-done((bf16[96,1152]{1,0:T(8,128)(2,1)}, bf16[96,1152]{1,0:T(8,128)(2,1)S(1)}, u32[]{:S(2)}) %copy-start.7) | copy-done | bytes 221208
  13.8 0.7 %copy-done.9 = bf16[384,256]{1,0:T(8,128)(2,1)} copy-done((bf16[384,256]{1,0:T(8,128)(2,1)}, bf16[384,256]{1,0:T(8,128)(2,1)S(1)}, u32[]{:S(2)}) %copy-start.9) | copy-done | bytes 196632
  14.5 0.6 %copy-done.11 = f32[32,128]{1,0:T(8,128)} copy-done((f32[32,128]{1,0:T(8,128)}, f32[32,128]{1,0:T(8,128)S(1)}, u32[]{:S(2)}) %copy-start.11) | copy-done | bytes 16408
  15.1 0.8 %reshape.9 = s32[2,4,8]{2,1,0:T(4,128)S(1)} reshape(s32[64]{0:T(128)} %param.12) | data formatting | bytes 512 | tf_op jit(solution)/shard_map/reshape | solution.py:420
  15.9 0.0 collective-permute-done.1.two_ref
  15.9 4.6 %collective-permute-done.2.three_ref = bf16[2,34,8,128]{3,2,1,0:T(8,128)(2,1)S(1)} collective-permute-done((bf16[2,34,8,128]{3,2,1,0:T(8,128)(2,1)S(1)}, bf16[2,34,8,128]{3,2,1,0:T(8,128)(2,1)S(1)}, u32[]{:S(2)}, u32[]{:S(2)}) %collective-permute-start.2) | collective-permute-done | bytes 139296 | tf_op jit(solution)/shard_map/ppermute | solution.py:411
  20.4 0.0 collective-permute-done.one_ref
  20.5 0.1 broadcast_in_dim.17.offs_ref
  20.5 0.0 copy-done
  20.5 0.0 copy-done.1
  20.5 0.3 fold.2
  20.9 1.9 %collective-permute-start.3 = (f32[2,8,128]{2,1,0:T(8,128)S(1)}, f32[2,8,128]{2,1,0:T(8,128)S(1)}, u32[]{:S(2)}, u32[]{:S(2)}) collective-permute-start(f32[2,8,128]{2,1,0:T(8,128)S(1)} %get-tuple-element.67), channel_id=1, source_target_pairs={{0,12},{1,13},{2,14},{3,15},{4,8},{5,9},{6,10},{7,11},{8,4},{9,5},... | collective-permute-start | bytes 24584 | tf_op jit(solution)/shard_map/ppermute | solution.py:411
  22.8 6.0 %collective-permute-start.4 = (f32[2,8,128]{2,1,0:T(8,128)S(1)}, f32[2,8,128]{2,1,0:T(8,128)S(1)}, u32[]{:S(2)}, u32[]{:S(2)}) collective-permute-start(f32[2,8,128]{2,1,0:T(8,128)S(1)} %get-tuple-element.68), channel_id=1, source_target_pairs={{0,8},{1,9},{2,10},{3,11},{4,12},{5,13},{6,14},{7,15},{8,0},{9,1},... | collective-permute-start | bytes 24584 | tf_op jit(solution)/shard_map/ppermute | solution.py:411
  28.8 0.6 %collective-permute-start.5 = (f32[2,8,128]{2,1,0:T(8,128)S(1)}, f32[2,8,128]{2,1,0:T(8,128)S(1)}, u32[]{:S(2)}, u32[]{:S(2)}) collective-permute-start(f32[2,8,128]{2,1,0:T(8,128)S(1)} %get-tuple-element.69), channel_id=1, source_target_pairs={{0,4},{1,5},{2,6},{3,7},{4,0},{5,1},{6,2},{7,3},{8,12},{9,13},{10,... | collective-permute-start | bytes 24584 | tf_op jit(solution)/shard_map/ppermute | solution.py:411
  29.4 0.0 collective-permute-done.6.two_ref
  29.4 0.0 collective-permute-done.7.three_ref
  29.4 0.3 fold.3
  29.7 2.4 %collective-permute-start.8 = (f32[2,8,128]{2,1,0:T(8,128)S(1)}, f32[2,8,128]{2,1,0:T(8,128)S(1)}, u32[]{:S(2)}, u32[]{:S(2)}) collective-permute-start(f32[2,8,128]{2,1,0:T(8,128)S(1)} %get-tuple-element.74), channel_id=1, source_target_pairs={{0,12},{1,13},{2,14},{3,15},{4,8},{5,9},{6,10},{7,11},{8,4},{9,5},... | collective-permute-start | bytes 24584 | tf_op jit(solution)/shard_map/ppermute | solution.py:411
  32.1 0.7 %collective-permute-start.9 = (f32[2,8,128]{2,1,0:T(8,128)S(1)}, f32[2,8,128]{2,1,0:T(8,128)S(1)}, u32[]{:S(2)}, u32[]{:S(2)}) collective-permute-start(f32[2,8,128]{2,1,0:T(8,128)S(1)} %get-tuple-element.75), channel_id=1, source_target_pairs={{0,8},{1,9},{2,10},{3,11},{4,12},{5,13},{6,14},{7,15},{8,0},{9,1},... | collective-permute-start | bytes 24584 | tf_op jit(solution)/shard_map/ppermute | solution.py:411
  32.8 0.0 collective-permute-done.3.refs_9_
  32.8 1.4 %collective-permute-start.10 = (f32[2,8,128]{2,1,0:T(8,128)S(1)}, f32[2,8,128]{2,1,0:T(8,128)S(1)}, u32[]{:S(2)}, u32[]{:S(2)}) collective-permute-start(f32[2,8,128]{2,1,0:T(8,128)S(1)} %get-tuple-element.76), channel_id=1, source_target_pairs={{0,4},{1,5},{2,6},{3,7},{4,0},{5,1},{6,2},{7,3},{8,12},{9,13},{10,... | collective-permute-start | bytes 24584 | tf_op jit(solution)/shard_map/ppermute | solution.py:411
  34.2 0.0 collective-permute-done.4.refs_10_
  34.2 0.0 collective-permute-done.5.refs_11_
  34.2 0.0 copy-done.8
  34.2 0.0 copy-done.10
  34.2 1.5 %denoise_first.1 = (f32[2,32,128]{2,1,0:T(8,128)S(1)}, f32[2,8,128]{2,1,0:T(8,128)S(1)}, bf16[256,128]{1,0:T(8,128)(2,1)S(1)}, bf16[64,128]{1,0:T(8,128)(2,1)S(1)}) custom-call(f32[64,128]{1,0:T(8,128)S(1)} %get-tuple-element.55.refs_0_, f32[32,128]{1,0:T(8,128)S(1)} %copy-done.12, f32[1,2,64,128]{3,2,1,0:T(8,128)S(1)} %copy-done.1, ...), custom_call_target="tpu_custom_call" | custom-call | flops 2000000000 | bytes 2000000 | tf_op jit(solution)/shard_map/denoise_first/pallas_call | solution.py:263
  35.7 0.0 collective-permute-done.8.refs_9_
  35.7 1.0 %collective-permute-done.9.refs_10_ = f32[2,8,128]{2,1,0:T(8,128)S(1)} collective-permute-done((f32[2,8,128]{2,1,0:T(8,128)S(1)}, f32[2,8,128]{2,1,0:T(8,128)S(1)}, u32[]{:S(2)}, u32[]{:S(2)}) %collective-permute-start.9) | collective-permute-done | bytes 8224 | tf_op jit(solution)/shard_map/ppermute | solution.py:411
  36.7 0.0 collective-permute-done.10.refs_11_
  36.7 2.2 %denoise_rest.1 = f32[1,2,64,128]{3,2,1,0:T(8,128)} custom-call(f32[64,128]{1,0:T(8,128)S(1)} %get-tuple-element.55.refs_0_, f32[32,128]{1,0:T(8,128)S(1)} %copy-done.12, f32[1,2,64,128]{3,2,1,0:T(8,128)S(1)} %copy-done.1, bf16[1024,192]{1,0:T(8,128)(2,1)S(1)} %get-tuple-element.57.refs_3_, f32[64,128]{1,0:T(8,128)S(1)} %get-tuple-element.58.refs_4_, ...), custom_call_target="tpu_custom_call" | custom-call | flops 2000000000 | bytes 2000000 | tf_op jit(solution)/shard_map/denoise_rest/pallas_call | solution.py:263
  (12 shorter events, 0.0 us)
Async XLA Ops:
  0.0 11.6 %copy-start.2 = (bf16[64,64,3,3]{1,0,3,2:T(8,128)(2,1)S(1)}, bf16[64,64,3,3]{1,0,3,2:T(8,128)(2,1)}, u32[]{:S(2)}) copy-start(bf16[64,64,3,3]{1,0,3,2:T(8,128)(2,1)} %param.16) | copy-start | bytes 221188
  1.4 9.5 %copy-start.13 = (bf16[64,2,3,3]{0,1,3,2:T(2,128)(2,1)S(1)}, bf16[64,2,3,3]{0,1,3,2:T(2,128)(2,1)}, u32[]{:S(2)}) copy-start(bf16[64,2,3,3]{0,1,3,2:T(2,128)(2,1)} %param.14) | copy-start | bytes 6916
  1.4 19.1 %collective-permute-start = (bf16[2,34,16,128]{3,2,1,0:T(8,128)(2,1)S(1)}, bf16[2,34,16,128]{3,2,1,0:T(8,128)(2,1)S(1)}, u32[]{:S(2)}, u32[]{:S(2)}) collective-permute-start(bf16[2,34,16,128]{3,2,1,0:T(8,128)(2,1)S(1)} %get-tuple-element.45), channel_id=1, source_target_pairs={{0,4},{1,13},{2,6},{3,15},{4,0},{5,9},{6,2},{7,11},{8,12},{9,5},{1... | collective-permute-start | bytes 835592 | tf_op jit(solution)/shard_map/ppermute | solution.py:411
  4.5 11.4 %collective-permute-start.1 = (bf16[2,34,8,128]{3,2,1,0:T(8,128)(2,1)S(1)}, bf16[2,34,8,128]{3,2,1,0:T(8,128)(2,1)S(1)}, u32[]{:S(2)}, u32[]{:S(2)}) collective-permute-start(bf16[2,34,8,128]{3,2,1,0:T(8,128)(2,1)S(1)} %get-tuple-element.46), channel_id=1, source_target_pairs={{0,8},{1,9},{2,10},{3,11},{4,12},{5,13},{6,14},{7,15},{8,0},{9,1},... | collective-permute-start | bytes 417800 | tf_op jit(solution)/shard_map/ppermute | solution.py:411
  7.1 13.4 %collective-permute-start.2 = (bf16[2,34,8,128]{3,2,1,0:T(8,128)(2,1)S(1)}, bf16[2,34,8,128]{3,2,1,0:T(8,128)(2,1)S(1)}, u32[]{:S(2)}, u32[]{:S(2)}) collective-permute-start(bf16[2,34,8,128]{3,2,1,0:T(8,128)(2,1)S(1)} %get-tuple-element.47), channel_id=1, source_target_pairs={{0,12},{1,5},{2,14},{3,7},{4,8},{5,1},{6,10},{7,3},{8,4},{9,13},{1... | collective-permute-start | bytes 417800 | tf_op jit(solution)/shard_map/ppermute | solution.py:411
  7.1 22.3 %collective-permute-start.6 = (bf16[2,34,8,128]{3,2,1,0:T(8,128)(2,1)S(1)}, bf16[2,34,8,128]{3,2,1,0:T(8,128)(2,1)S(1)}, u32[]{:S(2)}, u32[]{:S(2)}) collective-permute-start(bf16[2,34,8,128]{3,2,1,0:T(8,128)(2,1)S(1)} %get-tuple-element.70), channel_id=1, source_target_pairs={{0,8},{1,9},{2,10},{3,11},{4,12},{5,13},{6,14},{7,15},{8,0},{9,1},... | collective-permute-start | bytes 417800 | tf_op jit(solution)/shard_map/ppermute | solution.py:411
  9.0 20.4 %collective-permute-start.7 = (bf16[2,34,8,128]{3,2,1,0:T(8,128)(2,1)S(1)}, bf16[2,34,8,128]{3,2,1,0:T(8,128)(2,1)S(1)}, u32[]{:S(2)}, u32[]{:S(2)}) collective-permute-start(bf16[2,34,8,128]{3,2,1,0:T(8,128)(2,1)S(1)} %get-tuple-element.71), channel_id=1, source_target_pairs={{0,12},{1,5},{2,14},{3,7},{4,8},{5,1},{6,10},{7,3},{8,4},{9,13},{1... | collective-permute-start | bytes 417800 | tf_op jit(solution)/shard_map/ppermute | solution.py:411
  10.9 0.7 %copy-start.3 = (bf16[2,64,3,3]{1,0,3,2:T(2,128)(2,1)S(1)}, bf16[2,64,3,3]{1,0,3,2:T(2,128)(2,1)}, u32[]{:S(2)}) copy-start(bf16[2,64,3,3]{1,0,3,2:T(2,128)(2,1)} %param.18) | copy-start | bytes 6916
  11.6 0.7 %copy-start.4 = (f32[64]{0:T(128)S(1)}, f32[64]{0:T(128)}, u32[]{:S(2)}) copy-start(f32[64]{0:T(128)} %param.15) | copy-start | bytes 772
  11.6 0.7 %copy-start.5 = (f32[64]{0:T(128)S(1)}, f32[64]{0:T(128)}, u32[]{:S(2)}) copy-start(f32[64]{0:T(128)} %param.17) | copy-start | bytes 772
  11.6 0.7 %copy-start.6 = (f32[2]{0:T(128)S(1)}, f32[2]{0:T(128)}, u32[]{:S(2)}) copy-start(f32[2]{0:T(128)} %b_out_ref.1) | copy-start | bytes 28
  12.3 8.3 %copy-start = (bf16[1,2,32,64,128]{4,3,2,1,0:T(8,128)(2,1)S(1)}, bf16[1,2,32,64,128]{4,3,2,1,0:T(8,128)(2,1)}, u32[]{:S(2)}) copy-start(bf16[1,2,32,64,128]{4,3,2,1,0:T(8,128)(2,1)} %maps_ref.5) | copy-start | bytes 3145732
  13.1 0.7 %copy-start.7 = (bf16[96,1152]{1,0:T(8,128)(2,1)}, bf16[96,1152]{1,0:T(8,128)(2,1)S(1)}, u32[]{:S(2)}) copy-start(bf16[96,1152]{1,0:T(8,128)(2,1)S(1)} %get-tuple-element.61.refs_7_) | copy-start | bytes 663556
  13.8 0.7 %copy-start.9 = (bf16[384,256]{1,0:T(8,128)(2,1)}, bf16[384,256]{1,0:T(8,128)(2,1)S(1)}, u32[]{:S(2)}) copy-start(bf16[384,256]{1,0:T(8,128)(2,1)S(1)} %get-tuple-element.59.refs_5_) | copy-start | bytes 589828
  14.5 0.6 %copy-start.11 = (f32[32,128]{1,0:T(8,128)}, f32[32,128]{1,0:T(8,128)S(1)}, u32[]{:S(2)}) copy-start(f32[32,128]{1,0:T(8,128)S(1)} %get-tuple-element.56.refs_1_) | copy-start | bytes 49156
  15.1 5.4 %copy-start.1 = (f32[1,2,64,128]{3,2,1,0:T(8,128)S(1)}, f32[1,2,64,128]{3,2,1,0:T(8,128)}, u32[]{:S(2)}) copy-start(f32[1,2,64,128]{3,2,1,0:T(8,128)} %refs_2_.3) | copy-start | bytes 196612
  20.9 11.9 %collective-permute-start.3 = (f32[2,8,128]{2,1,0:T(8,128)S(1)}, f32[2,8,128]{2,1,0:T(8,128)S(1)}, u32[]{:S(2)}, u32[]{:S(2)}) collective-permute-start(f32[2,8,128]{2,1,0:T(8,128)S(1)} %get-tuple-element.67), channel_id=1, source_target_pairs={{0,12},{1,13},{2,14},{3,15},{4,8},{5,9},{6,10},{7,11},{8,4},{9,5},... | collective-permute-start | bytes 24584 | tf_op jit(solution)/shard_map/ppermute | solution.py:411
  22.8 11.4 %collective-permute-start.4 = (f32[2,8,128]{2,1,0:T(8,128)S(1)}, f32[2,8,128]{2,1,0:T(8,128)S(1)}, u32[]{:S(2)}, u32[]{:S(2)}) collective-permute-start(f32[2,8,128]{2,1,0:T(8,128)S(1)} %get-tuple-element.68), channel_id=1, source_target_pairs={{0,8},{1,9},{2,10},{3,11},{4,12},{5,13},{6,14},{7,15},{8,0},{9,1},... | collective-permute-start | bytes 24584 | tf_op jit(solution)/shard_map/ppermute | solution.py:411
  28.8 5.4 %copy-start.8 = (bf16[96,1152]{1,0:T(8,128)(2,1)S(1)}, bf16[96,1152]{1,0:T(8,128)(2,1)}, u32[]{:S(2)}) copy-start(bf16[96,1152]{1,0:T(8,128)(2,1)} %copy-done.7) | copy-start | bytes 663556
  28.8 5.4 %copy-start.10 = (bf16[384,256]{1,0:T(8,128)(2,1)S(1)}, bf16[384,256]{1,0:T(8,128)(2,1)}, u32[]{:S(2)}) copy-start(bf16[384,256]{1,0:T(8,128)(2,1)} %copy-done.9) | copy-start | bytes 589828
  28.8 5.4 %copy-start.12 = (f32[32,128]{1,0:T(8,128)S(1)}, f32[32,128]{1,0:T(8,128)}, u32[]{:S(2)}) copy-start(f32[32,128]{1,0:T(8,128)} %copy-done.11) | copy-start | bytes 49156
  28.8 5.4 %collective-permute-start.5 = (f32[2,8,128]{2,1,0:T(8,128)S(1)}, f32[2,8,128]{2,1,0:T(8,128)S(1)}, u32[]{:S(2)}, u32[]{:S(2)}) collective-permute-start(f32[2,8,128]{2,1,0:T(8,128)S(1)} %get-tuple-element.69), channel_id=1, source_target_pairs={{0,4},{1,5},{2,6},{3,7},{4,0},{5,1},{6,2},{7,3},{8,12},{9,13},{10,... | collective-permute-start | bytes 24584 | tf_op jit(solution)/shard_map/ppermute | solution.py:411
  29.7 6.0 %collective-permute-start.8 = (f32[2,8,128]{2,1,0:T(8,128)S(1)}, f32[2,8,128]{2,1,0:T(8,128)S(1)}, u32[]{:S(2)}, u32[]{:S(2)}) collective-permute-start(f32[2,8,128]{2,1,0:T(8,128)S(1)} %get-tuple-element.74), channel_id=1, source_target_pairs={{0,12},{1,13},{2,14},{3,15},{4,8},{5,9},{6,10},{7,11},{8,4},{9,5},... | collective-permute-start | bytes 24584 | tf_op jit(solution)/shard_map/ppermute | solution.py:411
  32.1 4.5 %collective-permute-start.9 = (f32[2,8,128]{2,1,0:T(8,128)S(1)}, f32[2,8,128]{2,1,0:T(8,128)S(1)}, u32[]{:S(2)}, u32[]{:S(2)}) collective-permute-start(f32[2,8,128]{2,1,0:T(8,128)S(1)} %get-tuple-element.75), channel_id=1, source_target_pairs={{0,8},{1,9},{2,10},{3,11},{4,12},{5,13},{6,14},{7,15},{8,0},{9,1},... | collective-permute-start | bytes 24584 | tf_op jit(solution)/shard_map/ppermute | solution.py:411
  32.8 3.9 %collective-permute-start.10 = (f32[2,8,128]{2,1,0:T(8,128)S(1)}, f32[2,8,128]{2,1,0:T(8,128)S(1)}, u32[]{:S(2)}, u32[]{:S(2)}) collective-permute-start(f32[2,8,128]{2,1,0:T(8,128)S(1)} %get-tuple-element.76), channel_id=1, source_target_pairs={{0,4},{1,5},{2,6},{3,7},{4,0},{5,1},{6,2},{7,3},{8,12},{9,13},{10,... | collective-permute-start | bytes 24584 | tf_op jit(solution)/shard_map/ppermute | solution.py:411

commit v7 on v5

--- a/solution.py
+++ b/solution.py
@@ -12,7 +12,7 @@
 QUAD = 4
 PAIR = 2
 PAD = 8
-ORDERS = ((1, 2, 3), (3, 2, 1))
+ORDERS = ((1, 2, 3), (3, 1, 2))
 BACK = (3, 2, 1)
 PACK_LIMIT = 8 << 20
 CHUNKS = 2

time: 39.1 us -> 39.1 us (level)
  no operation moved by 1% of the time
where the time goes in v7:
time: 39.1 us; the launch traced here: 38.9 us
  starting transfers between devices  22.4 us (57%)
  Pallas kernels  6.64 us (17%)
  waiting for transfers between devices  5.58 us (14%)
  local copies, waits for them, and re-layouts  3.5 us (9%)
  between operations  0.81 us (2%)
    ppermute x11, starting transfers between devices, trade(): return lax.ppermute(value, 'gy', pairs)  22.4 us
    ppermute x11, waiting for transfers between devices, trade(): return lax.ppermute(value, 'gy', pairs)  5.58 us
    pallas_call x2, Pallas kernels, denoise(): pl.pallas_call(functools.partial(denoise_kernel, stride, chunk), in_specs...  3.73 us
    unnamed x28, local copies, waits for them, and re-layouts  2.63 us
    pallas_call x1, Pallas kernels, pack(): pl.pallas_call(functools.partial(pack_kernel, stride), in_specs=[HBM, HBM...  1.35 us
    pallas_call x1, Pallas kernels, prepare(): pl.pallas_call(prepare_kernel, in_specs=[VMEM] * 5 + [SMEM] * 2, out_spec...  0.87 us
  transfers between devices with their start and end apart: 11, of which 2 were waited for; matrix products, arithmetic and copies ran while one was open for 2% of the time, Pallas kernels for 8%

profile of v7, /device:TPU:0, one launch (start us, length us, event | category | flops | bytes accessed | tf_op | source)
XLA Modules:
  0.0 38.9 jit_solution(12252225930021392287)
XLA Ops:
  0.0 1.4 %pack.1 = (bf16[2,34,16,128]{3,2,1,0:T(8,128)(2,1)S(1)}, bf16[2,34,8,128]{3,2,1,0:T(8,128)(2,1)S(1)}, bf16[2,34,8,128]{3,2,1,0:T(8,128)(2,1)S(1)}, bf16[2,34,8,1...) custom-call(bf16[1,2,32,64,128]{4,3,2,1,0:T(8,128)(2,1)} %maps_ref.5, f32[1,2,64,128]{3,2,1,0:T(8,128)} %refs_2_.3), custom_call_target="tpu_custom_call" | custom-call | bytes 2000000 | tf_op jit(solution)/shard_map/pack/pallas_call | solution.py:385
  1.4 0.0 copy-start.13
  1.4 3.1 %collective-permute-start = (bf16[2,34,16,128]{3,2,1,0:T(8,128)(2,1)S(1)}, bf16[2,34,16,128]{3,2,1,0:T(8,128)(2,1)S(1)}, u32[]{:S(2)}, u32[]{:S(2)}) collective-permute-start(bf16[2,34,16,128]{3,2,1,0:T(8,128)(2,1)S(1)} %get-tuple-element.45), channel_id=1, source_target_pairs={{0,4},{1,13},{2,6},{3,15},{4,0},{5,9},{6,2},{7,11},{8,12},{9,5},{1... | collective-permute-start | bytes 835592 | tf_op jit(solution)/shard_map/ppermute | solution.py:410
  4.5 2.6 %collective-permute-start.1 = (bf16[2,34,8,128]{3,2,1,0:T(8,128)(2,1)S(1)}, bf16[2,34,8,128]{3,2,1,0:T(8,128)(2,1)S(1)}, u32[]{:S(2)}, u32[]{:S(2)}) collective-permute-start(bf16[2,34,8,128]{3,2,1,0:T(8,128)(2,1)S(1)} %get-tuple-element.46), channel_id=1, source_target_pairs={{0,8},{1,5},{2,10},{3,7},{4,12},{5,1},{6,14},{7,3},{8,0},{9,13},{1... | collective-permute-start | bytes 417800 | tf_op jit(solution)/shard_map/ppermute | solution.py:410
  7.1 0.0 collective-permute-start.2
  7.1 1.9 %collective-permute-start.6 = (bf16[2,34,8,128]{3,2,1,0:T(8,128)(2,1)S(1)}, bf16[2,34,8,128]{3,2,1,0:T(8,128)(2,1)S(1)}, u32[]{:S(2)}, u32[]{:S(2)}) collective-permute-start(bf16[2,34,8,128]{3,2,1,0:T(8,128)(2,1)S(1)} %get-tuple-element.70), channel_id=1, source_target_pairs={{0,8},{1,5},{2,10},{3,7},{4,12},{5,1},{6,14},{7,3},{8,0},{9,13},{1... | collective-permute-start | bytes 417800 | tf_op jit(solution)/shard_map/ppermute | solution.py:410
  9.0 1.9 %collective-permute-start.7 = (bf16[2,34,8,128]{3,2,1,0:T(8,128)(2,1)S(1)}, bf16[2,34,8,128]{3,2,1,0:T(8,128)(2,1)S(1)}, u32[]{:S(2)}, u32[]{:S(2)}) collective-permute-start(bf16[2,34,8,128]{3,2,1,0:T(8,128)(2,1)S(1)} %get-tuple-element.71), channel_id=1, source_target_pairs={{0,12},{1,9},{2,14},{3,11},{4,8},{5,13},{6,10},{7,15},{8,4},{9,1},... | collective-permute-start | bytes 417800 | tf_op jit(solution)/shard_map/ppermute | solution.py:410
  10.9 0.0 copy-done.13
  11.6 0.0 copy-start.4
  11.6 0.0 copy-start.5
  11.6 0.0 copy-start.6
  11.6 0.0 copy-done.2
  11.6 0.0 copy-done.3
  11.6 0.6 %copy-done.4 = f32[64]{0:T(128)S(1)} copy-done((f32[64]{0:T(128)S(1)}, f32[64]{0:T(128)}, u32[]{:S(2)}) %copy-start.4) | copy-done | bytes 280
  12.2 0.0 copy-done.5
  12.2 0.0 copy-done.6
  12.3 0.9 %prepare.1 = (bf16[1024,192]{1,0:T(8,128)(2,1)S(1)}, f32[64,128]{1,0:T(8,128)S(1)}, bf16[384,256]{1,0:T(8,128)(2,1)S(1)}, f32[64,128]{1,0:T(8,128)S(1)}, bf16[96...) custom-call(bf16[18,64]{1,0:T(8,128)(2,1)S(1)} %reshape.8.w_in_ref, f32[1,64]{1,0:T(1,128)S(1)} %bitcast.8, ...), custom_call_target="tpu_custom_call" | custom-call | flops 1000000000 | bytes 8000000 | tf_op jit(solution)/shard_map/prepare/pallas_call | solution.py:331
  13.1 0.0 copy-start.7
  13.2 0.7 %copy-done.7 = bf16[96,1152]{1,0:T(8,128)(2,1)} copy-done((bf16[96,1152]{1,0:T(8,128)(2,1)}, bf16[96,1152]{1,0:T(8,128)(2,1)S(1)}, u32[]{:S(2)}) %copy-start.7) | copy-done | bytes 221208
  13.8 0.7 %copy-done.9 = bf16[384,256]{1,0:T(8,128)(2,1)} copy-done((bf16[384,256]{1,0:T(8,128)(2,1)}, bf16[384,256]{1,0:T(8,128)(2,1)S(1)}, u32[]{:S(2)}) %copy-start.9) | copy-done | bytes 196632
  14.5 0.6 %copy-done.11 = f32[32,128]{1,0:T(8,128)} copy-done((f32[32,128]{1,0:T(8,128)}, f32[32,128]{1,0:T(8,128)S(1)}, u32[]{:S(2)}) %copy-start.11) | copy-done | bytes 16408
  15.1 0.8 %reshape.9 = s32[2,4,8]{2,1,0:T(4,128)S(1)} reshape(s32[64]{0:T(128)} %param.12) | data formatting | bytes 512 | tf_op jit(solution)/shard_map/reshape | solution.py:419
  15.9 0.0 collective-permute-done.1.two_ref
  15.9 4.6 %collective-permute-done.2.three_ref = bf16[2,34,8,128]{3,2,1,0:T(8,128)(2,1)S(1)} collective-permute-done((bf16[2,34,8,128]{3,2,1,0:T(8,128)(2,1)S(1)}, bf16[2,34,8,128]{3,2,1,0:T(8,128)(2,1)S(1)}, u32[]{:S(2)}, u32[]{:S(2)}) %collective-permute-start.2) | collective-permute-done | bytes 139296 | tf_op jit(solution)/shard_map/ppermute | solution.py:410
  20.5 0.0 collective-permute-done.one_ref
  20.5 0.1 broadcast_in_dim.17.offs_ref
  20.6 0.0 copy-done
  20.6 0.0 copy-done.1
  20.6 0.3 fold.2
  20.9 1.4 %collective-permute-start.3 = (f32[2,8,128]{2,1,0:T(8,128)S(1)}, f32[2,8,128]{2,1,0:T(8,128)S(1)}, u32[]{:S(2)}, u32[]{:S(2)}) collective-permute-start(f32[2,8,128]{2,1,0:T(8,128)S(1)} %get-tuple-element.67), channel_id=1, source_target_pairs={{0,12},{1,13},{2,14},{3,15},{4,8},{5,9},{6,10},{7,11},{8,4},{9,5},... | collective-permute-start | bytes 24584 | tf_op jit(solution)/shard_map/ppermute | solution.py:410
  22.3 6.4 %collective-permute-start.4 = (f32[2,8,128]{2,1,0:T(8,128)S(1)}, f32[2,8,128]{2,1,0:T(8,128)S(1)}, u32[]{:S(2)}, u32[]{:S(2)}) collective-permute-start(f32[2,8,128]{2,1,0:T(8,128)S(1)} %get-tuple-element.68), channel_id=1, source_target_pairs={{0,8},{1,9},{2,10},{3,11},{4,12},{5,13},{6,14},{7,15},{8,0},{9,1},... | collective-permute-start | bytes 24584 | tf_op jit(solution)/shard_map/ppermute | solution.py:410
  28.8 0.6 %collective-permute-start.5 = (f32[2,8,128]{2,1,0:T(8,128)S(1)}, f32[2,8,128]{2,1,0:T(8,128)S(1)}, u32[]{:S(2)}, u32[]{:S(2)}) collective-permute-start(f32[2,8,128]{2,1,0:T(8,128)S(1)} %get-tuple-element.69), channel_id=1, source_target_pairs={{0,4},{1,5},{2,6},{3,7},{4,0},{5,1},{6,2},{7,3},{8,12},{9,13},{10,... | collective-permute-start | bytes 24584 | tf_op jit(solution)/shard_map/ppermute | solution.py:410
  29.3 0.0 collective-permute-done.6.two_ref
  29.4 0.0 collective-permute-done.7.three_ref
  29.4 0.3 fold.3
  29.7 2.4 %collective-permute-start.8 = (f32[2,8,128]{2,1,0:T(8,128)S(1)}, f32[2,8,128]{2,1,0:T(8,128)S(1)}, u32[]{:S(2)}, u32[]{:S(2)}) collective-permute-start(f32[2,8,128]{2,1,0:T(8,128)S(1)} %get-tuple-element.74), channel_id=1, source_target_pairs={{0,12},{1,13},{2,14},{3,15},{4,8},{5,9},{6,10},{7,11},{8,4},{9,5},... | collective-permute-start | bytes 24584 | tf_op jit(solution)/shard_map/ppermute | solution.py:410
  32.1 0.8 %collective-permute-start.9 = (f32[2,8,128]{2,1,0:T(8,128)S(1)}, f32[2,8,128]{2,1,0:T(8,128)S(1)}, u32[]{:S(2)}, u32[]{:S(2)}) collective-permute-start(f32[2,8,128]{2,1,0:T(8,128)S(1)} %get-tuple-element.75), channel_id=1, source_target_pairs={{0,8},{1,9},{2,10},{3,11},{4,12},{5,13},{6,14},{7,15},{8,0},{9,1},... | collective-permute-start | bytes 24584 | tf_op jit(solution)/shard_map/ppermute | solution.py:410
  32.9 0.0 collective-permute-done.3.refs_9_
  32.9 1.3 %collective-permute-start.10 = (f32[2,8,128]{2,1,0:T(8,128)S(1)}, f32[2,8,128]{2,1,0:T(8,128)S(1)}, u32[]{:S(2)}, u32[]{:S(2)}) collective-permute-start(f32[2,8,128]{2,1,0:T(8,128)S(1)} %get-tuple-element.76), channel_id=1, source_target_pairs={{0,4},{1,5},{2,6},{3,7},{4,0},{5,1},{6,2},{7,3},{8,12},{9,13},{10,... | collective-permute-start | bytes 24584 | tf_op jit(solution)/shard_map/ppermute | solution.py:410
  34.2 0.0 collective-permute-done.4.refs_10_
  34.2 0.0 collective-permute-done.5.refs_11_
  34.2 0.0 copy-done.8
  34.2 0.0 copy-done.10
  34.2 1.5 %denoise_first.1 = (f32[2,32,128]{2,1,0:T(8,128)S(1)}, f32[2,8,128]{2,1,0:T(8,128)S(1)}, bf16[256,128]{1,0:T(8,128)(2,1)S(1)}, bf16[64,128]{1,0:T(8,128)(2,1)S(1)}) custom-call(f32[64,128]{1,0:T(8,128)S(1)} %get-tuple-element.55.refs_0_, f32[32,128]{1,0:T(8,128)S(1)} %copy-done.12, f32[1,2,64,128]{3,2,1,0:T(8,128)S(1)} %copy-done.1, ...), custom_call_target="tpu_custom_call" | custom-call | flops 2000000000 | bytes 2000000 | tf_op jit(solution)/shard_map/denoise_first/pallas_call | solution.py:262
  35.7 0.0 collective-permute-done.8.refs_9_
  35.7 1.0 %collective-permute-done.9.refs_10_ = f32[2,8,128]{2,1,0:T(8,128)S(1)} collective-permute-done((f32[2,8,128]{2,1,0:T(8,128)S(1)}, f32[2,8,128]{2,1,0:T(8,128)S(1)}, u32[]{:S(2)}, u32[]{:S(2)}) %collective-permute-start.9) | collective-permute-done | bytes 8224 | tf_op jit(solution)/shard_map/ppermute | solution.py:410
  36.6 0.0 collective-permute-done.10.refs_11_
  36.6 2.3 %denoise_rest.1 = f32[1,2,64,128]{3,2,1,0:T(8,128)} custom-call(f32[64,128]{1,0:T(8,128)S(1)} %get-tuple-element.55.refs_0_, f32[32,128]{1,0:T(8,128)S(1)} %copy-done.12, f32[1,2,64,128]{3,2,1,0:T(8,128)S(1)} %copy-done.1, bf16[1024,192]{1,0:T(8,128)(2,1)S(1)} %get-tuple-element.57.refs_3_, f32[64,128]{1,0:T(8,128)S(1)} %get-tuple-element.58.refs_4_, ...), custom_call_target="tpu_custom_call" | custom-call | flops 2000000000 | bytes 2000000 | tf_op jit(solution)/shard_map/denoise_rest/pallas_call | solution.py:262
  (12 shorter events, 0.0 us)
Async XLA Ops:
  0.0 11.6 %copy-start.2 = (bf16[64,64,3,3]{1,0,3,2:T(8,128)(2,1)S(1)}, bf16[64,64,3,3]{1,0,3,2:T(8,128)(2,1)}, u32[]{:S(2)}) copy-start(bf16[64,64,3,3]{1,0,3,2:T(8,128)(2,1)} %param.16) | copy-start | bytes 221188
  1.4 9.5 %copy-start.13 = (bf16[64,2,3,3]{0,1,3,2:T(2,128)(2,1)S(1)}, bf16[64,2,3,3]{0,1,3,2:T(2,128)(2,1)}, u32[]{:S(2)}) copy-start(bf16[64,2,3,3]{0,1,3,2:T(2,128)(2,1)} %param.14) | copy-start | bytes 6916
  1.4 19.1 %collective-permute-start = (bf16[2,34,16,128]{3,2,1,0:T(8,128)(2,1)S(1)}, bf16[2,34,16,128]{3,2,1,0:T(8,128)(2,1)S(1)}, u32[]{:S(2)}, u32[]{:S(2)}) collective-permute-start(bf16[2,34,16,128]{3,2,1,0:T(8,128)(2,1)S(1)} %get-tuple-element.45), channel_id=1, source_target_pairs={{0,4},{1,13},{2,6},{3,15},{4,0},{5,9},{6,2},{7,11},{8,12},{9,5},{1... | collective-permute-start | bytes 835592 | tf_op jit(solution)/shard_map/ppermute | solution.py:410
  4.5 11.4 %collective-permute-start.1 = (bf16[2,34,8,128]{3,2,1,0:T(8,128)(2,1)S(1)}, bf16[2,34,8,128]{3,2,1,0:T(8,128)(2,1)S(1)}, u32[]{:S(2)}, u32[]{:S(2)}) collective-permute-start(bf16[2,34,8,128]{3,2,1,0:T(8,128)(2,1)S(1)} %get-tuple-element.46), channel_id=1, source_target_pairs={{0,8},{1,5},{2,10},{3,7},{4,12},{5,1},{6,14},{7,3},{8,0},{9,13},{1... | collective-permute-start | bytes 417800 | tf_op jit(solution)/shard_map/ppermute | solution.py:410
  7.1 13.4 %collective-permute-start.2 = (bf16[2,34,8,128]{3,2,1,0:T(8,128)(2,1)S(1)}, bf16[2,34,8,128]{3,2,1,0:T(8,128)(2,1)S(1)}, u32[]{:S(2)}, u32[]{:S(2)}) collective-permute-start(bf16[2,34,8,128]{3,2,1,0:T(8,128)(2,1)S(1)} %get-tuple-element.47), channel_id=1, source_target_pairs={{0,12},{1,9},{2,14},{3,11},{4,8},{5,13},{6,10},{7,15},{8,4},{9,1},... | collective-permute-start | bytes 417800 | tf_op jit(solution)/shard_map/ppermute | solution.py:410
  7.1 22.3 %collective-permute-start.6 = (bf16[2,34,8,128]{3,2,1,0:T(8,128)(2,1)S(1)}, bf16[2,34,8,128]{3,2,1,0:T(8,128)(2,1)S(1)}, u32[]{:S(2)}, u32[]{:S(2)}) collective-permute-start(bf16[2,34,8,128]{3,2,1,0:T(8,128)(2,1)S(1)} %get-tuple-element.70), channel_id=1, source_target_pairs={{0,8},{1,5},{2,10},{3,7},{4,12},{5,1},{6,14},{7,3},{8,0},{9,13},{1... | collective-permute-start | bytes 417800 | tf_op jit(solution)/shard_map/ppermute | solution.py:410
  9.0 20.4 %collective-permute-start.7 = (bf16[2,34,8,128]{3,2,1,0:T(8,128)(2,1)S(1)}, bf16[2,34,8,128]{3,2,1,0:T(8,128)(2,1)S(1)}, u32[]{:S(2)}, u32[]{:S(2)}) collective-permute-start(bf16[2,34,8,128]{3,2,1,0:T(8,128)(2,1)S(1)} %get-tuple-element.71), channel_id=1, source_target_pairs={{0,12},{1,9},{2,14},{3,11},{4,8},{5,13},{6,10},{7,15},{8,4},{9,1},... | collective-permute-start | bytes 417800 | tf_op jit(solution)/shard_map/ppermute | solution.py:410
  10.9 0.7 %copy-start.3 = (bf16[2,64,3,3]{1,0,3,2:T(2,128)(2,1)S(1)}, bf16[2,64,3,3]{1,0,3,2:T(2,128)(2,1)}, u32[]{:S(2)}) copy-start(bf16[2,64,3,3]{1,0,3,2:T(2,128)(2,1)} %param.18) | copy-start | bytes 6916
  11.6 0.7 %copy-start.4 = (f32[64]{0:T(128)S(1)}, f32[64]{0:T(128)}, u32[]{:S(2)}) copy-start(f32[64]{0:T(128)} %param.15) | copy-start | bytes 772
  11.6 0.7 %copy-start.5 = (f32[64]{0:T(128)S(1)}, f32[64]{0:T(128)}, u32[]{:S(2)}) copy-start(f32[64]{0:T(128)} %param.17) | copy-start | bytes 772
  11.6 0.7 %copy-start.6 = (f32[2]{0:T(128)S(1)}, f32[2]{0:T(128)}, u32[]{:S(2)}) copy-start(f32[2]{0:T(128)} %b_out_ref.1) | copy-start | bytes 28
  12.3 8.3 %copy-start = (bf16[1,2,32,64,128]{4,3,2,1,0:T(8,128)(2,1)S(1)}, bf16[1,2,32,64,128]{4,3,2,1,0:T(8,128)(2,1)}, u32[]{:S(2)}) copy-start(bf16[1,2,32,64,128]{4,3,2,1,0:T(8,128)(2,1)} %maps_ref.5) | copy-start | bytes 3145732
  13.1 0.7 %copy-start.7 = (bf16[96,1152]{1,0:T(8,128)(2,1)}, bf16[96,1152]{1,0:T(8,128)(2,1)S(1)}, u32[]{:S(2)}) copy-start(bf16[96,1152]{1,0:T(8,128)(2,1)S(1)} %get-tuple-element.61.refs_7_) | copy-start | bytes 663556
  13.8 0.7 %copy-start.9 = (bf16[384,256]{1,0:T(8,128)(2,1)}, bf16[384,256]{1,0:T(8,128)(2,1)S(1)}, u32[]{:S(2)}) copy-start(bf16[384,256]{1,0:T(8,128)(2,1)S(1)} %get-tuple-element.59.refs_5_) | copy-start | bytes 589828
  14.5 0.6 %copy-start.11 = (f32[32,128]{1,0:T(8,128)}, f32[32,128]{1,0:T(8,128)S(1)}, u32[]{:S(2)}) copy-start(f32[32,128]{1,0:T(8,128)S(1)} %get-tuple-element.56.refs_1_) | copy-start | bytes 49156
  15.1 5.5 %copy-start.1 = (f32[1,2,64,128]{3,2,1,0:T(8,128)S(1)}, f32[1,2,64,128]{3,2,1,0:T(8,128)}, u32[]{:S(2)}) copy-start(f32[1,2,64,128]{3,2,1,0:T(8,128)} %refs_2_.3) | copy-start | bytes 196612
  20.9 12.0 %collective-permute-start.3 = (f32[2,8,128]{2,1,0:T(8,128)S(1)}, f32[2,8,128]{2,1,0:T(8,128)S(1)}, u32[]{:S(2)}, u32[]{:S(2)}) collective-permute-start(f32[2,8,128]{2,1,0:T(8,128)S(1)} %get-tuple-element.67), channel_id=1, source_target_pairs={{0,12},{1,13},{2,14},{3,15},{4,8},{5,9},{6,10},{7,11},{8,4},{9,5},... | collective-permute-start | bytes 24584 | tf_op jit(solution)/shard_map/ppermute | solution.py:410
  22.3 11.8 %collective-permute-start.4 = (f32[2,8,128]{2,1,0:T(8,128)S(1)}, f32[2,8,128]{2,1,0:T(8,128)S(1)}, u32[]{:S(2)}, u32[]{:S(2)}) collective-permute-start(f32[2,8,128]{2,1,0:T(8,128)S(1)} %get-tuple-element.68), channel_id=1, source_target_pairs={{0,8},{1,9},{2,10},{3,11},{4,12},{5,13},{6,14},{7,15},{8,0},{9,1},... | collective-permute-start | bytes 24584 | tf_op jit(solution)/shard_map/ppermute | solution.py:410
  28.8 5.4 %copy-start.8 = (bf16[96,1152]{1,0:T(8,128)(2,1)S(1)}, bf16[96,1152]{1,0:T(8,128)(2,1)}, u32[]{:S(2)}) copy-start(bf16[96,1152]{1,0:T(8,128)(2,1)} %copy-done.7) | copy-start | bytes 663556
  28.8 5.4 %copy-start.10 = (bf16[384,256]{1,0:T(8,128)(2,1)S(1)}, bf16[384,256]{1,0:T(8,128)(2,1)}, u32[]{:S(2)}) copy-start(bf16[384,256]{1,0:T(8,128)(2,1)} %copy-done.9) | copy-start | bytes 589828
  28.8 5.4 %copy-start.12 = (f32[32,128]{1,0:T(8,128)S(1)}, f32[32,128]{1,0:T(8,128)}, u32[]{:S(2)}) copy-start(f32[32,128]{1,0:T(8,128)} %copy-done.11) | copy-start | bytes 49156
  28.8 5.4 %collective-permute-start.5 = (f32[2,8,128]{2,1,0:T(8,128)S(1)}, f32[2,8,128]{2,1,0:T(8,128)S(1)}, u32[]{:S(2)}, u32[]{:S(2)}) collective-permute-start(f32[2,8,128]{2,1,0:T(8,128)S(1)} %get-tuple-element.69), channel_id=1, source_target_pairs={{0,4},{1,5},{2,6},{3,7},{4,0},{5,1},{6,2},{7,3},{8,12},{9,13},{10,... | collective-permute-start | bytes 24584 | tf_op jit(solution)/shard_map/ppermute | solution.py:410
  29.7 6.0 %collective-permute-start.8 = (f32[2,8,128]{2,1,0:T(8,128)S(1)}, f32[2,8,128]{2,1,0:T(8,128)S(1)}, u32[]{:S(2)}, u32[]{:S(2)}) collective-permute-start(f32[2,8,128]{2,1,0:T(8,128)S(1)} %get-tuple-element.74), channel_id=1, source_target_pairs={{0,12},{1,13},{2,14},{3,15},{4,8},{5,9},{6,10},{7,11},{8,4},{9,5},... | collective-permute-start | bytes 24584 | tf_op jit(solution)/shard_map/ppermute | solution.py:410
  32.1 4.5 %collective-permute-start.9 = (f32[2,8,128]{2,1,0:T(8,128)S(1)}, f32[2,8,128]{2,1,0:T(8,128)S(1)}, u32[]{:S(2)}, u32[]{:S(2)}) collective-permute-start(f32[2,8,128]{2,1,0:T(8,128)S(1)} %get-tuple-element.75), channel_id=1, source_target_pairs={{0,8},{1,9},{2,10},{3,11},{4,12},{5,13},{6,14},{7,15},{8,0},{9,1},... | collective-permute-start | bytes 24584 | tf_op jit(solution)/shard_map/ppermute | solution.py:410
  32.9 3.8 %collective-permute-start.10 = (f32[2,8,128]{2,1,0:T(8,128)S(1)}, f32[2,8,128]{2,1,0:T(8,128)S(1)}, u32[]{:S(2)}, u32[]{:S(2)}) collective-permute-start(f32[2,8,128]{2,1,0:T(8,128)S(1)} %get-tuple-element.76), channel_id=1, source_target_pairs={{0,4},{1,5},{2,6},{3,7},{4,0},{5,1},{6,2},{7,3},{8,12},{9,13},{10,... | collective-permute-start | bytes 24584 | tf_op jit(solution)/shard_map/ppermute | solution.py:410
